TPU v7x, 256 devices: a whole 4x4x8 slice. The times are simulated.
256 devices in a mesh: seq: 64 (over z, x, core), tp: 4 (over y).
Axes of the slice: x: 4, y: 4, z: 8, core: 2. Of those that a mesh axis runs over, the one named last changes fastest.
Arguments:
- layer_input: bfloat16 [16384, 2048], P('seq'), may hold values from -1.5 to 1.5
- norm_gain: float32 [2048], replicated, may hold values from 0.5 to 1.5
- w_query: bfloat16 [2048, 2048], P(None, 'tp')
- key_weight: bfloat16 [2048, 1024], P(None, 'tp')
- value_weight: bfloat16 [2048, 1024], P(None, 'tp'), may hold values from -0.125 to 0.125
- w_out: bfloat16 [2048, 2048], P('tp'), may hold values from -1 to 1
- query_gain: float32 [128], replicated, may hold values from 0.6 to 6, as said below
- key_gain: float32 [128], replicated, may hold values from 0.6 to 6, as said below
- seg_ids: int32 [16384], P('seq'), may hold values from 0 to 7, as said below
- positions: int32 [16384], P('seq'), may hold values from 0 to 13106, as said below
- post_gain: float32 [2048], replicated, may hold values from 0.5 to 1.5
- w_gate: bfloat16 [2048, 3072], P('seq', 'tp'), may hold values from -0.125 to 0.125
- w_up: bfloat16 [2048, 3072], P('seq', 'tp'), may hold values from -0.125 to 0.125
- w_down: bfloat16 [3072, 2048], P('tp', 'seq'), may hold values from -0.21875 to 0.21875
Outputs:
- hidden: bfloat16 [16384, 2048], P('seq')
- key_cache: bfloat16 [16384, 1024], P('seq', 'tp')
- value_cache: bfloat16 [16384, 1024], P('seq', 'tp')
Inputs may be any that keep to these rules, and one draw needn't show every extreme that they name: `seg_ids`: prompt numbers never fall along the stream; each of the 8 prompts is a contiguous run of one or more tokens, and one prompt has exactly 13107 tokens. `positions`: each token's place in its prompt, counting from 0 at the prompt's first token. `query_gain`: positive gains. `key_gain`: positive gains.
All inputs are finite; a program needn't handle non-finite values.
Results may differ from a plain program's by a relative error of at most 0.02.
Values may be sent and summed in bfloat16 or wider, within the bound.
A program may use at most 128 MiB of HBM per device.

v0:
```python
import math

import jax
import jax.numpy as jnp
from jax import lax
from jax.sharding import PartitionSpec as P


def rms(v, gain):
    return v * lax.rsqrt(jnp.mean(v * v, axis=-1, keepdims=True) + 1e-06) * gain


def rope(v, place):
    half = v.shape[-1] // 2
    freqs = 1000000.0 ** (-2.0 * jnp.arange(half, dtype=jnp.float32) / v.shape[-1])
    angle = place.astype(jnp.float32)[:, None] * freqs[None, :]
    cosine = jnp.cos(angle)[:, None, :]
    sine = jnp.sin(angle)[:, None, :]
    block_start = v[..., :half]
    second = v[..., half:]
    return jnp.concatenate(
        [block_start * cosine - second * sine, second * cosine + block_start * sine], axis=-1
    )


def body(
    layer_input,
    norm_gain,
    w_query,
    key_weight,
    value_weight,
    w_out,
    query_gain,
    key_gain,
    seg_ids,
    positions,
    post_gain,
    w_gate,
    w_up,
    w_down,
):
    rows = layer_input.shape[0]
    head_size = query_gain.shape[0]
    query_local = w_query.shape[1] // head_size
    kv_local = key_weight.shape[1] // head_size
    head_group = query_local // kv_local
    scale = 1.0 / math.sqrt(head_size)
    xf = layer_input.astype(jnp.float32)
    normed_input = rms(xf, norm_gain).astype(jnp.bfloat16)
    query_matrix = jnp.dot(normed_input, w_query, preferred_element_type=jnp.float32).reshape(
        rows, query_local, head_size
    )
    query_matrix = rope(rms(query_matrix, query_gain), positions).astype(jnp.bfloat16)
    key_matrix = jnp.dot(normed_input, key_weight, preferred_element_type=jnp.float32).reshape(
        rows, kv_local, head_size
    )
    key_matrix = rope(rms(key_matrix, key_gain), positions).astype(jnp.bfloat16)
    key_cache = key_matrix.reshape(rows, kv_local * head_size)
    value_cache = jnp.dot(normed_input, value_weight, preferred_element_type=jnp.float32).astype(
        jnp.bfloat16
    )
    grouped = query_matrix.reshape(rows, kv_local, head_group, head_size).transpose(1, 2, 0, 3)
    me = lax.axis_index("seq")
    my_last = me * rows + rows - 1

    def update(state, key_rows, value_rows, seg_rows, place_rows):
        top, total, acc = state
        count = key_rows.shape[0]
        s = (
            jnp.einsum(
                "hgqd,khd->hgqk",
                grouped,
                key_rows.reshape(count, kv_local, head_size),
                preferred_element_type=jnp.float32,
            )
            * scale
        )
        allowed = (seg_ids[:, None] == seg_rows[None, :]) & (
            place_rows[None, :] <= positions[:, None]
        )
        s = jnp.where(allowed, s, -1e30)
        new_top = jnp.maximum(top, jnp.max(s, axis=-1))
        p = jnp.where(allowed, jnp.exp(s - new_top[..., None]), 0.0)
        decay = jnp.exp(top - new_top)
        total = total * decay + jnp.sum(p, axis=-1)
        acc = acc * decay[..., None] + jnp.einsum(
            "hgqk,khd->hgqd",
            p.astype(jnp.bfloat16),
            value_rows.reshape(count, kv_local, head_size),
            preferred_element_type=jnp.float32,
        )
        return (new_top, total, acc)

    start_state = (
        jnp.full((kv_local, head_group, rows), -1e30, jnp.float32),
        jnp.zeros((kv_local, head_group, rows), jnp.float32),
        jnp.zeros((kv_local, head_group, rows, head_size), jnp.float32),
    )
    travel = (key_cache, value_cache, seg_ids, positions)
    dead = jnp.int32(0) < 0
    key_rows = lax.all_gather(travel[0], "seq", axis=0, tiled=True)
    value_rows = lax.all_gather(travel[1], "seq", axis=0, tiled=True)
    seg_rows = lax.all_gather(travel[2], "seq", axis=0, tiled=True)
    place_rows = lax.all_gather(travel[3], "seq", axis=0, tiled=True)
    count = key_rows.shape[0]
    shards = count // rows
    limit = max(1, 1024 // rows)
    factor = 1
    for trial in range(1, limit + 1):
        if shards % trial == 0:
            factor = trial
    width = rows * factor

    def one_block(step, inner):
        offset = step * width
        kb = lax.dynamic_slice_in_dim(key_rows, offset, width, 0)
        vb = lax.dynamic_slice_in_dim(value_rows, offset, width, 0)
        sb = lax.dynamic_slice_in_dim(seg_rows, offset, width, 0)
        pb = lax.dynamic_slice_in_dim(place_rows, offset, width, 0)
        skip = dead | (offset > my_last) | (sb[width - 1] < seg_ids[0])
        return lax.cond(skip, lambda c: c, lambda c: update(c, kb, vb, sb, pb), inner)

    top, total, acc = lax.fori_loop(0, count // width, one_block, start_state)
    attended = (acc / total[..., None]).astype(jnp.bfloat16)
    attended = attended.transpose(2, 0, 1, 3).reshape(rows, query_local * head_size)
    partial_out = jnp.dot(attended, w_out, preferred_element_type=jnp.float32)
    summed = lax.psum(partial_out.astype(jnp.bfloat16), "tp").astype(jnp.float32)
    mid = (xf + summed).astype(jnp.bfloat16)
    mid_f = mid.astype(jnp.float32)
    post_normed = rms(mid_f, post_gain).astype(jnp.bfloat16)
    gate = jnp.dot(
        post_normed,
        lax.all_gather(w_gate, "seq", axis=0, tiled=True),
        preferred_element_type=jnp.float32,
    )
    up = jnp.dot(
        post_normed,
        lax.all_gather(w_up, "seq", axis=0, tiled=True),
        preferred_element_type=jnp.float32,
    )
    act = (jax.nn.silu(gate) * up).astype(jnp.bfloat16)
    terms = jnp.dot(
        act, lax.all_gather(w_down, "seq", axis=1, tiled=True), preferred_element_type=jnp.float32
    )
    ffn_total = lax.psum(terms.astype(jnp.bfloat16), "tp").astype(jnp.float32)
    hidden = (mid_f + ffn_total).astype(jnp.bfloat16)
    return (hidden, key_cache, value_cache)


def solution(mesh):
    in_specs = (
        P("seq", None),
        P(),
        P(None, "tp"),
        P(None, "tp"),
        P(None, "tp"),
        P("tp", None),
        P(),
        P(),
        P("seq"),
        P("seq"),
        P(),
        P("seq", "tp"),
        P("seq", "tp"),
        P("tp", "seq"),
    )
    out_specs = (P("seq", None), P("seq", "tp"), P("seq", "tp"))
    return jax.shard_map(body, mesh=mesh, in_specs=in_specs, out_specs=out_specs, check_vma=False)
```

profile of v0, /device:TPU:1, one launch (start us, length us, event | category | flops | bytes accessed | tf_op | source)
XLA Modules:
  0.0 657.4 jit_solution(4688254087747547651)
XLA Ops:
  7.3 1.6 fusion.12
  8.9 3.0 multiply_reduce_fusion.1
  14.6 2.4 convolution_convert_fusion.2
  17.1 3.2 fusion.28
  20.3 1.2 reshape.128
  22.9 48.2 %all-gather = s32[64,1,256]{2,1,0:T(1,128)S(1)} all-gather(s32[1,1,256]{2,1,0:T(1,128)S(1)} %bitcast.61), channel_id=1, replica_groups=mesh['seq'=64,'tp'=4] {'seq'}, dimensions={0}, use_global_device_ids=true | all-gather | bytes 66560 | tf_op jit(solution)/shard_map/all_gather | solution.py:103
  71.0 42.7 %all-gather.1 = s32[64,1,256]{2,1,0:T(1,128)S(1)} all-gather(s32[1,1,256]{2,1,0:T(1,128)S(1)} %bitcast.60), channel_id=1, replica_groups=mesh['seq'=64,'tp'=4] {'seq'}, dimensions={0}, use_global_device_ids=true | all-gather | bytes 66560 | tf_op jit(solution)/shard_map/all_gather | solution.py:104
  113.9 11.9 %copy.67 = bf16[16384,256]{0,1:T(8,128)(2,1)} copy(bf16[16384,256]{1,0:T(8,128)(2,1)} %all-gather.8.cloned.1.call-done) | data formatting | bytes 16777216 | tf_op jit(solution)/shard_map/while | solution.py:123
  125.8 59.9 %all-gather.10.cloned.1.call-done = bf16[16384,256]{1,0:T(8,128)(2,1)} async-done(((bf16[256,256]{1,0:T(8,128)(2,1)}), bf16[16384,256]{1,0:T(8,128)(2,1)}) %all-gather.10.cloned.1.call-update) | async-done | bytes 8388624 | tf_op jit(solution)/shard_map/all_gather | solution.py:102
  185.7 11.8 %copy.68 = bf16[16384,256]{0,1:T(8,128)(2,1)} copy(bf16[16384,256]{1,0:T(8,128)(2,1)} %all-gather.10.cloned.1.call-done) | data formatting | bytes 16777216 | tf_op jit(solution)/shard_map/while | solution.py:123
  197.5 44.5 %while.17 = (s32[]{:T(128)}, f32[2,2,256]{2,1,0:T(2,128)S(1)}, f32[2,2,256]{2,1,0:T(2,128)S(1)}, f32[2,2,256,128]{3,2,1,0:T(8,128)S(1)}, s32[]{:T(128)}, /*index...) while((s32[]{:T(128)}, f32[2,2,256]{2,1,0:T(2,128)S(1)}, ...), condition=%wide.region_8.9_spmd, body=%wide.region_3.8_spmd.sunk | while | flops 551553024 | bytes 18180480 | solution.py:123
  199.9 5.3 conditional.2
  200.3 1.3 constant_dynamic-slice_fusion
  203.6 1.6 fusion.6
  242.3 1.7 convolution_convert_fusion
  246.0 107.3 %all-reduce.3.cloned.1.call-done = bf16[256,2048]{1,0:T(8,128)(2,1)} async-done(((bf16[256,2048]{1,0:T(8,128)(2,1)}), bf16[256,2048]{1,0:T(8,128)(2,1)}) %all-reduce.3.cloned.1.call-update) | async-done | bytes 1048592 | tf_op jit(solution)/shard_map/psum | solution.py:127
  353.3 2.0 fusion.16
  355.3 81.9 %all-gather.12.cloned.1.call-done = bf16[2048,768]{1,0:T(8,128)(2,1)} async-done(((bf16[32,768]{1,0:T(8,128)(2,1)}), bf16[2048,768]{1,0:T(8,128)(2,1)}) %all-gather.12.cloned.1.call-update) | async-done | bytes 3145744 | tf_op jit(solution)/shard_map/all_gather | solution.py:133
  437.3 3.8 fusion.24
  441.1 75.0 %all-gather.14.cloned.1.call-done = bf16[2048,768]{1,0:T(8,128)(2,1)} async-done(((bf16[32,768]{1,0:T(8,128)(2,1)}), bf16[2048,768]{1,0:T(8,128)(2,1)}) %all-gather.14.cloned.1.call-update) | async-done | bytes 3145744 | tf_op jit(solution)/shard_map/all_gather | solution.py:138
  516.0 78.8 %all-gather.16.cloned.1.call-done = bf16[768,2048]{0,1:T(8,128)(2,1)} async-done(((bf16[768,32]{0,1:T(8,128)(2,1)}), bf16[768,2048]{0,1:T(8,128)(2,1)}) %all-gather.16.cloned.1.call-update) | async-done | bytes 3145744 | tf_op jit(solution)/shard_map/all_gather | solution.py:143
  594.8 6.2 convolution_convert_fusion.1
  601.1 46.8 %all-reduce.5.cloned.1.call-done = bf16[256,2048]{1,0:T(8,128)(2,1)} async-done(((bf16[256,2048]{1,0:T(8,128)(2,1)}), bf16[256,2048]{1,0:T(8,128)(2,1)}) %all-reduce.5.cloned.1.call-update) | async-done | bytes 1048592 | tf_op jit(solution)/shard_map/psum | solution.py:145
  647.9 2.6 fusion.19
  (153 shorter events, 27.5 us)
Async XLA Ops:
  7.2 235.2 %copy-start = (bf16[512,2048]{1,0:T(8,128)(2,1)S(1)}, bf16[512,2048]{1,0:T(8,128)(2,1)}, u32[]{:S(2)}) copy-start(bf16[512,2048]{1,0:T(8,128)(2,1)} %param.23) | copy-start | bytes 6291460
  7.2 4.8 copy-start.2
  7.2 106.7 %all-gather.8.cloned.1.call-start = ((), (), s32[]{:S(2)}) async-start(), calls=%async_computation | async-start | bytes 8519680 | tf_op jit(solution)/shard_map/all_gather | solution.py:101
  8.9 3.8 copy-start.4
  8.9 5.7 copy-start.1
  14.6 171.1 %all-gather.10.cloned.1.call-start = ((), (), s32[]{:S(2)}) async-start(), calls=%async_computation.1 | async-start | bytes 8519680 | tf_op jit(solution)/shard_map/all_gather | solution.py:102
  17.0 336.2 %all-reduce.3.cloned.1.call-start = ((), (), s32[]{:S(2)}) async-start(), calls=%async_computation.2 | async-start | bytes 2097152 | tf_op jit(solution)/shard_map/psum | solution.py:127
  17.1 4.8 copy-start.5
  21.9 1.0 copy-start.3
  244.0 193.2 %copy-start.6 = (f32[2048]{0:T(1024)S(1)}, f32[2048]{0:T(1024)}, u32[]{:S(2)}) copy-start(f32[2048]{0:T(1024)} %param.28) | copy-start | bytes 24580
  244.1 193.2 %all-gather.12.cloned.1.call-start = ((), (), s32[]{:S(2)}) async-start(), calls=%async_computation.3 | async-start | bytes 3194880 | tf_op jit(solution)/shard_map/all_gather | solution.py:133
  244.6 271.4 %all-gather.14.cloned.1.call-start = ((), (), s32[]{:S(2)}) async-start(), calls=%async_computation.4 | async-start | bytes 3194880 | tf_op jit(solution)/shard_map/all_gather | solution.py:138
  245.2 349.6 %all-gather.16.cloned.1.call-start = ((), (), s32[]{:S(2)}) async-start(), calls=%async_computation.5 | async-start | bytes 3194880 | tf_op jit(solution)/shard_map/all_gather | solution.py:143
  245.8 402.1 %all-reduce.5.cloned.1.call-start = ((), (), s32[]{:S(2)}) async-start(), calls=%async_computation.6 | async-start | bytes 2097152 | tf_op jit(solution)/shard_map/psum | solution.py:145
Sparse Core Ops, SparseCore 0:
  14.7 87.2 all-gather.7
  105.3 80.3 all-gather.9
  244.2 109.0 all-reduce.2
  356.3 80.9 all-gather.11
  440.2 75.7 all-gather.13
  519.0 75.7 all-gather.15
  601.2 46.6 all-reduce.4
where the time goes:
time: 659 us; the launch traced here: 657 us
  waiting for transfers between devices  451 us (68%)
  blocking collectives  90.9 us (14%)
  local copies, waits for them, and re-layouts  45.7 us (7%)
  matrix products  22.9 us (3%)
  loops' own time  21 us (3%)
  between operations  14.4 us (2%)
  other arithmetic  10.7 us (2%)
    psum x1, waiting for transfers between devices, body(): lax.psum(partial_out.astype(jnp.bfloat16), 'tp').astype(jnp.float32)  107 us
    all_gather x1, waiting for transfers between devices, body(): lax.all_gather(w_gate, 'seq', axis=0, tiled=True)  81.9 us
    all_gather x1, waiting for transfers between devices, body(): lax.all_gather(w_down, 'seq', axis=1, tiled=True)  78.8 us
    all_gather x1, waiting for transfers between devices, body(): lax.all_gather(w_up, 'seq', axis=0, tiled=True)  75 us
    all_gather x1, waiting for transfers between devices, body(): value_rows = lax.all_gather(travel[1], 'seq', axis=0, tiled=True)  59.9 us
    all_gather x1, blocking collectives, body(): seg_rows = lax.all_gather(travel[2], 'seq', axis=0, tiled=True)  48.2 us
    psum x1, waiting for transfers between devices, body(): ffn_total = lax.psum(terms.astype(jnp.bfloat16), 'tp').astype(jnp.float32)  46.8 us
    all_gather x1, blocking collectives, body(): place_rows = lax.all_gather(travel[3], 'seq', axis=0, tiled=True)  42.7 us
  transfers between devices with their start and end apart: 7, of which 6 were waited for; matrix products, arithmetic and copies ran while one was open for 4% of the time, Pallas kernels for 0%

commit v1 on v0

--- a/solution.py
+++ b/solution.py
@@ -43,8 +43,10 @@
     head_size = query_gain.shape[0]
     query_local = w_query.shape[1] // head_size
     kv_local = key_weight.shape[1] // head_size
+    kv_cols = kv_local * head_size
     head_group = query_local // kv_local
     scale = 1.0 / math.sqrt(head_size)
+    shards = lax.axis_size("seq")
     xf = layer_input.astype(jnp.float32)
     normed_input = rms(xf, norm_gain).astype(jnp.bfloat16)
     query_matrix = jnp.dot(normed_input, w_query, preferred_element_type=jnp.float32).reshape(
@@ -55,29 +57,57 @@
         rows, kv_local, head_size
     )
     key_matrix = rope(rms(key_matrix, key_gain), positions).astype(jnp.bfloat16)
-    key_cache = key_matrix.reshape(rows, kv_local * head_size)
+    key_cache = key_matrix.reshape(rows, kv_cols)
     value_cache = jnp.dot(normed_input, value_weight, preferred_element_type=jnp.float32).astype(
         jnp.bfloat16
     )
+
+    width_all = 2 * kv_cols
+    ff_rows, ff_local = w_gate.shape
+    w_rows = ff_rows * ff_local // width_all
+    packed = jnp.concatenate(
+        [
+            jnp.concatenate([key_cache, value_cache], axis=1),
+            w_gate.reshape(w_rows, width_all),
+            w_up.reshape(w_rows, width_all),
+            w_down.T.reshape(w_rows, width_all),
+        ],
+        axis=0,
+    )
+    gathered = lax.all_gather(packed, "seq", axis=0, tiled=False)
+    kv_rows = gathered[:, :rows].reshape(shards * rows, width_all)
+    key_rows = kv_rows[:, :kv_cols]
+    value_rows = kv_rows[:, kv_cols:]
+
+    def weight_part(k):
+        lo = rows + k * w_rows
+        return gathered[:, lo : lo + w_rows].reshape(shards * ff_rows, ff_local)
+
+    gate_w = weight_part(0)
+    up_w = weight_part(1)
+    down_wt = weight_part(2)
+
     grouped = query_matrix.reshape(rows, kv_local, head_group, head_size).transpose(1, 2, 0, 3)
     me = lax.axis_index("seq")
-    my_last = me * rows + rows - 1
+    first = me * rows
+    my_last = first + rows - 1
+    q_index = first + jnp.arange(rows, dtype=jnp.int32)
+    q_start = q_index - positions
+    my_start = q_start[0]
 
-    def update(state, key_rows, value_rows, seg_rows, place_rows):
+    def update(state, key_blk, value_blk, k_index):
         top, total, acc = state
-        count = key_rows.shape[0]
+        count = key_blk.shape[0]
         s = (
             jnp.einsum(
                 "hgqd,khd->hgqk",
                 grouped,
-                key_rows.reshape(count, kv_local, head_size),
+                key_blk.reshape(count, kv_local, head_size),
                 preferred_element_type=jnp.float32,
             )
             * scale
         )
-        allowed = (seg_ids[:, None] == seg_rows[None, :]) & (
-            place_rows[None, :] <= positions[:, None]
-        )
+        allowed = (k_index[None, :] <= q_index[:, None]) & (k_index[None, :] >= q_start[:, None])
         s = jnp.where(allowed, s, -1e30)
         new_top = jnp.maximum(top, jnp.max(s, axis=-1))
         p = jnp.where(allowed, jnp.exp(s - new_top[..., None]), 0.0)
@@ -86,7 +116,7 @@
         acc = acc * decay[..., None] + jnp.einsum(
             "hgqk,khd->hgqd",
             p.astype(jnp.bfloat16),
-            value_rows.reshape(count, kv_local, head_size),
+            value_blk.reshape(count, kv_local, head_size),
             preferred_element_type=jnp.float32,
         )
         return (new_top, total, acc)
@@ -96,14 +126,7 @@
         jnp.zeros((kv_local, head_group, rows), jnp.float32),
         jnp.zeros((kv_local, head_group, rows, head_size), jnp.float32),
     )
-    travel = (key_cache, value_cache, seg_ids, positions)
-    dead = jnp.int32(0) < 0
-    key_rows = lax.all_gather(travel[0], "seq", axis=0, tiled=True)
-    value_rows = lax.all_gather(travel[1], "seq", axis=0, tiled=True)
-    seg_rows = lax.all_gather(travel[2], "seq", axis=0, tiled=True)
-    place_rows = lax.all_gather(travel[3], "seq", axis=0, tiled=True)
     count = key_rows.shape[0]
-    shards = count // rows
     limit = max(1, 1024 // rows)
     factor = 1
     for trial in range(1, limit + 1):
@@ -115,10 +138,9 @@
         offset = step * width
         kb = lax.dynamic_slice_in_dim(key_rows, offset, width, 0)
         vb = lax.dynamic_slice_in_dim(value_rows, offset, width, 0)
-        sb = lax.dynamic_slice_in_dim(seg_rows, offset, width, 0)
-        pb = lax.dynamic_slice_in_dim(place_rows, offset, width, 0)
-        skip = dead | (offset > my_last) | (sb[width - 1] < seg_ids[0])
-        return lax.cond(skip, lambda c: c, lambda c: update(c, kb, vb, sb, pb), inner)
+        k_index = offset + jnp.arange(width, dtype=jnp.int32)
+        skip = (offset > my_last) | (offset + width - 1 < my_start)
+        return lax.cond(skip, lambda c: c, lambda c: update(c, kb, vb, k_index), inner)
 
     top, total, acc = lax.fori_loop(0, count // width, one_block, start_state)
     attended = (acc / total[..., None]).astype(jnp.bfloat16)
@@ -128,19 +150,11 @@
     mid = (xf + summed).astype(jnp.bfloat16)
     mid_f = mid.astype(jnp.float32)
     post_normed = rms(mid_f, post_gain).astype(jnp.bfloat16)
-    gate = jnp.dot(
-        post_normed,
-        lax.all_gather(w_gate, "seq", axis=0, tiled=True),
-        preferred_element_type=jnp.float32,
-    )
-    up = jnp.dot(
-        post_normed,
-        lax.all_gather(w_up, "seq", axis=0, tiled=True),
-        preferred_element_type=jnp.float32,
-    )
+    gate = jnp.dot(post_normed, gate_w, preferred_element_type=jnp.float32)
+    up = jnp.dot(post_normed, up_w, preferred_element_type=jnp.float32)
     act = (jax.nn.silu(gate) * up).astype(jnp.bfloat16)
-    terms = jnp.dot(
-        act, lax.all_gather(w_down, "seq", axis=1, tiled=True), preferred_element_type=jnp.float32
+    terms = lax.dot_general(
+        act, down_wt, (((1,), (1,)), ((), ())), preferred_element_type=jnp.float32
     )
     ffn_total = lax.psum(terms.astype(jnp.bfloat16), "tp").astype(jnp.float32)
     hidden = (mid_f + ffn_total).astype(jnp.bfloat16)

time: 659 us -> 396 us (0.60)
  waiting for transfers between devices: 451 us -> 261 us
  blocking collectives: 90.9 us -> 0 us
  local copies, waits for them, and re-layouts: 45.7 us -> 74.9 us
  loops' own time: 21 us -> 11.4 us
    all_gather x5 -> x1, waiting for transfers between devices: 296 us -> 122 us  [body(): gathered = lax.all_gather(packed, 'seq', axis=0, tiled=False)]
    all_gather x2 -> x0, blocking collectives: 90.9 us -> none  [the longest x1 48.2 us: body(): seg_rows = lax.all_gather(travel[2], 'seq', axis=0, tiled=True)]
    unnamed x14 -> x26, local copies, waits for them, and re-layouts: 0.04 us -> 25.8 us
    while x3 -> x1, local copies, waits for them, and re-layouts: 23.9 us -> 0.2 us  [body(): top, total, acc = lax.fori_loop(0, count // width, one_block, start_state)]
    reshape x0 -> x9, local copies, waits for them, and re-layouts: none -> 22.6 us  [the longest x3 17.8 us: weight_part(): return gathered[:, lo:lo + w_rows].reshape(shards * ff_rows, ff_local)]
    psum x1, waiting for transfers between devices: 107 us -> 88.8 us  [body(): lax.psum(partial_out.astype(jnp.bfloat16), 'tp').astype(jnp.float32)]
    another operation x1, loops' own time: 20.5 us -> 10.8 us  [body(): top, total, acc = lax.fori_loop(0, count // width, one_block, start_state)]
    slice x32 -> x4, local copies, waits for them, and re-layouts: 18.1 us -> 21.5 us  [the longest x1 8.16 us: body(): kv_rows = gathered[:, :rows].reshape(shards * rows, width_all)]
  transfers between devices with their start and end apart: 7 -> 3, of which waited for: 6 -> 3; matrix products, arithmetic and copies ran while one was open for 4% -> 8% of each run, Pallas kernels for 0% -> 0%
where the time goes in v1:
time: 396 us; the launch traced here: 393 us
  waiting for transfers between devices  261 us (66%)
  local copies, waits for them, and re-layouts  74.9 us (19%)
  matrix products  19.9 us (5%)
  between operations  14.1 us (4%)
  other arithmetic  11.7 us (3%)
  loops' own time  11.4 us (3%)
    all_gather x1, waiting for transfers between devices, body(): gathered = lax.all_gather(packed, 'seq', axis=0, tiled=False)  122 us
    psum x1, waiting for transfers between devices, body(): lax.psum(partial_out.astype(jnp.bfloat16), 'tp').astype(jnp.float32)  88.8 us
    psum x1, waiting for transfers between devices, body(): ffn_total = lax.psum(terms.astype(jnp.bfloat16), 'tp').astype(jnp.float32)  50.4 us
    unnamed x26, local copies, waits for them, and re-layouts  25.8 us
    reshape x3, local copies, waits for them, and re-layouts, weight_part(): return gathered[:, lo:lo + w_rows].reshape(shards * ff_rows, ff_local)  17.8 us
    another operation x1, loops' own time, body(): top, total, acc = lax.fori_loop(0, count // width, one_block, start_state)  10.8 us
    slice x1, local copies, waits for them, and re-layouts, body(): kv_rows = gathered[:, :rows].reshape(shards * rows, width_all)  8.16 us
  transfers between devices with their start and end apart: 3, of which 3 were waited for; matrix products, arithmetic and copies ran while one was open for 8% of the time, Pallas kernels for 0%

profile of v1, /device:TPU:1, one launch (start us, length us, event | category | flops | bytes accessed | tf_op | source)
XLA Modules:
  0.0 393.3 jit_solution(1556739157459538463)
XLA Ops:
  7.3 1.7 fusion.14
  15.3 2.3 convolution_convert_fusion.2
  17.6 1.9 multiply_reduce_fusion.1
  20.8 2.0 copy.81
  23.4 3.2 fusion.29
  29.2 121.8 %all-gather.3.cloned.1.call-done = bf16[25600,512]{1,0:T(8,128)(2,1)} async-done(((bf16[400,512]{1,0:T(8,128)(2,1)}), bf16[25600,512]{1,0:T(8,128)(2,1)}) %all-gather.3.cloned.1.call-update) | async-done | bytes 26214416 | tf_op jit(solution)/shard_map/all_gather | solution.py:77
  151.0 8.2 %slice.46 = bf16[64,256,512]{2,1,0:T(8,128)(2,1)S(1)} slice(bf16[64,400,512]{2,1,0:T(8,128)(2,1)} %bitcast.51), slice={[0:64], [0:256], [0:512]} | slice | bytes 33554432 | tf_op jit(solution)/shard_map/slice | solution.py:78
  159.2 6.0 %fusion.36 = (bf16[16384,256]{1,0:T(8,128)(2,1)}, bf16[16384,256]{1,0:T(8,128)(2,1)}) fusion(bf16[16384,512]{1,0:T(8,128)(2,1)S(1)} %bitcast.49), kind=kLoop, calls=%fused_computation.64 | loop fusion | bytes 33554432 | tf_op jit(solution)/shard_map/slice | solution.py:80
  165.2 12.0 %copy.99 = bf16[16384,256]{0,1:T(8,128)(2,1)} copy(bf16[16384,256]{1,0:T(8,128)(2,1)} %get-tuple-element.580) | data formatting | bytes 16777216
  177.2 12.0 %copy.98 = bf16[16384,256]{0,1:T(8,128)(2,1)} copy(bf16[16384,256]{1,0:T(8,128)(2,1)} %get-tuple-element.581) | data formatting | bytes 16777216
  189.2 16.7 %while.22 = (s32[]{:T(128)}, f32[2,2,256]{2,1,0:T(2,128)S(1)}, f32[2,2,256]{2,1,0:T(2,128)S(1)}, f32[2,2,256,128]{3,2,1,0:T(8,128)S(1)}, s32[]{:T(128)}, /*index...) while((s32[]{:T(128)}, f32[2,2,256]{2,1,0:T(2,128)S(1)}, ...), condition=%wide.region_8.9_spmd.clone, body=%wide.region_3.8_spmd.clone.sunk | while | flops 551554304 | bytes 18175340 | solution.py:145
  189.9 5.3 %conditional.3 = (f32[2,2,256]{2,1,0:T(2,128)S(1)}, f32[2,2,256]{2,1,0:T(2,128)S(1)}, f32[2,2,256,128]{3,2,1,0:T(8,128)S(1)}) conditional(s32[]{:T(128)} %convert_element_type.145, (s32[]{:T(128)}, s32[1024]{0:T(1024)S(1)}, s32[]{:T(128)}, s32[256]{0:T(256)S(1)}, bf16[16384,256]{0,1:T(8,128)(2,1)}, /*index=5*/bf16[2,2,256,128]{3,2,1,0:T(8,128)(2,1)S(1)}, ...), branch_computations={%region_4.6_spmd, %region_7.7_spmd} | conditional | flops 551554304 | bytes 18161734 | solution.py:143
  193.5 1.6 fusion.8
  206.2 1.7 convolution_convert_fusion
  208.2 6.7 %fusion.35 = (bf16[64,48,512]{2,1,0:T(8,128)(2,1)}, bf16[64,48,512]{2,1,0:T(8,128)(2,1)}, bf16[64,48,512]{2,1,0:T(8,128)(2,1)}) fusion(bf16[64,400,512]{2,1,0:T(8,128)(2,1)} %bitcast.52), kind=kLoop, calls=%fused_computation.63 | loop fusion | bytes 18874368 | tf_op jit(solution)/shard_map/slice | solution.py:84
  214.9 5.9 %reshape.155 = bf16[2048,768]{1,0:T(8,128)(2,1)} reshape(bf16[64,48,512]{2,1,0:T(8,128)(2,1)} %get-tuple-element.577) | data formatting | bytes 6291456 | tf_op jit(solution)/shard_map/reshape | solution.py:84
  220.8 5.9 %reshape.157 = bf16[2048,768]{1,0:T(8,128)(2,1)} reshape(bf16[64,48,512]{2,1,0:T(8,128)(2,1)} %get-tuple-element.578) | data formatting | bytes 6291456 | tf_op jit(solution)/shard_map/reshape | solution.py:84
  226.7 5.9 %reshape.156 = bf16[2048,768]{1,0:T(8,128)(2,1)} reshape(bf16[64,48,512]{2,1,0:T(8,128)(2,1)} %get-tuple-element.579) | data formatting | bytes 6291456 | tf_op jit(solution)/shard_map/reshape | solution.py:84
  232.7 88.8 %all-reduce.3.cloned.1.call-done = bf16[256,2048]{1,0:T(8,128)(2,1)} async-done(((bf16[256,2048]{1,0:T(8,128)(2,1)}), bf16[256,2048]{1,0:T(8,128)(2,1)}) %all-reduce.3.cloned.1.call-update) | async-done | bytes 1048592 | tf_op jit(solution)/shard_map/psum | solution.py:149
  321.4 2.2 fusion.18
  324.0 2.0 fusion.26
  325.9 6.3 %convolution_convert_fusion.1 = bf16[256,2048]{1,0:T(8,128)(2,1)} fusion(bf16[2048,768]{1,0:T(8,128)(2,1)} %reshape.157, bf16[2048,768]{1,0:T(8,128)(2,1)} %reshape.156, f32[256,768]{1,0:T(8,128)} %fusion.26, bf16[256,2048]{1,0:T(8,128)(2,1)S(1)} %get-tuple-element.572, f32[2048]{0:T(1024)S(1)} %copy-done.10, f32[256]{0:T(256)S(1)} %add_rsqrt_fusion.2), kind=kOutput, calls=%fused_computation.26 | convolution fusion | flops 1614413824 | bytes 9184256 | tf_op jit(solution)/shard_map/dot_general | solution.py:156
  333.8 50.4 %all-reduce.5.cloned.1.call-done = bf16[256,2048]{1,0:T(8,128)(2,1)} async-done(((bf16[256,2048]{1,0:T(8,128)(2,1)}), bf16[256,2048]{1,0:T(8,128)(2,1)}) %all-reduce.5.cloned.1.call-update) | async-done | bytes 1048592 | tf_op jit(solution)/shard_map/psum | solution.py:159
  384.2 2.6 fusion.21
  (148 shorter events, 17.3 us)
Async XLA Ops:
  7.2 199.1 %copy-start = (bf16[512,2048]{1,0:T(8,128)(2,1)S(1)}, bf16[512,2048]{1,0:T(8,128)(2,1)}, u32[]{:S(2)}) copy-start(bf16[512,2048]{1,0:T(8,128)(2,1)} %param.23) | copy-start | bytes 6291460
  7.2 10.4 %copy-start.1 = (bf16[256,2048]{1,0:T(8,128)(2,1)S(1)}, bf16[256,2048]{1,0:T(8,128)(2,1)}, u32[]{:S(2)}) copy-start(bf16[256,2048]{1,0:T(8,128)(2,1)} %param.18) | copy-start | bytes 3145732
  7.2 143.8 %all-gather.3.cloned.1.call-start = ((), (), s32[]{:S(2)}) async-start(), calls=%async_computation.2 | async-start | bytes 26624000 | tf_op jit(solution)/shard_map/all_gather | solution.py:77
  15.2 4.4 %copy-start.8 = (f32[128]{0:T(128)S(1)}, f32[128]{0:T(128)}, u32[]{:S(2)}) copy-start(f32[128]{0:T(128)} %param.25) | copy-start | bytes 1540
  15.3 4.5 %copy-start.5 = (bf16[48,512]{0,1:T(8,128)(2,1)S(1)}, bf16[48,512]{0,1:T(8,128)(2,1)}, u32[]{:S(2)}) copy-start(bf16[48,512]{0,1:T(8,128)(2,1)} %copy.80) | copy-start | bytes 147460
  15.3 4.5 %copy-start.6 = (bf16[48,512]{0,1:T(8,128)(2,1)S(1)}, bf16[48,512]{0,1:T(8,128)(2,1)}, u32[]{:S(2)}) copy-start(bf16[48,512]{0,1:T(8,128)(2,1)} %copy.79) | copy-start | bytes 147460
  15.3 4.5 %copy-start.7 = (bf16[48,512]{0,1:T(8,128)(2,1)S(1)}, bf16[48,512]{0,1:T(8,128)(2,1)}, u32[]{:S(2)}) copy-start(bf16[48,512]{0,1:T(8,128)(2,1)} %copy.78) | copy-start | bytes 147460
  17.6 2.1 copy-start.3
  22.8 298.7 %all-reduce.3.cloned.1.call-start = ((), (), s32[]{:S(2)}) async-start(), calls=%async_computation | async-start | bytes 2097152 | tf_op jit(solution)/shard_map/psum | solution.py:149
  23.4 4.8 %copy-start.9 = (f32[128]{0:T(128)S(1)}, f32[128]{0:T(128)}, u32[]{:S(2)}) copy-start(f32[128]{0:T(128)} %param.24) | copy-start | bytes 1540
  208.0 176.2 %all-reduce.5.cloned.1.call-start = ((), (), s32[]{:S(2)}) async-start(), calls=%async_computation.1 | async-start | bytes 2097152 | tf_op jit(solution)/shard_map/psum | solution.py:159
  226.7 96.9 %copy-start.10 = (f32[2048]{0:T(1024)S(1)}, f32[2048]{0:T(1024)}, u32[]{:S(2)}) copy-start(f32[2048]{0:T(1024)} %param.27) | copy-start | bytes 24580
  321.4 2.5 copy-start.2
  325.9 6.3 %copy-start.4 = (bf16[256,256]{0,1:T(8,128)(2,1)S(1)}, bf16[256,256]{0,1:T(8,128)(2,1)}, u32[]{:S(2)}) copy-start(bf16[256,256]{0,1:T(8,128)(2,1)} %copy-done.3) | copy-start | bytes 393220
Sparse Core Ops, SparseCore 0:
  22.9 128.0 all-gather.2
  208.1 113.3 all-reduce.2
  332.4 51.7 all-reduce.4

commit v2 on v1

--- a/solution.py
+++ b/solution.py
@@ -1,9 +1,14 @@
+import functools
 import math
 
 import jax
 import jax.numpy as jnp
 from jax import lax
+from jax.experimental import pallas as pl
+from jax.experimental.pallas import tpu as pltpu
 from jax.sharding import PartitionSpec as P
+
+MESH = pl.DeviceIdType.MESH
 
 
 def rms(v, gain):
@@ -21,6 +26,78 @@
     return jnp.concatenate(
         [block_start * cosine - second * sine, second * cosine + block_start * sine], axis=-1
     )
+
+
+def tp_sum_kernel(n, x_ref, out_ref, slots, reduced, send1, recv1, send2, recv2):
+    me = lax.axis_index("tp")
+    row = lax.axis_index("seq")
+    cols = x_ref.shape[1] // n
+
+    barrier = pltpu.get_barrier_semaphore()
+    for k in range(1, n):
+        pl.semaphore_signal(barrier, inc=1, device_id=(row, lax.rem(me + k, n)), device_id_type=MESH)
+    pl.semaphore_wait(barrier, n - 1)
+
+    def block(ref, owner):
+        return ref.at[:, pl.ds(pl.multiple_of(owner * cols, cols), cols)]
+
+    first = []
+    for k in range(1, n):
+        peer = lax.rem(me + k, n)
+        copy = pltpu.make_async_remote_copy(
+            src_ref=block(x_ref, peer),
+            dst_ref=slots.at[k],
+            send_sem=send1.at[k],
+            recv_sem=recv1.at[k],
+            device_id=(row, peer),
+            device_id_type=MESH,
+        )
+        copy.start()
+        first.append(copy)
+    for copy in first:
+        copy.wait()
+    total = block(x_ref, me)[...].astype(jnp.float32)
+    for k in range(1, n):
+        total = total + slots[k].astype(jnp.float32)
+    reduced[...] = total.astype(reduced.dtype)
+    block(out_ref, me)[...] = reduced[...]
+
+    second = []
+    for k in range(1, n):
+        peer = lax.rem(me + k, n)
+        copy = pltpu.make_async_remote_copy(
+            src_ref=reduced,
+            dst_ref=block(out_ref, me),
+            send_sem=send2.at[k],
+            recv_sem=recv2.at[k],
+            device_id=(row, peer),
+            device_id_type=MESH,
+        )
+        copy.start()
+        second.append(copy)
+    for copy in second:
+        copy.wait()
+
+
+def tp_sum(x, collective_id):
+    n = lax.axis_size("tp")
+    rows, width = x.shape
+    cols = width // n
+    return pl.pallas_call(
+        functools.partial(tp_sum_kernel, n),
+        out_shape=jax.ShapeDtypeStruct((rows, width), x.dtype),
+        in_specs=[pl.BlockSpec(memory_space=pltpu.VMEM)],
+        out_specs=pl.BlockSpec(memory_space=pltpu.VMEM),
+        scratch_shapes=[
+            pltpu.VMEM((n, rows, cols), x.dtype),
+            pltpu.VMEM((rows, cols), x.dtype),
+            pltpu.SemaphoreType.DMA((n,)),
+            pltpu.SemaphoreType.DMA((n,)),
+            pltpu.SemaphoreType.DMA((n,)),
+            pltpu.SemaphoreType.DMA((n,)),
+        ],
+        compiler_params=pltpu.CompilerParams(collective_id=collective_id, has_side_effects=True),
+    )(x)
 
 
 def body(
@@ -146,7 +223,7 @@
     attended = (acc / total[..., None]).astype(jnp.bfloat16)
     attended = attended.transpose(2, 0, 1, 3).reshape(rows, query_local * head_size)
     partial_out = jnp.dot(attended, w_out, preferred_element_type=jnp.float32)
-    summed = lax.psum(partial_out.astype(jnp.bfloat16), "tp").astype(jnp.float32)
+    summed = tp_sum(partial_out.astype(jnp.bfloat16), 0).astype(jnp.float32)
     mid = (xf + summed).astype(jnp.bfloat16)
     mid_f = mid.astype(jnp.float32)
     post_normed = rms(mid_f, post_gain).astype(jnp.bfloat16)
@@ -156,7 +233,7 @@
     terms = lax.dot_general(
         act, down_wt, (((1,), (1,)), ((), ())), preferred_element_type=jnp.float32
     )
-    ffn_total = lax.psum(terms.astype(jnp.bfloat16), "tp").astype(jnp.float32)
+    ffn_total = tp_sum(terms.astype(jnp.bfloat16), 1).astype(jnp.float32)
     hidden = (mid_f + ffn_total).astype(jnp.bfloat16)
     return (hidden, key_cache, value_cache)
 

time: 396 us -> 390 us (0.985)
  the two profiles are of different devices: /device:TPU:1 before, /device:TPU:196 now
where the time goes in v2:
time: 390 us; the launch traced here: 388 us
  waiting for transfers between devices  112 us (29%)
  local copies, waits for them, and re-layouts  103 us (26%)
  Pallas kernels  63.1 us (16%)
  matrix products  53.3 us (14%)
  other arithmetic  29.1 us (7%)
  between operations  14.4 us (4%)
  loops' own time  12.2 us (3%)
    all_gather x1, waiting for transfers between devices, body(): gathered = lax.all_gather(packed, 'seq', axis=0, tiled=False)  112 us
    pallas_call x2, Pallas kernels, tp_sum(): pl.pallas_call(functools.partial(tp_sum_kernel, n), out_shape=jax.ShapeDt...  63.1 us
    unnamed x24, local copies, waits for them, and re-layouts  26.6 us
    dot_general x14, matrix products, update(): jnp.einsum('hgqk,khd->hgqd', p.astype(jnp.bfloat16), value_blk.reshape(co...  22.9 us
    dynamic_slice x14, local copies, waits for them, and re-layouts, one_block(): vb = lax.dynamic_slice_in_dim(value_rows, offset, width, 0)  17.9 us
    reshape x3, local copies, waits for them, and re-layouts, weight_part(): return gathered[:, lo:lo + w_rows].reshape(shards * ff_rows, ff_local)  17.7 us
    reduce_sum x14, other arithmetic, update(): total = total * decay + jnp.sum(p, axis=-1)  14.5 us
    slice x1, local copies, waits for them, and re-layouts, body(): kv_rows = gathered[:, :rows].reshape(shards * rows, width_all)  13.8 us
  transfers between devices with their start and end apart: 1, of which 1 were waited for; matrix products, arithmetic and copies ran while one was open for 2% of the time, Pallas kernels for 0%

profile of v2, /device:TPU:196, one launch (start us, length us, event | category | flops | bytes accessed | tf_op | source)
XLA Modules:
  0.0 387.7 jit_solution(8238009464556683512)
XLA Ops:
  31.7 112.4 %all-gather.3.cloned.1.call-done = bf16[25600,512]{1,0:T(8,128)(2,1)} async-done(((bf16[400,512]{1,0:T(8,128)(2,1)}), bf16[25600,512]{1,0:T(8,128)(2,1)}) %all-gather.3.cloned.1.call-update) | async-done | bytes 26214416 | tf_op jit(solution)/shard_map/all_gather | solution.py:154
  144.1 6.7 %fusion.35 = (bf16[64,48,512]{2,1,0:T(8,128)(2,1)}, bf16[64,48,512]{2,1,0:T(8,128)(2,1)}, bf16[64,48,512]{2,1,0:T(8,128)(2,1)}) fusion(bf16[64,400,512]{2,1,0:T(8,128)(2,1)} %bitcast.51), kind=kLoop, calls=%fused_computation.63 | loop fusion | bytes 18874368 | tf_op jit(solution)/shard_map/slice | solution.py:161
  150.8 13.8 %slice.46 = bf16[64,256,512]{2,1,0:T(8,128)(2,1)} slice(bf16[64,400,512]{2,1,0:T(8,128)(2,1)} %bitcast.52), slice={[0:64], [0:256], [0:512]} | slice | bytes 33554432 | tf_op jit(solution)/shard_map/slice | solution.py:155
  164.5 5.9 %reshape.155 = bf16[2048,768]{1,0:T(8,128)(2,1)} reshape(bf16[64,48,512]{2,1,0:T(8,128)(2,1)} %get-tuple-element.577) | data formatting | bytes 6291456 | tf_op jit(solution)/shard_map/reshape | solution.py:161
  170.5 11.3 %fusion.36 = (bf16[16384,256]{1,0:T(8,128)(2,1)}, bf16[16384,256]{1,0:T(8,128)(2,1)}) fusion(bf16[16384,512]{1,0:T(8,128)(2,1)} %bitcast.49), kind=kLoop, calls=%fused_computation.64 | loop fusion | bytes 33554432 | tf_op jit(solution)/shard_map/slice | solution.py:157
  181.8 11.9 %copy.99 = bf16[16384,256]{0,1:T(8,128)(2,1)} copy(bf16[16384,256]{1,0:T(8,128)(2,1)} %get-tuple-element.580) | data formatting | bytes 16777216
  193.7 5.9 %reshape.157 = bf16[2048,768]{1,0:T(8,128)(2,1)} reshape(bf16[64,48,512]{2,1,0:T(8,128)(2,1)} %get-tuple-element.578) | data formatting | bytes 6291456 | tf_op jit(solution)/shard_map/reshape | solution.py:161
  199.7 5.9 %reshape.156 = bf16[2048,768]{1,0:T(8,128)(2,1)} reshape(bf16[64,48,512]{2,1,0:T(8,128)(2,1)} %get-tuple-element.579) | data formatting | bytes 6291456 | tf_op jit(solution)/shard_map/reshape | solution.py:161
  205.5 11.9 %copy.98 = bf16[16384,256]{0,1:T(8,128)(2,1)} copy(bf16[16384,256]{1,0:T(8,128)(2,1)} %get-tuple-element.581) | data formatting | bytes 16777216
  217.5 85.0 %while.22 = (s32[]{:T(128)}, f32[2,2,256]{2,1,0:T(2,128)S(1)}, f32[2,2,256]{2,1,0:T(2,128)S(1)}, f32[2,2,256,128]{3,2,1,0:T(8,128)S(1)}, s32[]{:T(128)}, /*index...) while((s32[]{:T(128)}, f32[2,2,256]{2,1,0:T(2,128)S(1)}, ...), condition=%wide.region_8.9_spmd.clone, body=%wide.region_3.8_spmd.clone.sunk | while | flops 551554304 | bytes 18175340 | solution.py:222
  218.2 5.3 %conditional.3 = (f32[2,2,256]{2,1,0:T(2,128)S(1)}, f32[2,2,256]{2,1,0:T(2,128)S(1)}, f32[2,2,256,128]{3,2,1,0:T(8,128)S(1)}) conditional(s32[]{:T(128)} %convert_element_type.145, (s32[]{:T(128)}, s32[1024]{0:T(1024)S(1)}, s32[]{:T(128)}, s32[256]{0:T(256)S(1)}, bf16[16384,256]{0,1:T(8,128)(2,1)}, /*index=5*/bf16[2,2,256,128]{3,2,1,0:T(8,128)(2,1)S(1)}, ...), branch_computations={%region_4.6_spmd, %region_7.7_spmd} | conditional | flops 551554304 | bytes 18161734 | solution.py:220
  224.1 5.3 %conditional.3 = (f32[2,2,256]{2,1,0:T(2,128)S(1)}, f32[2,2,256]{2,1,0:T(2,128)S(1)}, f32[2,2,256,128]{3,2,1,0:T(8,128)S(1)}) conditional(s32[]{:T(128)} %convert_element_type.145, (s32[]{:T(128)}, s32[1024]{0:T(1024)S(1)}, s32[]{:T(128)}, s32[256]{0:T(256)S(1)}, bf16[16384,256]{0,1:T(8,128)(2,1)}, /*index=5*/bf16[2,2,256,128]{3,2,1,0:T(8,128)(2,1)S(1)}, ...), branch_computations={%region_4.6_spmd, %region_7.7_spmd} | conditional | flops 551554304 | bytes 18161734 | solution.py:220
  230.1 5.3 %conditional.3 = (f32[2,2,256]{2,1,0:T(2,128)S(1)}, f32[2,2,256]{2,1,0:T(2,128)S(1)}, f32[2,2,256,128]{3,2,1,0:T(8,128)S(1)}) conditional(s32[]{:T(128)} %convert_element_type.145, (s32[]{:T(128)}, s32[1024]{0:T(1024)S(1)}, s32[]{:T(128)}, s32[256]{0:T(256)S(1)}, bf16[16384,256]{0,1:T(8,128)(2,1)}, /*index=5*/bf16[2,2,256,128]{3,2,1,0:T(8,128)(2,1)S(1)}, ...), branch_computations={%region_4.6_spmd, %region_7.7_spmd} | conditional | flops 551554304 | bytes 18161734 | solution.py:220
  236.0 5.3 %conditional.3 = (f32[2,2,256]{2,1,0:T(2,128)S(1)}, f32[2,2,256]{2,1,0:T(2,128)S(1)}, f32[2,2,256,128]{3,2,1,0:T(8,128)S(1)}) conditional(s32[]{:T(128)} %convert_element_type.145, (s32[]{:T(128)}, s32[1024]{0:T(1024)S(1)}, s32[]{:T(128)}, s32[256]{0:T(256)S(1)}, bf16[16384,256]{0,1:T(8,128)(2,1)}, /*index=5*/bf16[2,2,256,128]{3,2,1,0:T(8,128)(2,1)S(1)}, ...), branch_computations={%region_4.6_spmd, %region_7.7_spmd} | conditional | flops 551554304 | bytes 18161734 | solution.py:220
  247.9 5.3 %conditional.3 = (f32[2,2,256]{2,1,0:T(2,128)S(1)}, f32[2,2,256]{2,1,0:T(2,128)S(1)}, f32[2,2,256,128]{3,2,1,0:T(8,128)S(1)}) conditional(s32[]{:T(128)} %convert_element_type.145, (s32[]{:T(128)}, s32[1024]{0:T(1024)S(1)}, s32[]{:T(128)}, s32[256]{0:T(256)S(1)}, bf16[16384,256]{0,1:T(8,128)(2,1)}, /*index=5*/bf16[2,2,256,128]{3,2,1,0:T(8,128)(2,1)S(1)}, ...), branch_computations={%region_4.6_spmd, %region_7.7_spmd} | conditional | flops 551554304 | bytes 18161734 | solution.py:220
  253.9 5.3 %conditional.3 = (f32[2,2,256]{2,1,0:T(2,128)S(1)}, f32[2,2,256]{2,1,0:T(2,128)S(1)}, f32[2,2,256,128]{3,2,1,0:T(8,128)S(1)}) conditional(s32[]{:T(128)} %convert_element_type.145, (s32[]{:T(128)}, s32[1024]{0:T(1024)S(1)}, s32[]{:T(128)}, s32[256]{0:T(256)S(1)}, bf16[16384,256]{0,1:T(8,128)(2,1)}, /*index=5*/bf16[2,2,256,128]{3,2,1,0:T(8,128)(2,1)S(1)}, ...), branch_computations={%region_4.6_spmd, %region_7.7_spmd} | conditional | flops 551554304 | bytes 18161734 | solution.py:220
  259.8 5.3 %conditional.3 = (f32[2,2,256]{2,1,0:T(2,128)S(1)}, f32[2,2,256]{2,1,0:T(2,128)S(1)}, f32[2,2,256,128]{3,2,1,0:T(8,128)S(1)}) conditional(s32[]{:T(128)} %convert_element_type.145, (s32[]{:T(128)}, s32[1024]{0:T(1024)S(1)}, s32[]{:T(128)}, s32[256]{0:T(256)S(1)}, bf16[16384,256]{0,1:T(8,128)(2,1)}, /*index=5*/bf16[2,2,256,128]{3,2,1,0:T(8,128)(2,1)S(1)}, ...), branch_computations={%region_4.6_spmd, %region_7.7_spmd} | conditional | flops 551554304 | bytes 18161734 | solution.py:220
  265.8 5.3 %conditional.3 = (f32[2,2,256]{2,1,0:T(2,128)S(1)}, f32[2,2,256]{2,1,0:T(2,128)S(1)}, f32[2,2,256,128]{3,2,1,0:T(8,128)S(1)}) conditional(s32[]{:T(128)} %convert_element_type.145, (s32[]{:T(128)}, s32[1024]{0:T(1024)S(1)}, s32[]{:T(128)}, s32[256]{0:T(256)S(1)}, bf16[16384,256]{0,1:T(8,128)(2,1)}, /*index=5*/bf16[2,2,256,128]{3,2,1,0:T(8,128)(2,1)S(1)}, ...), branch_computations={%region_4.6_spmd, %region_7.7_spmd} | conditional | flops 551554304 | bytes 18161734 | solution.py:220
  271.7 5.3 %conditional.3 = (f32[2,2,256]{2,1,0:T(2,128)S(1)}, f32[2,2,256]{2,1,0:T(2,128)S(1)}, f32[2,2,256,128]{3,2,1,0:T(8,128)S(1)}) conditional(s32[]{:T(128)} %convert_element_type.145, (s32[]{:T(128)}, s32[1024]{0:T(1024)S(1)}, s32[]{:T(128)}, s32[256]{0:T(256)S(1)}, bf16[16384,256]{0,1:T(8,128)(2,1)}, /*index=5*/bf16[2,2,256,128]{3,2,1,0:T(8,128)(2,1)S(1)}, ...), branch_computations={%region_4.6_spmd, %region_7.7_spmd} | conditional | flops 551554304 | bytes 18161734 | solution.py:220
  277.7 5.3 %conditional.3 = (f32[2,2,256]{2,1,0:T(2,128)S(1)}, f32[2,2,256]{2,1,0:T(2,128)S(1)}, f32[2,2,256,128]{3,2,1,0:T(8,128)S(1)}) conditional(s32[]{:T(128)} %convert_element_type.145, (s32[]{:T(128)}, s32[1024]{0:T(1024)S(1)}, s32[]{:T(128)}, s32[256]{0:T(256)S(1)}, bf16[16384,256]{0,1:T(8,128)(2,1)}, /*index=5*/bf16[2,2,256,128]{3,2,1,0:T(8,128)(2,1)S(1)}, ...), branch_computations={%region_4.6_spmd, %region_7.7_spmd} | conditional | flops 551554304 | bytes 18161734 | solution.py:220
  295.5 5.3 %conditional.3 = (f32[2,2,256]{2,1,0:T(2,128)S(1)}, f32[2,2,256]{2,1,0:T(2,128)S(1)}, f32[2,2,256,128]{3,2,1,0:T(8,128)S(1)}) conditional(s32[]{:T(128)} %convert_element_type.145, (s32[]{:T(128)}, s32[1024]{0:T(1024)S(1)}, s32[]{:T(128)}, s32[256]{0:T(256)S(1)}, bf16[16384,256]{0,1:T(8,128)(2,1)}, /*index=5*/bf16[2,2,256,128]{3,2,1,0:T(8,128)(2,1)S(1)}, ...), branch_computations={%region_4.6_spmd, %region_7.7_spmd} | conditional | flops 551554304 | bytes 18161734 | solution.py:220
  304.5 33.0 %shard_map.148 = bf16[256,2048]{1,0:T(8,128)(2,1)} custom-call(bf16[256,2048]{1,0:T(8,128)(2,1)} %convolution_convert_fusion.x_ref), custom_call_target="tpu_custom_call" | custom-call | tf_op jit(solution)/shard_map/pallas_call | solution.py:86
  342.0 6.2 %convolution_convert_fusion.1.x_ref = bf16[256,2048]{1,0:T(8,128)(2,1)} fusion(bf16[2048,768]{1,0:T(8,128)(2,1)} %reshape.157, bf16[2048,768]{1,0:T(8,128)(2,1)} %reshape.156, f32[256,768]{1,0:T(8,128)} %fusion.26, bf16[256,2048]{1,0:T(8,128)(2,1)S(1)} %get-tuple-element.572, f32[2048]{0:T(1024)S(1)} %copy-done.9, f32[256]{0:T(256)S(1)} %add_rsqrt_fusion.2), kind=kOutput, calls=%fused_computation.26 | convolution fusion | flops 1614413824 | bytes 9184256 | tf_op jit(solution)/shard_map/dot_general | solution.py:233
  348.2 30.1 %shard_map.149 = bf16[256,2048]{1,0:T(8,128)(2,1)} custom-call(bf16[256,2048]{1,0:T(8,128)(2,1)} %convolution_convert_fusion.1.x_ref), custom_call_target="tpu_custom_call" | custom-call | tf_op jit(solution)/shard_map/pallas_call | solution.py:86
  (246 shorter events, 121.9 us)
Async XLA Ops:
  7.2 295.6 %copy-start = (bf16[512,2048]{1,0:T(8,128)(2,1)S(1)}, bf16[512,2048]{1,0:T(8,128)(2,1)}, u32[]{:S(2)}) copy-start(bf16[512,2048]{1,0:T(8,128)(2,1)} %param.23) | copy-start | bytes 6291460
  7.2 10.4 %copy-start.1 = (bf16[256,2048]{1,0:T(8,128)(2,1)S(1)}, bf16[256,2048]{1,0:T(8,128)(2,1)}, u32[]{:S(2)}) copy-start(bf16[256,2048]{1,0:T(8,128)(2,1)} %param.18) | copy-start | bytes 3145732
  7.2 136.9 %all-gather.3.cloned.1.call-start = ((), (), s32[]{:S(2)}) async-start(), calls=%async_computation | async-start | bytes 26624000 | tf_op jit(solution)/shard_map/all_gather | solution.py:154
  15.2 4.4 %copy-start.7 = (f32[128]{0:T(128)S(1)}, f32[128]{0:T(128)}, u32[]{:S(2)}) copy-start(f32[128]{0:T(128)} %param.25) | copy-start | bytes 1540
  15.3 4.5 %copy-start.3 = (bf16[48,512]{0,1:T(8,128)(2,1)S(1)}, bf16[48,512]{0,1:T(8,128)(2,1)}, u32[]{:S(2)}) copy-start(bf16[48,512]{0,1:T(8,128)(2,1)} %copy.80) | copy-start | bytes 147460
  15.3 4.5 %copy-start.4 = (bf16[48,512]{0,1:T(8,128)(2,1)S(1)}, bf16[48,512]{0,1:T(8,128)(2,1)}, u32[]{:S(2)}) copy-start(bf16[48,512]{0,1:T(8,128)(2,1)} %copy.79) | copy-start | bytes 147460
  15.3 4.5 %copy-start.5 = (bf16[48,512]{0,1:T(8,128)(2,1)S(1)}, bf16[48,512]{0,1:T(8,128)(2,1)}, u32[]{:S(2)}) copy-start(bf16[48,512]{0,1:T(8,128)(2,1)} %copy.78) | copy-start | bytes 147460
  17.6 2.1 copy-start.6
  25.8 4.8 %copy-start.8 = (f32[128]{0:T(128)S(1)}, f32[128]{0:T(128)}, u32[]{:S(2)}) copy-start(f32[128]{0:T(128)} %param.24) | copy-start | bytes 1540
  304.5 35.2 %copy-start.9 = (f32[2048]{0:T(1024)S(1)}, f32[2048]{0:T(1024)}, u32[]{:S(2)}) copy-start(f32[2048]{0:T(1024)} %param.27) | copy-start | bytes 24580
  337.5 2.5 copy-start.2
Sparse Core Ops, SparseCore 0:
  22.9 121.1 all-gather.2

commit v3 on v2

--- a/solution.py
+++ b/solution.py
@@ -98,6 +98,98 @@
         ],
         compiler_params=pltpu.CompilerParams(collective_id=collective_id, has_side_effects=True),
     )(x)
+
+
+def attention_kernel(info, q_ref, q_last_ref, q_first_ref, kv_ref, o_ref, top_ref, total_ref, acc_ref):
+    step = pl.program_id(0)
+    groups, rows_all, head_size = q_ref.shape
+    shards_per, rows, _ = kv_ref.shape
+    width = shards_per * rows
+    half = kv_ref.shape[2] // 2
+    rows_q = o_ref.shape[0]
+    per_group = rows_all // rows_q
+    scale = 1.0 / math.sqrt(head_size)
+
+    @pl.when(step == 0)
+    def _():
+        top_ref[...] = jnp.full(top_ref.shape, -1e30, jnp.float32)
+        total_ref[...] = jnp.zeros(total_ref.shape, jnp.float32)
+        acc_ref[...] = jnp.zeros(acc_ref.shape, jnp.float32)
+
+    offset = step * width
+    needed = (step >= info[0]) & (step <= info[1])
+    whole = (offset >= info[2]) & (offset + width - 1 <= info[3])
+
+    def run(masked):
+        for g in range(groups):
+            q = q_ref[g]
+            k = kv_ref[:, :, g * head_size : (g + 1) * head_size].reshape(width, head_size)
+            v = kv_ref[:, :, half + g * head_size : half + (g + 1) * head_size].reshape(width, head_size)
+            s = lax.dot_general(q, k, (((1,), (1,)), ((), ())), preferred_element_type=jnp.float32) * scale
+            if masked:
+                k_index = offset + lax.broadcasted_iota(jnp.int32, s.shape, 1)
+                allowed = (k_index <= q_last_ref[...]) & (k_index >= q_first_ref[...])
+                s = jnp.where(allowed, s, -1e30)
+            top = top_ref[g]
+            new_top = jnp.maximum(top, jnp.max(s, axis=-1, keepdims=True))
+            p = jnp.exp(s - new_top)
+            if masked:
+                p = jnp.where(allowed, p, 0.0)
+            decay = jnp.exp(top - new_top)
+            total_ref[g] = total_ref[g] * decay + jnp.sum(p, axis=-1, keepdims=True)
+            acc_ref[g] = acc_ref[g] * decay + jnp.dot(
+                p.astype(jnp.bfloat16), v, preferred_element_type=jnp.float32
+            )
+            top_ref[g] = new_top
+
+    @pl.when(needed & whole)
+    def _():
+        run(False)
+
+    @pl.when(needed & jnp.logical_not(whole))
+    def _():
+        run(True)
+
+    @pl.when(step == pl.num_programs(0) - 1)
+    def _():
+        for g in range(groups):
+            out = acc_ref[g] / total_ref[g]
+            for h in range(per_group):
+                col = (g * per_group + h) * head_size
+                o_ref[:, col : col + head_size] = out[h * rows_q : (h + 1) * rows_q].astype(o_ref.dtype)
+
+
+def attention(q_grouped, q_last, q_first, gathered, info, rows, kv_rows_per_shard, shards_per):
+    groups, rows_all, head_size = q_grouped.shape
+    shards, _, width_all = gathered.shape
+    blocks = shards // shards_per
+    out_cols = rows_all // rows * groups * head_size
+
+    def kv_map(j, info):
+        return (jnp.minimum(jnp.maximum(j, info[0]), info[1]), 0, 0)
+
+    grid_spec = pltpu.PrefetchScalarGridSpec(
+        num_scalar_prefetch=1,
+        grid=(blocks,),
+        in_specs=[
+            pl.BlockSpec((groups, rows_all, head_size), lambda j, info: (0, 0, 0)),
+            pl.BlockSpec((rows_all, 1), lambda j, info: (0, 0)),
+            pl.BlockSpec((rows_all, 1), lambda j, info: (0, 0)),
+            pl.BlockSpec((shards_per, kv_rows_per_shard, width_all), kv_map),
+        ],
+        out_specs=pl.BlockSpec((rows, out_cols), lambda j, info: (0, 0)),
+        scratch_shapes=[
+            pltpu.VMEM((groups, rows_all, 1), jnp.float32),
+            pltpu.VMEM((groups, rows_all, 1), jnp.float32),
+            pltpu.VMEM((groups, rows_all, head_size), jnp.float32),
+        ],
+    )
+    return pl.pallas_call(
+        attention_kernel,
+        out_shape=jax.ShapeDtypeStruct((rows, out_cols), jnp.bfloat16),
+        grid_spec=grid_spec,
+        compiler_params=pltpu.CompilerParams(dimension_semantics=("arbitrary",)),
+    )(info, q_grouped, q_last, q_first, gathered)
 
 
 def body(
@@ -152,10 +244,6 @@
         axis=0,
     )
     gathered = lax.all_gather(packed, "seq", axis=0, tiled=False)
-    kv_rows = gathered[:, :rows].reshape(shards * rows, width_all)
-    key_rows = kv_rows[:, :kv_cols]
-    value_rows = kv_rows[:, kv_cols:]
-
     def weight_part(k):
         lo = rows + k * w_rows
         return gathered[:, lo : lo + w_rows].reshape(shards * ff_rows, ff_local)
@@ -164,64 +252,25 @@
     up_w = weight_part(1)
     down_wt = weight_part(2)
 
-    grouped = query_matrix.reshape(rows, kv_local, head_group, head_size).transpose(1, 2, 0, 3)
     me = lax.axis_index("seq")
     first = me * rows
     my_last = first + rows - 1
     q_index = first + jnp.arange(rows, dtype=jnp.int32)
     q_start = q_index - positions
-    my_start = q_start[0]
-
-    def update(state, key_blk, value_blk, k_index):
-        top, total, acc = state
-        count = key_blk.shape[0]
-        s = (
-            jnp.einsum(
-                "hgqd,khd->hgqk",
-                grouped,
-                key_blk.reshape(count, kv_local, head_size),
-                preferred_element_type=jnp.float32,
-            )
-            * scale
-        )
-        allowed = (k_index[None, :] <= q_index[:, None]) & (k_index[None, :] >= q_start[:, None])
-        s = jnp.where(allowed, s, -1e30)
-        new_top = jnp.maximum(top, jnp.max(s, axis=-1))
-        p = jnp.where(allowed, jnp.exp(s - new_top[..., None]), 0.0)
-        decay = jnp.exp(top - new_top)
-        total = total * decay + jnp.sum(p, axis=-1)
-        acc = acc * decay[..., None] + jnp.einsum(
-            "hgqk,khd->hgqd",
-            p.astype(jnp.bfloat16),
-            value_blk.reshape(count, kv_local, head_size),
-            preferred_element_type=jnp.float32,
-        )
-        return (new_top, total, acc)
-
-    start_state = (
-        jnp.full((kv_local, head_group, rows), -1e30, jnp.float32),
-        jnp.zeros((kv_local, head_group, rows), jnp.float32),
-        jnp.zeros((kv_local, head_group, rows, head_size), jnp.float32),
-    )
-    count = key_rows.shape[0]
-    limit = max(1, 1024 // rows)
-    factor = 1
-    for trial in range(1, limit + 1):
+    shards_per = 1
+    for trial in range(1, max(1, 1024 // rows) + 1):
         if shards % trial == 0:
-            factor = trial
-    width = rows * factor
-
-    def one_block(step, inner):
-        offset = step * width
-        kb = lax.dynamic_slice_in_dim(key_rows, offset, width, 0)
-        vb = lax.dynamic_slice_in_dim(value_rows, offset, width, 0)
-        k_index = offset + jnp.arange(width, dtype=jnp.int32)
-        skip = (offset > my_last) | (offset + width - 1 < my_start)
-        return lax.cond(skip, lambda c: c, lambda c: update(c, kb, vb, k_index), inner)
-
-    top, total, acc = lax.fori_loop(0, count // width, one_block, start_state)
-    attended = (acc / total[..., None]).astype(jnp.bfloat16)
-    attended = attended.transpose(2, 0, 1, 3).reshape(rows, query_local * head_size)
+            shards_per = trial
+    width = rows * shards_per
+    info = jnp.stack([q_start[0] // width, my_last // width, q_start[rows - 1], first])
+    q_grouped = (
+        query_matrix.reshape(rows, kv_local, head_group, head_size)
+        .transpose(1, 2, 0, 3)
+        .reshape(kv_local, head_group * rows, head_size)
+    )
+    q_last = jnp.tile(q_index, head_group).reshape(head_group * rows, 1)
+    q_first = jnp.tile(q_start, head_group).reshape(head_group * rows, 1)
+    attended = attention(q_grouped, q_last, q_first, gathered, info, rows, rows, shards_per)
     partial_out = jnp.dot(attended, w_out, preferred_element_type=jnp.float32)
     summed = tp_sum(partial_out.astype(jnp.bfloat16), 0).astype(jnp.float32)
     mid = (xf + summed).astype(jnp.bfloat16)

time: 390 us -> 297 us (0.76)
  local copies, waits for them, and re-layouts: 103 us -> 37.4 us
  Pallas kernels: 63.1 us -> 103 us
  matrix products: 53.3 us -> 19.5 us
  other arithmetic: 29.1 us -> 13 us
  loops' own time: 12.2 us -> 0 us
  waiting for transfers between devices: 112 us -> 106 us
    pallas_call x0 -> x1, Pallas kernels: none -> 40.1 us  [attention(): pl.pallas_call(attention_kernel, out_shape=jax.ShapeDtypeStruct((rows, ou...]
    dot_general x28 -> x0, matrix products: 36 us -> none  [the longest x14 22.9 us: update(): jnp.einsum('hgqk,khd->hgqd', p.astype(jnp.bfloat16), value_blk.reshape(co...]
    slice x3 -> x1, local copies, waits for them, and re-layouts: 25.7 us -> 0.59 us  [body(): q_start[0] // width]
    unnamed x24 -> x26, local copies, waits for them, and re-layouts: 26.6 us -> 3.3 us
    dynamic_slice x14 -> x0, local copies, waits for them, and re-layouts: 17.9 us -> none  [one_block(): vb = lax.dynamic_slice_in_dim(value_rows, offset, width, 0)]
    reduce_sum x14 -> x0, other arithmetic: 14.5 us -> none  [update(): total = total * decay + jnp.sum(p, axis=-1)]
    another operation x17 -> x0, loops' own time: 12.2 us -> none  [the longest x1 11.1 us: body(): top, total, acc = lax.fori_loop(0, count // width, one_block, start_state)]
    all_gather x1, waiting for transfers between devices: 112 us -> 106 us  [body(): gathered = lax.all_gather(packed, 'seq', axis=0, tiled=False)]
  transfers between devices with their start and end apart: 1 -> 1, of which waited for: 1 -> 1; matrix products, arithmetic and copies ran while one was open for 2% -> 4% of each run, Pallas kernels for 0% -> 0%
where the time goes in v3:
time: 297 us; the launch traced here: 296 us
  waiting for transfers between devices  106 us (36%)
  Pallas kernels  103 us (35%)
  local copies, waits for them, and re-layouts  37.4 us (13%)
  matrix products  19.5 us (7%)
  between operations  16.9 us (6%)
  other arithmetic  13 us (4%)
    all_gather x1, waiting for transfers between devices, body(): gathered = lax.all_gather(packed, 'seq', axis=0, tiled=False)  106 us
    pallas_call x2, Pallas kernels, tp_sum(): pl.pallas_call(functools.partial(tp_sum_kernel, n), out_shape=jax.ShapeDt...  63.1 us
    pallas_call x1, Pallas kernels, attention(): pl.pallas_call(attention_kernel, out_shape=jax.ShapeDtypeStruct((rows, ou...  40.1 us
    reshape x3, local copies, waits for them, and re-layouts, weight_part(): return gathered[:, lo:lo + w_rows].reshape(shards * ff_rows, ff_local)  17.7 us
    slice x1, local copies, waits for them, and re-layouts, weight_part(): return gathered[:, lo:lo + w_rows].reshape(shards * ff_rows, ff_local)  6.76 us
    dot_general x1, matrix products, body(): lax.dot_general(act, down_wt, (((1,), (1,)), ((), ())), preferred_element...  6.25 us
  transfers between devices with their start and end apart: 1, of which 1 were waited for; matrix products, arithmetic and copies ran while one was open for 4% of the time, Pallas kernels for 0%

profile of v3, /device:TPU:196, one launch (start us, length us, event | category | flops | bytes accessed | tf_op | source)
XLA Modules:
  0.0 296.2 jit_solution(8721108939428463504)
XLA Ops:
  7.2 1.6 fusion
  8.9 0.9 reshape.135
  13.8 2.3 convolution_convert_fusion.2
  16.2 1.4 multiply_reduce_fusion.1
  17.9 1.0 multiply_multiply_fusion.1
  19.0 2.0 pad_maximum_fusion
  21.0 2.0 copy.69
  28.6 0.9 copy.75
  30.3 3.2 %fusion.19 = f32[256,512]{1,0:T(8,128)} fusion(bf16[2048,512]{1,0:T(8,128)(2,1)} %param.16, bf16[256,2048]{1,0:T(8,128)(2,1)S(1)} %copy-done.1, f32[2048]{0:T(1024)} %param.15, f32[256]{0:T(256)S(1)} %add_rsqrt_fusion.3), kind=kOutput, calls=%fused_computation.46 | convolution fusion | flops 538968064 | bytes 3679232 | tf_op jit(solution)/shard_map/dot_general | solution.py:221
  33.5 1.2 reshape.132
  36.1 1.2 pad_add_fusion.info
  38.2 106.2 %all-gather.3.cloned.1.call-done = bf16[25600,512]{1,0:T(8,128)(2,1)} async-done(((bf16[400,512]{1,0:T(8,128)(2,1)}), bf16[25600,512]{1,0:T(8,128)(2,1)}) %all-gather.3.cloned.1.call-update) | async-done | bytes 26214416 | tf_op jit(solution)/shard_map/all_gather | solution.py:246
  144.3 6.8 %fusion.22 = (bf16[64,48,512]{2,1,0:T(8,128)(2,1)}, bf16[64,48,512]{2,1,0:T(8,128)(2,1)}, bf16[64,48,512]{2,1,0:T(8,128)(2,1)}) fusion(bf16[64,400,512]{2,1,0:T(8,128)(2,1)} %bitcast.33), kind=kLoop, calls=%fused_computation.47 | loop fusion | bytes 18874368 | tf_op jit(solution)/shard_map/slice | solution.py:249
  151.1 5.9 %reshape.138 = bf16[2048,768]{1,0:T(8,128)(2,1)} reshape(bf16[64,48,512]{2,1,0:T(8,128)(2,1)} %get-tuple-element.20) | data formatting | bytes 6291456 | tf_op jit(solution)/shard_map/reshape | solution.py:249
  157.0 40.1 %shard_map.148 = bf16[256,512]{1,0:T(8,128)(2,1)} custom-call(s32[4]{0:T(128)} %pad_add_fusion.info, bf16[2,512,128]{2,1,0:T(8,128)(2,1)} %bitcast.37, s32[512,1]{1,0:T(8,128)} %bitcast.38, s32[512,1]{1,0:T(8,128)} %bitcast.39, bf16[64,400,512]{2,1,0:T(8,128)(2,1)} %bitcast.34), custom_call_target="tpu_custom_call" | custom-call | tf_op jit(solution)/shard_map/pallas_call | solution.py:187
  197.2 2.6 convolution_convert_fusion.x_ref
  199.8 33.0 %shard_map.149 = bf16[256,2048]{1,0:T(8,128)(2,1)} custom-call(bf16[256,2048]{1,0:T(8,128)(2,1)} %convolution_convert_fusion.x_ref), custom_call_target="tpu_custom_call" | custom-call | tf_op jit(solution)/shard_map/pallas_call | solution.py:86
  232.8 2.0 fusion.4
  234.8 5.9 %reshape.140 = bf16[2048,768]{1,0:T(8,128)(2,1)} reshape(bf16[64,48,512]{2,1,0:T(8,128)(2,1)} %get-tuple-element.21) | data formatting | bytes 6291456 | tf_op jit(solution)/shard_map/reshape | solution.py:249
  240.7 5.9 %reshape.139 = bf16[2048,768]{1,0:T(8,128)(2,1)} reshape(bf16[64,48,512]{2,1,0:T(8,128)(2,1)} %get-tuple-element.22) | data formatting | bytes 6291456 | tf_op jit(solution)/shard_map/reshape | solution.py:249
  246.6 3.8 %fusion.12 = f32[256,768]{1,0:T(8,128)} fusion(bf16[2048,768]{1,0:T(8,128)(2,1)} %reshape.138, bf16[256,2048]{1,0:T(8,128)(2,1)S(1)} %get-tuple-element.19, f32[2048]{0:T(1024)S(1)} %copy-done.8, f32[256]{0:T(256)S(1)} %add_rsqrt_fusion.2), kind=kOutput, calls=%fused_computation.25 | convolution fusion | flops 807403520 | bytes 4989952 | tf_op jit(solution)/shard_map/dot_general | solution.py:279
  250.5 6.3 %convolution_convert_fusion.1.x_ref = bf16[256,2048]{1,0:T(8,128)(2,1)} fusion(bf16[2048,768]{1,0:T(8,128)(2,1)} %reshape.140, bf16[2048,768]{1,0:T(8,128)(2,1)} %reshape.139, f32[256,768]{1,0:T(8,128)} %fusion.12, bf16[256,2048]{1,0:T(8,128)(2,1)S(1)} %get-tuple-element.19, f32[2048]{0:T(1024)S(1)} %copy-done.8, f32[256]{0:T(256)S(1)} %add_rsqrt_fusion.2), kind=kOutput, calls=%fused_computation.7 | convolution fusion | flops 1614413824 | bytes 9184256 | tf_op jit(solution)/shard_map/dot_general | solution.py:282
  256.7 30.1 %shard_map.150 = bf16[256,2048]{1,0:T(8,128)(2,1)} custom-call(bf16[256,2048]{1,0:T(8,128)(2,1)} %convolution_convert_fusion.1.x_ref), custom_call_target="tpu_custom_call" | custom-call | tf_op jit(solution)/shard_map/pallas_call | solution.py:86
  286.8 2.6 fusion.7
  (50 shorter events, 10.4 us)
Async XLA Ops:
  7.2 190.0 %copy-start = (bf16[512,2048]{1,0:T(8,128)(2,1)S(1)}, bf16[512,2048]{1,0:T(8,128)(2,1)}, u32[]{:S(2)}) copy-start(bf16[512,2048]{1,0:T(8,128)(2,1)} %param.19) | copy-start | bytes 6291460
  7.2 137.2 %all-gather.3.cloned.1.call-start = ((), (), s32[]{:S(2)}) async-start(), calls=%async_computation | async-start | bytes 26624000 | tf_op jit(solution)/shard_map/all_gather | solution.py:246
  8.9 7.2 %copy-start.1 = (bf16[256,2048]{1,0:T(8,128)(2,1)S(1)}, bf16[256,2048]{1,0:T(8,128)(2,1)}, u32[]{:S(2)}) copy-start(bf16[256,2048]{1,0:T(8,128)(2,1)} %param.14) | copy-start | bytes 3145732
  8.9 7.2 %copy-start.7 = (f32[2048]{0:T(1024)S(1)}, f32[2048]{0:T(1024)}, u32[]{:S(2)}) copy-start(f32[2048]{0:T(1024)} %param.15) | copy-start | bytes 24580
  13.8 2.3 copy-start.6
  16.2 1.4 copy-start.3
  16.2 1.7 copy-start.4
  30.3 4.8 %copy-start.5 = (f32[128]{0:T(128)S(1)}, f32[128]{0:T(128)}, u32[]{:S(2)}) copy-start(f32[128]{0:T(128)} %param.20) | copy-start | bytes 1540
  33.5 2.0 copy-start.2
  240.7 5.9 %copy-start.8 = (f32[2048]{0:T(1024)S(1)}, f32[2048]{0:T(1024)}, u32[]{:S(2)}) copy-start(f32[2048]{0:T(1024)} %param.23) | copy-start | bytes 24580
Sparse Core Ops, SparseCore 0:
  23.2 121.1 all-gather.2

commit v4 on v3

--- a/solution.py
+++ b/solution.py
@@ -233,24 +233,34 @@
 
     width_all = 2 * kv_cols
     ff_rows, ff_local = w_gate.shape
-    w_rows = ff_rows * ff_local // width_all
+    rest = ff_local - width_all
+    down_t = w_down.T
     packed = jnp.concatenate(
         [
             jnp.concatenate([key_cache, value_cache], axis=1),
-            w_gate.reshape(w_rows, width_all),
-            w_up.reshape(w_rows, width_all),
-            w_down.T.reshape(w_rows, width_all),
+            w_gate[:, :width_all],
+            w_up[:, :width_all],
+            down_t[:, :width_all],
+            jnp.concatenate([w_gate[:, width_all:], w_up[:, width_all:]], axis=1),
+            jnp.concatenate(
+                [down_t[:, width_all:], jnp.zeros((ff_rows, 2 * width_all - ff_local), down_t.dtype)],
+                axis=1,
+            ),
         ],
         axis=0,
     )
     gathered = lax.all_gather(packed, "seq", axis=0, tiled=False)
-    def weight_part(k):
-        lo = rows + k * w_rows
-        return gathered[:, lo : lo + w_rows].reshape(shards * ff_rows, ff_local)
-
-    gate_w = weight_part(0)
-    up_w = weight_part(1)
-    down_wt = weight_part(2)
+
+    def weight_part(k, lo, hi):
+        top = rows + k * ff_rows
+        return gathered[:, top : top + ff_rows, lo:hi].reshape(shards * ff_rows, hi - lo)
+
+    gate_a = weight_part(0, 0, width_all)
+    up_a = weight_part(1, 0, width_all)
+    down_a = weight_part(2, 0, width_all)
+    gate_b = weight_part(3, 0, rest)
+    up_b = weight_part(3, rest, 2 * rest)
+    down_b = weight_part(4, 0, rest)
 
     me = lax.axis_index("seq")
     first = me * rows
@@ -276,12 +286,15 @@
     mid = (xf + summed).astype(jnp.bfloat16)
     mid_f = mid.astype(jnp.float32)
     post_normed = rms(mid_f, post_gain).astype(jnp.bfloat16)
-    gate = jnp.dot(post_normed, gate_w, preferred_element_type=jnp.float32)
-    up = jnp.dot(post_normed, up_w, preferred_element_type=jnp.float32)
-    act = (jax.nn.silu(gate) * up).astype(jnp.bfloat16)
-    terms = lax.dot_general(
-        act, down_wt, (((1,), (1,)), ((), ())), preferred_element_type=jnp.float32
-    )
+    def ffn_piece(gate_w, up_w, down_w):
+        gate = jnp.dot(post_normed, gate_w, preferred_element_type=jnp.float32)
+        up = jnp.dot(post_normed, up_w, preferred_element_type=jnp.float32)
+        act = (jax.nn.silu(gate) * up).astype(jnp.bfloat16)
+        return lax.dot_general(
+            act, down_w, (((1,), (1,)), ((), ())), preferred_element_type=jnp.float32
+        )
+
+    terms = ffn_piece(gate_a, up_a, down_a) + ffn_piece(gate_b, up_b, down_b)
     ffn_total = tp_sum(terms.astype(jnp.bfloat16), 1).astype(jnp.float32)
     hidden = (mid_f + ffn_total).astype(jnp.bfloat16)
     return (hidden, key_cache, value_cache)

time: 297 us -> 295 us (level)
  the two profiles are of different devices: /device:TPU:196 before, /device:TPU:228 now
where the time goes in v4:
time: 295 us; the launch traced here: 294 us
  Pallas kernels  106 us (36%)
  waiting for transfers between devices  102 us (35%)
  local copies, waits for them, and re-layouts  30.2 us (10%)
  matrix products  21.4 us (7%)
  other arithmetic  17.3 us (6%)
  between operations  16.9 us (6%)
    all_gather x1, waiting for transfers between devices, body(): gathered = lax.all_gather(packed, 'seq', axis=0, tiled=False)  102 us
    pallas_call x2, Pallas kernels, tp_sum(): pl.pallas_call(functools.partial(tp_sum_kernel, n), out_shape=jax.ShapeDt...  63.1 us
    pallas_call x1, Pallas kernels, attention(): pl.pallas_call(attention_kernel, out_shape=jax.ShapeDtypeStruct((rows, ou...  42.8 us
    dot_general x2, matrix products, ffn_piece(): lax.dot_general(act, down_w, (((1,), (1,)), ((), ())), preferred_element_...  10.1 us
    slice x2, local copies, waits for them, and re-layouts, weight_part(): gathered[:, top:top + ff_rows, lo:hi].reshape(shards * ff_rows, hi - lo)  9.45 us
    unnamed x35, local copies, waits for them, and re-layouts  8.03 us
  transfers between devices with their start and end apart: 1, of which 1 were waited for; matrix products, arithmetic and copies ran while one was open for 6% of the time, Pallas kernels for 0%

profile of v4, /device:TPU:228, one launch (start us, length us, event | category | flops | bytes accessed | tf_op | source)
XLA Modules:
  0.0 293.6 jit_solution(4592368227528103507)
XLA Ops:
  10.1 1.7 fusion.1
  11.7 2.2 multiply_reduce_fusion.1
  14.1 1.3 convolution_convert_fusion.1
  21.2 1.5 concatenate.31
  22.7 2.0 concatenate.32
  24.7 2.0 copy.79
  32.5 1.7 copy.83
  34.2 3.2 %fusion.30 = f32[256,512]{1,0:T(8,128)} fusion(bf16[2048,512]{1,0:T(8,128)(2,1)} %param.16, bf16[256,2048]{1,0:T(8,128)(2,1)S(1)} %copy-done.1, f32[2048]{0:T(1024)} %param.15, f32[256]{0:T(256)S(1)} %add_rsqrt_fusion.3), kind=kOutput, calls=%fused_computation.62 | convolution fusion | flops 538968064 | bytes 3679232 | tf_op jit(solution)/shard_map/dot_general | solution.py:221
  37.3 2.0 reshape.132
  39.3 1.4 multiply_reduce_fusion
  40.8 1.4 multiply_multiply_fusion
  46.4 1.8 pad_maximum_fusion
  48.2 101.7 %all-gather.3.cloned.1.call-done = bf16[26624,512]{1,0:T(8,128)(2,1)} async-done(((bf16[416,512]{1,0:T(8,128)(2,1)}), bf16[26624,512]{1,0:T(8,128)(2,1)}) %all-gather.3.cloned.1.call-update) | async-done | bytes 27262992 | tf_op jit(solution)/shard_map/all_gather | solution.py:252
  150.0 5.8 %fusion.32 = (bf16[64,32,512]{2,1,0:T(8,128)(2,1)}, bf16[64,32,512]{2,1,0:T(8,128)(2,1)}, bf16[64,32,512]{2,1,0:T(8,128)(2,1)}) fusion(bf16[64,416,512]{2,1,0:T(8,128)(2,1)} %bitcast.46), kind=kLoop, calls=%fused_computation.63 | loop fusion | bytes 12582912 | tf_op jit(solution)/shard_map/slice | solution.py:256
  155.8 3.7 %fusion.33 = (bf16[64,32,256]{2,1,0:T(8,128)(2,1)}, bf16[64,32,256]{2,1,0:T(8,128)(2,1)}, bf16[64,32,256]{2,1,0:T(8,128)(2,1)}) fusion(bf16[64,416,512]{2,1,0:T(8,128)(2,1)} %bitcast.47), kind=kLoop, calls=%fused_computation.64 | loop fusion | bytes 6291456 | tf_op jit(solution)/shard_map/slice | solution.py:256
  159.4 42.8 %shard_map.148 = bf16[256,512]{1,0:T(8,128)(2,1)} custom-call(s32[4]{0:T(128)} %pad_add_fusion.info, bf16[2,512,128]{2,1,0:T(8,128)(2,1)} %bitcast.59, s32[512,1]{1,0:T(8,128)} %bitcast.61, s32[512,1]{1,0:T(8,128)} %bitcast.60, bf16[64,416,512]{2,1,0:T(8,128)(2,1)} %bitcast.48), custom_call_target="tpu_custom_call" | custom-call | tf_op jit(solution)/shard_map/pallas_call | solution.py:187
  202.3 2.6 convolution_convert_fusion.x_ref
  204.9 33.0 %shard_map.149 = bf16[256,2048]{1,0:T(8,128)(2,1)} custom-call(bf16[256,2048]{1,0:T(8,128)(2,1)} %convolution_convert_fusion.x_ref), custom_call_target="tpu_custom_call" | custom-call | tf_op jit(solution)/shard_map/pallas_call | solution.py:86
  237.9 1.7 fusion.5
  241.5 1.5 fusion.35
  243.4 4.5 %fusion.11 = f32[256,2048]{1,0:T(8,128)} fusion(bf16[2048,256]{1,0:T(8,128)(2,1)} %bitcast.50, bf16[256,2048]{1,0:T(8,128)(2,1)} %copy-done.3, bf16[2048,256]{1,0:T(8,128)(2,1)} %bitcast.51, f32[256,256]{1,0:T(8,128)S(1)} %fusion.36), kind=kOutput, calls=%fused_computation.22 | convolution fusion | flops 537264128 | bytes 5505024 | tf_op jit(solution)/shard_map/dot_general | solution.py:293
  247.9 5.6 %fusion.x_ref = bf16[256,2048]{1,0:T(8,128)(2,1)} fusion(f32[256,2048]{1,0:T(8,128)} %fusion.11, bf16[2048,512]{1,0:T(8,128)(2,1)} %bitcast.52, bf16[256,2048]{1,0:T(8,128)(2,1)} %copy-done.3, bf16[2048,512]{1,0:T(8,128)(2,1)} %bitcast.53, f32[256,512]{1,0:T(8,128)} %fusion.35), kind=kOutput, calls=%fused_computation.7 | convolution fusion | flops 1075576832 | bytes 8912896 | tf_op jit(solution)/shard_map/dot_general | solution.py:293
  253.5 30.1 %shard_map.150 = bf16[256,2048]{1,0:T(8,128)(2,1)} custom-call(bf16[256,2048]{1,0:T(8,128)(2,1)} %fusion.x_ref), custom_call_target="tpu_custom_call" | custom-call | tf_op jit(solution)/shard_map/pallas_call | solution.py:86
  283.6 3.1 %fusion.8 = bf16[256,2048]{1,0:T(8,128)(2,1)} fusion(bf16[256,2048]{1,0:T(8,128)(2,1)} %shard_map.150, bf16[256,2048]{1,0:T(8,128)(2,1)} %shard_map.149, bf16[256,2048]{1,0:T(8,128)(2,1)S(1)} %copy-done.1), kind=kLoop, calls=%fused_computation.16 | loop fusion | flops 4194304 | bytes 4194304 | tf_op jit(solution)/shard_map/convert_element_type | solution.py:299
  (68 shorter events, 18.4 us)
Async XLA Ops:
  7.2 195.1 %copy-start = (bf16[512,2048]{1,0:T(8,128)(2,1)S(1)}, bf16[512,2048]{1,0:T(8,128)(2,1)}, u32[]{:S(2)}) copy-start(bf16[512,2048]{1,0:T(8,128)(2,1)} %param.19) | copy-start | bytes 6291460
  7.2 142.8 %all-gather.3.cloned.1.call-start = ((), (), s32[]{:S(2)}) async-start(), calls=%async_computation | async-start | bytes 27688960 | tf_op jit(solution)/shard_map/all_gather | solution.py:252
  10.1 4.0 %copy-start.1 = (bf16[256,2048]{1,0:T(8,128)(2,1)S(1)}, bf16[256,2048]{1,0:T(8,128)(2,1)}, u32[]{:S(2)}) copy-start(bf16[256,2048]{1,0:T(8,128)(2,1)} %param.14) | copy-start | bytes 3145732
  10.1 4.0 %copy-start.11 = (f32[2048]{0:T(1024)S(1)}, f32[2048]{0:T(1024)}, u32[]{:S(2)}) copy-start(f32[2048]{0:T(1024)} %param.15) | copy-start | bytes 24580
  10.1 4.0 %copy-start.10 = (bf16[2048,256]{1,0:T(8,128)(2,1)S(1)}, bf16[2048,256]{1,0:T(8,128)(2,1)}, u32[]{:S(2)}) copy-start(bf16[2048,256]{1,0:T(8,128)(2,1)} %param.18) | copy-start | bytes 3145732
  14.0 1.4 slice-start
  14.0 1.4 slice-start.2
  14.0 2.2 slice-start.1
  14.0 2.9 slice-start.3
  19.4 0.9 copy-start.6
  19.4 0.9 copy-start.7
  34.2 6.6 %copy-start.9 = (f32[128]{0:T(128)S(1)}, f32[128]{0:T(128)}, u32[]{:S(2)}) copy-start(f32[128]{0:T(128)} %param.20) | copy-start | bytes 1540
  204.9 34.8 %copy-start.8 = (f32[2048]{0:T(1024)S(1)}, f32[2048]{0:T(1024)}, u32[]{:S(2)}) copy-start(f32[2048]{0:T(1024)} %param.23) | copy-start | bytes 24580
  237.9 1.8 copy-start.2
  239.6 1.8 copy-start.5
  240.2 3.2 %copy-start.3 = (bf16[256,2048]{1,0:T(8,128)(2,1)}, bf16[256,2048]{1,0:T(8,128)(2,1)S(1)}, u32[]{:S(2)}) copy-start(bf16[256,2048]{1,0:T(8,128)(2,1)S(1)} %fusion.7) | copy-start | bytes 3145732
  240.2 2.8 copy-start.4
Sparse Core Ops, SparseCore 0:
  26.8 123.1 all-gather.2

commit v5 on v4

--- a/solution.py
+++ b/solution.py
@@ -30,12 +30,13 @@
 
 def tp_sum_kernel(n, x_ref, out_ref, slots, reduced, send1, recv1, send2, recv2):
     me = lax.axis_index("tp")
-    row = lax.axis_index("seq")
+    chip = lax.axis_index("chip")
+    core = lax.axis_index("core")
     cols = x_ref.shape[1] // n
 
     barrier = pltpu.get_barrier_semaphore()
     for k in range(1, n):
-        pl.semaphore_signal(barrier, inc=1, device_id=(row, lax.rem(me + k, n)), device_id_type=MESH)
+        pl.semaphore_signal(barrier, inc=1, device_id=(chip, core, lax.rem(me + k, n)), device_id_type=MESH)
     pl.semaphore_wait(barrier, n - 1)
 
     def block(ref, owner):
@@ -49,7 +50,7 @@
             dst_ref=slots.at[k],
             send_sem=send1.at[k],
             recv_sem=recv1.at[k],
-            device_id=(row, peer),
+            device_id=(chip, core, peer),
             device_id_type=MESH,
         )
         copy.start()
@@ -70,7 +71,7 @@
             dst_ref=block(out_ref, me),
             send_sem=send2.at[k],
             recv_sem=recv2.at[k],
-            device_id=(row, peer),
+            device_id=(chip, core, peer),
             device_id_type=MESH,
         )
         copy.start()
@@ -215,7 +216,7 @@
     kv_cols = kv_local * head_size
     head_group = query_local // kv_local
     scale = 1.0 / math.sqrt(head_size)
-    shards = lax.axis_size("seq")
+    shards = lax.axis_size("chip") * lax.axis_size("core")
     xf = layer_input.astype(jnp.float32)
     normed_input = rms(xf, norm_gain).astype(jnp.bfloat16)
     query_matrix = jnp.dot(normed_input, w_query, preferred_element_type=jnp.float32).reshape(
@@ -249,7 +250,10 @@
         ],
         axis=0,
     )
-    gathered = lax.all_gather(packed, "seq", axis=0, tiled=False)
+    half_gathered = lax.all_gather(packed, "chip", axis=0, tiled=False)
+    gathered = lax.all_gather(half_gathered, "core", axis=1, tiled=False).reshape(
+        (shards,) + packed.shape
+    )
 
     def weight_part(k, lo, hi):
         top = rows + k * ff_rows
@@ -262,7 +266,7 @@
     up_b = weight_part(3, rest, 2 * rest)
     down_b = weight_part(4, 0, rest)
 
-    me = lax.axis_index("seq")
+    me = lax.axis_index("chip") * lax.axis_size("core") + lax.axis_index("core")
     first = me * rows
     my_last = first + rows - 1
     q_index = first + jnp.arange(rows, dtype=jnp.int32)
@@ -301,8 +305,14 @@
 
 
 def solution(mesh):
+    devices = mesh.devices
+    per_chip = 2
+    split = jax.sharding.Mesh(
+        devices.reshape(devices.shape[0] // per_chip, per_chip, devices.shape[1]), ("chip", "core", "tp")
+    )
+    seq = ("chip", "core")
     in_specs = (
-        P("seq", None),
+        P(seq, None),
         P(),
         P(None, "tp"),
         P(None, "tp"),
@@ -310,12 +320,12 @@
         P("tp", None),
         P(),
         P(),
-        P("seq"),
-        P("seq"),
+        P(seq),
+        P(seq),
         P(),
-        P("seq", "tp"),
-        P("seq", "tp"),
-        P("tp", "seq"),
-    )
-    out_specs = (P("seq", None), P("seq", "tp"), P("seq", "tp"))
-    return jax.shard_map(body, mesh=mesh, in_specs=in_specs, out_specs=out_specs, check_vma=False)
+        P(seq, "tp"),
+        P(seq, "tp"),
+        P("tp", seq),
+    )
+    out_specs = (P(seq, None), P(seq, "tp"), P(seq, "tp"))
+    return jax.shard_map(body, mesh=split, in_specs=in_specs, out_specs=out_specs, check_vma=False)

time: 295 us -> 342 us (1.16)
  the two profiles are of different devices: /device:TPU:228 before, /device:TPU:192 now
where the time goes in v5:
time: 342 us; the launch traced here: 341 us
  waiting for transfers between devices  153 us (45%)
  Pallas kernels  103 us (30%)
  local copies, waits for them, and re-layouts  29.2 us (9%)
  matrix products  21.4 us (6%)
  other arithmetic  17.6 us (5%)
  between operations  17 us (5%)
    all_gather x1, waiting for transfers between devices, body(): half_gathered = lax.all_gather(packed, 'chip', axis=0, tiled=False)  124 us
    pallas_call x2, Pallas kernels, tp_sum(): pl.pallas_call(functools.partial(tp_sum_kernel, n), out_shape=jax.ShapeDt...  63.2 us
    pallas_call x1, Pallas kernels, attention(): pl.pallas_call(attention_kernel, out_shape=jax.ShapeDtypeStruct((rows, ou...  39.6 us
    all_gather x1, waiting for transfers between devices, body(): lax.all_gather(half_gathered, 'core', axis=1, tiled=False)  29.2 us
    dot_general x2, matrix products, ffn_piece(): lax.dot_general(act, down_w, (((1,), (1,)), ((), ())), preferred_element_...  10.1 us
    slice x2, local copies, waits for them, and re-layouts, weight_part(): gathered[:, top:top + ff_rows, lo:hi].reshape(shards * ff_rows, hi - lo)  9.41 us
    unnamed x41, local copies, waits for them, and re-layouts  7.98 us
  transfers between devices with their start and end apart: 2, of which 2 were waited for; matrix products, arithmetic and copies ran while one was open for 5% of the time, Pallas kernels for 0%

profile of v5, /device:TPU:192, one launch (start us, length us, event | category | flops | bytes accessed | tf_op | source)
XLA Modules:
  0.0 340.9 jit_solution(17599802741022224958)
XLA Ops:
  10.1 1.7 fusion.1
  11.7 2.2 multiply_reduce_fusion.1
  21.2 1.5 concatenate.31
  22.7 2.0 concatenate.32
  24.7 2.0 copy.79
  26.8 123.5 %all-gather.5.cloned.1.call-done = bf16[13312,512]{1,0:T(8,128)(2,1)} async-done(((bf16[416,512]{1,0:T(8,128)(2,1)}), bf16[13312,512]{1,0:T(8,128)(2,1)}) %all-gather.5.cloned.1.call-update) | async-done | bytes 13631504 | tf_op jit(solution)/shard_map/all_gather | solution.py:253
  155.1 1.7 copy.83
  156.8 3.2 fusion.30
  159.9 2.0 reshape.135
  162.0 1.5 multiply_reduce_fusion
  163.5 1.5 multiply_multiply_fusion
  169.3 1.9 pad_maximum_fusion
  171.2 29.2 %all-gather.7.cloned.1.call-done = bf16[32,832,512]{2,1,0:T(8,128)(2,1)} async-done(((bf16[32,416,512]{2,1,0:T(8,128)(2,1)}), bf16[32,832,512]{2,1,0:T(8,128)(2,1)}) %all-gather.7.cloned.1.call-update) | async-done | bytes 27262992 | tf_op jit(solution)/shard_map/all_gather | solution.py:254
  200.4 5.8 %fusion.32 = (bf16[64,32,512]{2,1,0:T(8,128)(2,1)}, bf16[64,32,512]{2,1,0:T(8,128)(2,1)}, bf16[64,32,512]{2,1,0:T(8,128)(2,1)}) fusion(bf16[64,416,512]{2,1,0:T(8,128)(2,1)} %bitcast.47), kind=kLoop, calls=%fused_computation.63 | loop fusion | bytes 12582912 | tf_op jit(solution)/shard_map/slice | solution.py:260
  206.1 3.7 %fusion.33 = (bf16[64,32,256]{2,1,0:T(8,128)(2,1)}, bf16[64,32,256]{2,1,0:T(8,128)(2,1)}, bf16[64,32,256]{2,1,0:T(8,128)(2,1)}) fusion(bf16[64,416,512]{2,1,0:T(8,128)(2,1)} %bitcast.48), kind=kLoop, calls=%fused_computation.64 | loop fusion | bytes 6291456 | tf_op jit(solution)/shard_map/slice | solution.py:260
  209.8 39.6 %shard_map.148 = bf16[256,512]{1,0:T(8,128)(2,1)} custom-call(s32[4]{0:T(128)} %pad_add_fusion.info, bf16[2,512,128]{2,1,0:T(8,128)(2,1)} %bitcast.61, s32[512,1]{1,0:T(8,128)} %bitcast.63, s32[512,1]{1,0:T(8,128)} %bitcast.62, bf16[64,416,512]{2,1,0:T(8,128)(2,1)} %bitcast.49), custom_call_target="tpu_custom_call" | custom-call | tf_op jit(solution)/shard_map/pallas_call | solution.py:188
  249.4 2.7 convolution_convert_fusion.x_ref
  252.1 33.1 %shard_map.149 = bf16[256,2048]{1,0:T(8,128)(2,1)} custom-call(bf16[256,2048]{1,0:T(8,128)(2,1)} %convolution_convert_fusion.x_ref), custom_call_target="tpu_custom_call" | custom-call | tf_op jit(solution)/shard_map/pallas_call | solution.py:87
  285.2 1.7 fusion.5
  288.7 1.5 fusion.35
  290.7 4.5 %fusion.11 = f32[256,2048]{1,0:T(8,128)} fusion(bf16[2048,256]{1,0:T(8,128)(2,1)} %bitcast.52, bf16[256,2048]{1,0:T(8,128)(2,1)} %copy-done.3, bf16[2048,256]{1,0:T(8,128)(2,1)} %bitcast.53, f32[256,256]{1,0:T(8,128)S(1)} %fusion.36), kind=kOutput, calls=%fused_computation.22 | convolution fusion | flops 537264128 | bytes 5505024 | tf_op jit(solution)/shard_map/dot_general | solution.py:297
  295.1 5.6 %fusion.x_ref = bf16[256,2048]{1,0:T(8,128)(2,1)} fusion(f32[256,2048]{1,0:T(8,128)} %fusion.11, bf16[2048,512]{1,0:T(8,128)(2,1)} %bitcast.54, bf16[256,2048]{1,0:T(8,128)(2,1)} %copy-done.3, bf16[2048,512]{1,0:T(8,128)(2,1)} %bitcast.55, f32[256,512]{1,0:T(8,128)} %fusion.35), kind=kOutput, calls=%fused_computation.7 | convolution fusion | flops 1075576832 | bytes 8912896 | tf_op jit(solution)/shard_map/dot_general | solution.py:297
  300.8 30.2 %shard_map.150 = bf16[256,2048]{1,0:T(8,128)(2,1)} custom-call(bf16[256,2048]{1,0:T(8,128)(2,1)} %fusion.x_ref), custom_call_target="tpu_custom_call" | custom-call | tf_op jit(solution)/shard_map/pallas_call | solution.py:87
  330.9 3.1 fusion.8
  (77 shorter events, 18.8 us)
Async XLA Ops:
  7.2 242.3 %copy-start = (bf16[512,2048]{1,0:T(8,128)(2,1)S(1)}, bf16[512,2048]{1,0:T(8,128)(2,1)}, u32[]{:S(2)}) copy-start(bf16[512,2048]{1,0:T(8,128)(2,1)} %param.19) | copy-start | bytes 6291460
  7.2 143.1 %all-gather.5.cloned.1.call-start = ((), (), s32[]{:S(2)}) async-start(), calls=%async_computation | async-start | bytes 14057472 | tf_op jit(solution)/shard_map/all_gather | solution.py:253
  10.1 4.0 %copy-start.1 = (bf16[256,2048]{1,0:T(8,128)(2,1)S(1)}, bf16[256,2048]{1,0:T(8,128)(2,1)}, u32[]{:S(2)}) copy-start(bf16[256,2048]{1,0:T(8,128)(2,1)} %param.14) | copy-start | bytes 3145732
  10.1 4.0 %copy-start.14 = (f32[2048]{0:T(1024)S(1)}, f32[2048]{0:T(1024)}, u32[]{:S(2)}) copy-start(f32[2048]{0:T(1024)} %param.15) | copy-start | bytes 24580
  10.1 4.0 %copy-start.13 = (bf16[2048,256]{1,0:T(8,128)(2,1)S(1)}, bf16[2048,256]{1,0:T(8,128)(2,1)}, u32[]{:S(2)}) copy-start(bf16[2048,256]{1,0:T(8,128)(2,1)} %param.18) | copy-start | bytes 3145732
  14.0 1.4 slice-start
  14.0 1.4 slice-start.2
  14.0 2.2 slice-start.1
  14.0 2.9 slice-start.3
  19.4 0.9 copy-start.6
  19.4 0.9 copy-start.8
  26.7 173.7 %all-gather.7.cloned.1.call-start = ((), (), s32[]{:S(2)}) async-start(), calls=%async_computation.1 | async-start | bytes 40894464 | tf_op jit(solution)/shard_map/all_gather | solution.py:254
  150.3 3.2 copy-start.9
  150.3 3.3 copy-start.7
  156.8 6.8 %copy-start.12 = (f32[128]{0:T(128)S(1)}, f32[128]{0:T(128)}, u32[]{:S(2)}) copy-start(f32[128]{0:T(128)} %param.20) | copy-start | bytes 1540
  159.9 5.1 %copy-start.10 = (f32[256,64]{1,0:T(8,128)S(1)}, f32[256,64]{1,0:T(8,128)}, u32[]{:S(2)}) copy-start(f32[256,64]{1,0:T(8,128)} %copy.72) | copy-start | bytes 196612
  252.1 34.8 %copy-start.11 = (f32[2048]{0:T(1024)S(1)}, f32[2048]{0:T(1024)}, u32[]{:S(2)}) copy-start(f32[2048]{0:T(1024)} %param.23) | copy-start | bytes 24580
  285.2 1.8 copy-start.2
  286.9 1.8 copy-start.5
  287.4 3.2 copy-start.3
  287.4 2.8 copy-start.4
Sparse Core Ops, SparseCore 0:
  26.8 123.3 all-gather.4
  152.1 48.2 all-gather.6

commit v6 on v4

--- a/solution.py
+++ b/solution.py
@@ -103,9 +103,9 @@
 def attention_kernel(info, q_ref, q_last_ref, q_first_ref, kv_ref, o_ref, top_ref, total_ref, acc_ref):
     step = pl.program_id(0)
     groups, rows_all, head_size = q_ref.shape
-    shards_per, rows, _ = kv_ref.shape
+    shards_per, both, _ = kv_ref.shape
+    rows = both // 2
     width = shards_per * rows
-    half = kv_ref.shape[2] // 2
     rows_q = o_ref.shape[0]
     per_group = rows_all // rows_q
     scale = 1.0 / math.sqrt(head_size)
@@ -123,8 +123,8 @@
     def run(masked):
         for g in range(groups):
             q = q_ref[g]
-            k = kv_ref[:, :, g * head_size : (g + 1) * head_size].reshape(width, head_size)
-            v = kv_ref[:, :, half + g * head_size : half + (g + 1) * head_size].reshape(width, head_size)
+            k = kv_ref[:, :rows, g * head_size : (g + 1) * head_size].reshape(width, head_size)
+            v = kv_ref[:, rows:, g * head_size : (g + 1) * head_size].reshape(width, head_size)
             s = lax.dot_general(q, k, (((1,), (1,)), ((), ())), preferred_element_type=jnp.float32) * scale
             if masked:
                 k_index = offset + lax.broadcasted_iota(jnp.int32, s.shape, 1)
@@ -235,9 +235,10 @@
     ff_rows, ff_local = w_gate.shape
     rest = ff_local - width_all
     down_t = w_down.T
-    packed = jnp.concatenate(
+    kv_packed = jnp.concatenate([key_cache, value_cache], axis=0)
+    kv_gathered = lax.all_gather(kv_packed, "seq", axis=0, tiled=False)
+    weights_packed = jnp.concatenate(
         [
-            jnp.concatenate([key_cache, value_cache], axis=1),
             w_gate[:, :width_all],
             w_up[:, :width_all],
             down_t[:, :width_all],
@@ -249,11 +250,12 @@
         ],
         axis=0,
     )
-    gathered = lax.all_gather(packed, "seq", axis=0, tiled=False)
+    kv_gathered, weights_packed = lax.optimization_barrier((kv_gathered, weights_packed))
+    w_gathered = lax.all_gather(weights_packed, "seq", axis=0, tiled=False)
 
     def weight_part(k, lo, hi):
-        top = rows + k * ff_rows
-        return gathered[:, top : top + ff_rows, lo:hi].reshape(shards * ff_rows, hi - lo)
+        top = k * ff_rows
+        return w_gathered[:, top : top + ff_rows, lo:hi].reshape(shards * ff_rows, hi - lo)
 
     gate_a = weight_part(0, 0, width_all)
     up_a = weight_part(1, 0, width_all)
@@ -280,7 +282,7 @@
     )
     q_last = jnp.tile(q_index, head_group).reshape(head_group * rows, 1)
     q_first = jnp.tile(q_start, head_group).reshape(head_group * rows, 1)
-    attended = attention(q_grouped, q_last, q_first, gathered, info, rows, rows, shards_per)
+    attended = attention(q_grouped, q_last, q_first, kv_gathered, info, rows, 2 * rows, shards_per)
     partial_out = jnp.dot(attended, w_out, preferred_element_type=jnp.float32)
     summed = tp_sum(partial_out.astype(jnp.bfloat16), 0).astype(jnp.float32)
     mid = (xf + summed).astype(jnp.bfloat16)

time: 295 us -> 274 us (0.929)
  the two profiles are of different devices: /device:TPU:228 before, /device:TPU:192 now
where the time goes in v6:
time: 274 us; the launch traced here: 273 us
  Pallas kernels  103 us (38%)
  waiting for transfers between devices  91.9 us (34%)
  local copies, waits for them, and re-layouts  22.1 us (8%)
  matrix products  22 us (8%)
  between operations  17 us (6%)
  other arithmetic  16.7 us (6%)
    all_gather x1, waiting for transfers between devices, body(): kv_gathered = lax.all_gather(kv_packed, 'seq', axis=0, tiled=False)  91.9 us
    pallas_call x2, Pallas kernels, tp_sum(): pl.pallas_call(functools.partial(tp_sum_kernel, n), out_shape=jax.ShapeDt...  63.3 us
    pallas_call x1, Pallas kernels, attention(): pl.pallas_call(attention_kernel, out_shape=jax.ShapeDtypeStruct((rows, ou...  40 us
    dot_general x2, matrix products, ffn_piece(): lax.dot_general(act, down_w, (((1,), (1,)), ((), ())), preferred_element_...  10.1 us
    slice x2, local copies, waits for them, and re-layouts, weight_part(): w_gathered[:, top:top + ff_rows, lo:hi].reshape(shards * ff_rows, hi - lo)  9.68 us
    unnamed x35, local copies, waits for them, and re-layouts  5.92 us
  transfers between devices with their start and end apart: 2, of which 1 were waited for; matrix products, arithmetic and copies ran while one was open for 10% of the time, Pallas kernels for 27%

profile of v6, /device:TPU:192, one launch (start us, length us, event | category | flops | bytes accessed | tf_op | source)
XLA Modules:
  0.0 273.0 jit_solution(1329727943639834437)
XLA Ops:
  7.3 1.6 fusion.1
  8.9 2.3 multiply_reduce_fusion.1
  12.4 1.8 convolution_convert_fusion.1
  16.5 1.4 slice_dynamic-update-slice_fusion.2
  17.9 1.4 slice_dynamic-update-slice_fusion.1
  19.2 1.4 slice_dynamic-update-slice_fusion
  21.8 91.9 %all-gather.5.cloned.1.call-done = bf16[32768,256]{1,0:T(8,128)(2,1)} async-done(((bf16[512,256]{1,0:T(8,128)(2,1)}), bf16[32768,256]{1,0:T(8,128)(2,1)}) %all-gather.5.cloned.1.call-update) | async-done | bytes 16777232 | tf_op jit(solution)/shard_map/all_gather | solution.py:239
  117.9 3.2 %fusion.30 = f32[256,512]{1,0:T(8,128)} fusion(bf16[2048,512]{1,0:T(8,128)(2,1)} %param.16, bf16[256,2048]{1,0:T(8,128)(2,1)S(1)} %copy-done.1, f32[2048]{0:T(1024)} %param.15, f32[256]{0:T(256)} %copy-done.9), kind=kOutput, calls=%fused_computation.66 | convolution fusion | flops 538968064 | bytes 3679232 | tf_op jit(solution)/shard_map/dot_general | solution.py:221
  121.1 2.0 reshape.132
  123.1 1.4 multiply_reduce_fusion
  124.5 1.4 multiply_multiply_fusion
  130.3 1.8 pad_maximum_fusion
  132.1 40.0 %shard_map.148 = bf16[256,512]{1,0:T(8,128)(2,1)} custom-call(s32[4]{0:T(128)} %pad_add_fusion.info, bf16[2,512,128]{2,1,0:T(8,128)(2,1)} %bitcast.56, s32[512,1]{1,0:T(8,128)} %bitcast.58, s32[512,1]{1,0:T(8,128)} %bitcast.57, bf16[64,512,256]{2,1,0:T(8,128)(2,1)} %bitcast.47), custom_call_target="tpu_custom_call" | custom-call | tf_op jit(solution)/shard_map/pallas_call | solution.py:187
  172.1 2.6 convolution_convert_fusion.x_ref
  174.7 33.1 %shard_map.149 = bf16[256,2048]{1,0:T(8,128)(2,1)} custom-call(bf16[256,2048]{1,0:T(8,128)(2,1)} %convolution_convert_fusion.x_ref), custom_call_target="tpu_custom_call" | custom-call | tf_op jit(solution)/shard_map/pallas_call | solution.py:86
  207.8 1.7 fusion.5
  209.6 1.5 fusion.7
  211.1 6.0 %fusion.32 = (bf16[64,32,512]{2,1,0:T(8,128)(2,1)S(1)}, bf16[64,32,512]{2,1,0:T(8,128)(2,1)}, bf16[64,32,512]{2,1,0:T(8,128)(2,1)}) fusion(bf16[64,160,512]{2,1,0:T(8,128)(2,1)} %bitcast.48), kind=kLoop, calls=%fused_computation.67 | loop fusion | bytes 12582912 | tf_op jit(solution)/shard_map/slice | solution.py:258
  217.1 3.7 %fusion.33 = (bf16[64,32,256]{2,1,0:T(8,128)(2,1)S(1)}, bf16[64,32,256]{2,1,0:T(8,128)(2,1)}, bf16[64,32,256]{2,1,0:T(8,128)(2,1)}) fusion(bf16[64,160,512]{2,1,0:T(8,128)(2,1)} %bitcast.49), kind=kLoop, calls=%fused_computation.68 | loop fusion | bytes 6291456 | tf_op jit(solution)/shard_map/slice | solution.py:258
  220.8 1.5 fusion.35
  222.8 4.5 %fusion.11 = f32[256,2048]{1,0:T(8,128)} fusion(bf16[2048,256]{1,0:T(8,128)(2,1)} %bitcast.51, bf16[256,2048]{1,0:T(8,128)(2,1)} %fusion.7, bf16[2048,256]{1,0:T(8,128)(2,1)} %bitcast.52, f32[256,256]{1,0:T(8,128)S(1)} %fusion.36), kind=kOutput, calls=%fused_computation.22 | convolution fusion | flops 537264128 | bytes 5505024 | tf_op jit(solution)/shard_map/dot_general | solution.py:295
  227.3 5.6 %fusion.x_ref = bf16[256,2048]{1,0:T(8,128)(2,1)} fusion(f32[256,2048]{1,0:T(8,128)} %fusion.11, bf16[2048,512]{1,0:T(8,128)(2,1)} %bitcast.53, bf16[256,2048]{1,0:T(8,128)(2,1)} %fusion.7, bf16[2048,512]{1,0:T(8,128)(2,1)} %bitcast.54, f32[256,512]{1,0:T(8,128)} %fusion.35), kind=kOutput, calls=%fused_computation.7 | convolution fusion | flops 1075576832 | bytes 8912896 | tf_op jit(solution)/shard_map/dot_general | solution.py:295
  232.9 30.2 %shard_map.150 = bf16[256,2048]{1,0:T(8,128)(2,1)} custom-call(bf16[256,2048]{1,0:T(8,128)(2,1)} %fusion.x_ref), custom_call_target="tpu_custom_call" | custom-call | tf_op jit(solution)/shard_map/pallas_call | solution.py:86
  263.1 3.1 %fusion.8 = bf16[256,2048]{1,0:T(8,128)(2,1)} fusion(bf16[256,2048]{1,0:T(8,128)(2,1)} %shard_map.150, bf16[256,2048]{1,0:T(8,128)(2,1)} %shard_map.149, bf16[256,2048]{1,0:T(8,128)(2,1)S(1)} %copy-done.1), kind=kLoop, calls=%fused_computation.16 | loop fusion | flops 4194304 | bytes 4194304 | tf_op jit(solution)/shard_map/convert_element_type | solution.py:301
  (63 shorter events, 11.0 us)
Async XLA Ops:
  7.2 164.9 %copy-start = (bf16[512,2048]{1,0:T(8,128)(2,1)S(1)}, bf16[512,2048]{1,0:T(8,128)(2,1)}, u32[]{:S(2)}) copy-start(bf16[512,2048]{1,0:T(8,128)(2,1)} %param.19) | copy-start | bytes 6291460
  7.2 4.1 %copy-start.10 = (s32[256]{0:T(256)S(1)}, s32[256]{0:T(256)}, u32[]{:S(2)}) copy-start(s32[256]{0:T(256)} %param.22) | copy-start | bytes 3076
  7.2 106.5 %all-gather.5.cloned.1.call-start = ((), (), s32[]{:S(2)}) async-start(), calls=%async_computation | async-start | bytes 17039360 | tf_op jit(solution)/shard_map/all_gather | solution.py:239
  7.3 4.9 %copy-start.11 = (f32[128]{0:T(128)S(1)}, f32[128]{0:T(128)}, u32[]{:S(2)}) copy-start(f32[128]{0:T(128)} %param.21) | copy-start | bytes 1540
  8.9 2.3 copy-start.9
  8.9 3.5 %copy-start.1 = (bf16[256,2048]{1,0:T(8,128)(2,1)S(1)}, bf16[256,2048]{1,0:T(8,128)(2,1)}, u32[]{:S(2)}) copy-start(bf16[256,2048]{1,0:T(8,128)(2,1)} %param.14) | copy-start | bytes 3145732
  12.4 6.8 %copy-start.4 = (bf16[256,256]{1,0:T(8,128)(2,1)}, bf16[256,256]{1,0:T(8,128)(2,1)S(1)}, u32[]{:S(2)}) copy-start(bf16[256,256]{1,0:T(8,128)(2,1)S(1)} %copy.45) | copy-start | bytes 393220
  12.4 8.2 %slice-start = ((bf16[32,768]{1,0:T(8,128)(2,1)}), bf16[32,256]{1,0:T(8,128)(2,1)S(1)}, s32[]{:S(2)}) async-start(bf16[32,768]{1,0:T(8,128)(2,1)} %param.24), calls=%async_computation.2 | async-start | bytes 32768 | tf_op jit(solution)/shard_map/slice | solution.py:245
  14.2 103.4 %copy-start.5 = (bf16[256,256]{1,0:T(8,128)(2,1)}, bf16[256,256]{1,0:T(8,128)(2,1)S(1)}, u32[]{:S(2)}) copy-start(bf16[256,256]{1,0:T(8,128)(2,1)S(1)} %convolution_convert_fusion.1) | copy-start | bytes 393220
  15.0 196.1 %all-gather.7.cloned.1.call-start = ((), (), s32[]{:S(2)}) async-start(), calls=%async_computation.1 | async-start | bytes 10649600 | tf_op jit(solution)/shard_map/all_gather | solution.py:254
  117.9 6.6 %copy-start.12 = (f32[128]{0:T(128)S(1)}, f32[128]{0:T(128)}, u32[]{:S(2)}) copy-start(f32[128]{0:T(128)} %param.20) | copy-start | bytes 1540
  124.5 2.7 copy-start.6
  124.5 3.6 %copy-start.8 = (s32[256]{0:T(256)S(1)}, s32[256]{0:T(256)}, u32[]{:S(2)}) copy-start(s32[256]{0:T(256)} %get-tuple-element.25) | copy-start | bytes 3076
  174.7 34.8 %copy-start.7 = (f32[2048]{0:T(1024)S(1)}, f32[2048]{0:T(1024)}, u32[]{:S(2)}) copy-start(f32[2048]{0:T(1024)} %param.23) | copy-start | bytes 24580
  207.8 1.8 copy-start.2
  217.1 3.7 %copy-start.3 = (bf16[256,2048]{1,0:T(8,128)(2,1)S(1)}, bf16[256,2048]{1,0:T(8,128)(2,1)}, u32[]{:S(2)}) copy-start(bf16[256,2048]{1,0:T(8,128)(2,1)} %fusion.7) | copy-start | bytes 3145732
Sparse Core Ops, SparseCore 0:
  15.1 98.5 all-gather.4
  116.4 82.8 all-gather.6

commit v7 on v6

--- a/solution.py
+++ b/solution.py
@@ -250,19 +250,11 @@
         ],
         axis=0,
     )
-    kv_gathered, weights_packed = lax.optimization_barrier((kv_gathered, weights_packed))
-    w_gathered = lax.all_gather(weights_packed, "seq", axis=0, tiled=False)
 
     def weight_part(k, lo, hi):
         top = k * ff_rows
         return w_gathered[:, top : top + ff_rows, lo:hi].reshape(shards * ff_rows, hi - lo)
 
-    gate_a = weight_part(0, 0, width_all)
-    up_a = weight_part(1, 0, width_all)
-    down_a = weight_part(2, 0, width_all)
-    gate_b = weight_part(3, 0, rest)
-    up_b = weight_part(3, rest, 2 * rest)
-    down_b = weight_part(4, 0, rest)
 
     me = lax.axis_index("seq")
     first = me * rows
@@ -282,6 +274,16 @@
     )
     q_last = jnp.tile(q_index, head_group).reshape(head_group * rows, 1)
     q_first = jnp.tile(q_start, head_group).reshape(head_group * rows, 1)
+    kv_gathered, weights_packed, q_grouped, q_last, q_first, info = lax.optimization_barrier(
+        (kv_gathered, weights_packed, q_grouped, q_last, q_first, info)
+    )
+    w_gathered = lax.all_gather(weights_packed, "seq", axis=0, tiled=False)
+    gate_a = weight_part(0, 0, width_all)
+    up_a = weight_part(1, 0, width_all)
+    down_a = weight_part(2, 0, width_all)
+    gate_b = weight_part(3, 0, rest)
+    up_b = weight_part(3, rest, 2 * rest)
+    down_b = weight_part(4, 0, rest)
     attended = attention(q_grouped, q_last, q_first, kv_gathered, info, rows, 2 * rows, shards_per)
     partial_out = jnp.dot(attended, w_out, preferred_element_type=jnp.float32)
     summed = tp_sum(partial_out.astype(jnp.bfloat16), 0).astype(jnp.float32)

time: 274 us -> 272 us (level)
  the two profiles are of different devices: /device:TPU:192 before, /device:TPU:1 now
where the time goes in v7:
time: 272 us
  waiting for transfers between devices  121 us (44%)
  Pallas kernels  70.2 us (26%)
  local copies, waits for them, and re-layouts  22.9 us (8%)
  matrix products  22.6 us (8%)
  other arithmetic  18 us (7%)
  between operations  16.9 us (6%)
    all_gather x1, waiting for transfers between devices, body(): kv_gathered = lax.all_gather(kv_packed, 'seq', axis=0, tiled=False)  82.5 us
    pallas_call x2, Pallas kernels, tp_sum(): pl.pallas_call(functools.partial(tp_sum_kernel, n), out_shape=jax.ShapeDt...  63 us
    all_gather x1, waiting for transfers between devices, body(): w_gathered = lax.all_gather(weights_packed, 'seq', axis=0, tiled=False)  38.2 us
    dot_general x2, matrix products, ffn_piece(): lax.dot_general(act, down_w, (((1,), (1,)), ((), ())), preferred_element_...  10.1 us
    slice x2, local copies, waits for them, and re-layouts, weight_part(): w_gathered[:, top:top + ff_rows, lo:hi].reshape(shards * ff_rows, hi - lo)  9.68 us
    pallas_call x1, Pallas kernels, attention(): pl.pallas_call(attention_kernel, out_shape=jax.ShapeDtypeStruct((rows, ou...  7.26 us
  transfers between devices with their start and end apart: 2, of which 2 were waited for; matrix products, arithmetic and copies ran while one was open for 10% of the time, Pallas kernels for 14%

profile of v7, /device:TPU:1, one launch (start us, length us, event | category | flops | bytes accessed | tf_op | source)
XLA Modules:
  0.0 271.6 jit_solution(2542199222768874280)
XLA Ops:
  7.3 1.6 fusion.1
  8.9 3.0 %multiply_reduce_fusion.1 = (f32[256,2]{0,1:T(2,128)S(1)}, f32[256,256]{0,1:T(8,128)}) fusion(bf16[2048,256]{1,0:T(8,128)(2,1)} %param.17, bf16[256,2048]{1,0:T(8,128)(2,1)} %param.14, f32[2048]{0:T(1024)} %param.15, f32[256]{0:T(256)S(1)} %add_rsqrt_fusion.3), kind=kOutput, calls=%fused_computation.41 | convolution fusion | flops 270663168 | bytes 2370560 | tf_op jit(solution)/shard_map/dot_general | solution.py:225
  15.1 1.8 convolution_convert_fusion.1
  21.6 3.2 %fusion.27 = f32[256,512]{1,0:T(8,128)} fusion(bf16[2048,512]{1,0:T(8,128)(2,1)} %param.16, bf16[256,2048]{1,0:T(8,128)(2,1)S(1)} %copy-done.1, f32[2048]{0:T(1024)} %param.15, f32[256]{0:T(256)S(1)} %add_rsqrt_fusion.3), kind=kOutput, calls=%fused_computation.65 | convolution fusion | flops 538968064 | bytes 3679232 | tf_op jit(solution)/shard_map/dot_general | solution.py:221
  24.8 2.0 reshape.133
  26.8 1.4 multiply_reduce_fusion
  28.3 1.4 multiply_multiply_fusion
  38.0 1.8 pad_maximum_fusion.1
  39.8 82.5 %all-gather.5.cloned.1.call-done = bf16[32768,256]{1,0:T(8,128)(2,1)} async-done(((bf16[512,256]{1,0:T(8,128)(2,1)}), bf16[32768,256]{1,0:T(8,128)(2,1)}) %all-gather.5.cloned.1.call-update) | async-done | bytes 16777232 | tf_op jit(solution)/shard_map/all_gather | solution.py:239
  122.4 1.5 copy.43.q_last_ref
  123.9 1.5 copy.44.q_first_ref
  125.5 7.3 %shard_map.148 = bf16[256,512]{1,0:T(8,128)(2,1)} custom-call(s32[4]{0:T(128)} %pad_add_fusion.info, bf16[2,512,128]{2,1,0:T(8,128)(2,1)} %bitcast.56, s32[512,1]{1,0:T(8,128)} %copy.43.q_last_ref, s32[512,1]{1,0:T(8,128)} %copy.44.q_first_ref, bf16[64,512,256]{2,1,0:T(8,128)(2,1)} %bitcast.47), custom_call_target="tpu_custom_call" | custom-call | tf_op jit(solution)/shard_map/pallas_call | solution.py:187
  132.7 2.6 convolution_convert_fusion.x_ref
  135.4 31.6 %shard_map.149 = bf16[256,2048]{1,0:T(8,128)(2,1)} custom-call(bf16[256,2048]{1,0:T(8,128)(2,1)} %convolution_convert_fusion.x_ref), custom_call_target="tpu_custom_call" | custom-call | tf_op jit(solution)/shard_map/pallas_call | solution.py:86
  167.0 1.7 fusion.5
  168.7 1.6 fusion.7
  170.3 38.2 %all-gather.7.cloned.1.call-done = bf16[10240,512]{1,0:T(8,128)(2,1)} async-done(((bf16[160,512]{1,0:T(8,128)(2,1)}), bf16[10240,512]{1,0:T(8,128)(2,1)}) %all-gather.7.cloned.1.call-update) | async-done | bytes 10485776 | tf_op jit(solution)/shard_map/all_gather | solution.py:280
  208.5 5.9 %fusion.32 = (bf16[64,32,512]{2,1,0:T(8,128)(2,1)S(1)}, bf16[64,32,512]{2,1,0:T(8,128)(2,1)}, bf16[64,32,512]{2,1,0:T(8,128)(2,1)}) fusion(bf16[64,160,512]{2,1,0:T(8,128)(2,1)} %bitcast.48), kind=kLoop, calls=%fused_computation.67 | loop fusion | bytes 12582912 | tf_op jit(solution)/shard_map/slice | solution.py:256
  214.5 3.7 %fusion.33 = (bf16[64,32,256]{2,1,0:T(8,128)(2,1)S(1)}, bf16[64,32,256]{2,1,0:T(8,128)(2,1)}, bf16[64,32,256]{2,1,0:T(8,128)(2,1)}) fusion(bf16[64,160,512]{2,1,0:T(8,128)(2,1)} %bitcast.49), kind=kLoop, calls=%fused_computation.68 | loop fusion | bytes 6291456 | tf_op jit(solution)/shard_map/slice | solution.py:256
  218.2 1.5 fusion.35
  220.2 4.5 %fusion.11 = f32[256,2048]{1,0:T(8,128)} fusion(bf16[2048,256]{1,0:T(8,128)(2,1)} %bitcast.51, bf16[256,2048]{1,0:T(8,128)(2,1)} %fusion.7, bf16[2048,256]{1,0:T(8,128)(2,1)} %bitcast.52, f32[256,256]{1,0:T(8,128)S(1)} %fusion.36), kind=kOutput, calls=%fused_computation.22 | convolution fusion | flops 537264128 | bytes 5505024 | tf_op jit(solution)/shard_map/dot_general | solution.py:297
  224.7 5.6 %fusion.x_ref = bf16[256,2048]{1,0:T(8,128)(2,1)} fusion(f32[256,2048]{1,0:T(8,128)} %fusion.11, bf16[2048,512]{1,0:T(8,128)(2,1)} %bitcast.53, bf16[256,2048]{1,0:T(8,128)(2,1)} %fusion.7, bf16[2048,512]{1,0:T(8,128)(2,1)} %bitcast.54, f32[256,512]{1,0:T(8,128)} %fusion.35), kind=kOutput, calls=%fused_computation.7 | convolution fusion | flops 1075576832 | bytes 8912896 | tf_op jit(solution)/shard_map/dot_general | solution.py:297
  230.3 31.4 %shard_map.150 = bf16[256,2048]{1,0:T(8,128)(2,1)} custom-call(bf16[256,2048]{1,0:T(8,128)(2,1)} %fusion.x_ref), custom_call_target="tpu_custom_call" | custom-call | tf_op jit(solution)/shard_map/pallas_call | solution.py:86
  261.7 3.1 %fusion.8 = bf16[256,2048]{1,0:T(8,128)(2,1)} fusion(bf16[256,2048]{1,0:T(8,128)(2,1)} %shard_map.150, bf16[256,2048]{1,0:T(8,128)(2,1)} %shard_map.149, bf16[256,2048]{1,0:T(8,128)(2,1)S(1)} %copy-done.1), kind=kLoop, calls=%fused_computation.16 | loop fusion | flops 4194304 | bytes 4194304 | tf_op jit(solution)/shard_map/convert_element_type | solution.py:303
  (68 shorter events, 14.1 us)
Async XLA Ops:
  7.2 125.6 %copy-start = (bf16[512,2048]{1,0:T(8,128)(2,1)S(1)}, bf16[512,2048]{1,0:T(8,128)(2,1)}, u32[]{:S(2)}) copy-start(bf16[512,2048]{1,0:T(8,128)(2,1)} %param.19) | copy-start | bytes 6291460
  7.2 4.8 %copy-start.12 = (s32[256]{0:T(256)S(1)}, s32[256]{0:T(256)}, u32[]{:S(2)}) copy-start(s32[256]{0:T(256)} %param.22) | copy-start | bytes 3076
  7.2 115.2 %all-gather.5.cloned.1.call-start = ((), (), s32[]{:S(2)}) async-start(), calls=%async_computation | async-start | bytes 17039360 | tf_op jit(solution)/shard_map/all_gather | solution.py:239
  8.9 4.3 %copy-start.13 = (f32[128]{0:T(128)S(1)}, f32[128]{0:T(128)}, u32[]{:S(2)}) copy-start(f32[128]{0:T(128)} %param.21) | copy-start | bytes 1540
  8.9 6.2 %copy-start.1 = (bf16[256,2048]{1,0:T(8,128)(2,1)S(1)}, bf16[256,2048]{1,0:T(8,128)(2,1)}, u32[]{:S(2)}) copy-start(bf16[256,2048]{1,0:T(8,128)(2,1)} %param.14) | copy-start | bytes 3145732
  12.5 5.8 %copy-start.8 = (s32[256]{0:T(256)}, s32[256]{0:T(256)S(1)}, u32[]{:S(2)}) copy-start(s32[256]{0:T(256)S(1)} %get-tuple-element.29) | copy-start | bytes 3076
  15.1 2.4 copy-start.4
  16.9 0.7 copy-start.5
  18.3 190.2 %all-gather.7.cloned.1.call-start = ((), (), s32[]{:S(2)}) async-start(), calls=%async_computation.1 | async-start | bytes 10649600 | tf_op jit(solution)/shard_map/all_gather | solution.py:280
  21.6 6.6 %copy-start.14 = (f32[128]{0:T(128)S(1)}, f32[128]{0:T(128)}, u32[]{:S(2)}) copy-start(f32[128]{0:T(128)} %param.20) | copy-start | bytes 1540
  28.3 2.8 %copy-start.9 = (s32[256]{0:T(256)S(1)}, s32[256]{0:T(256)}, u32[]{:S(2)}) copy-start(s32[256]{0:T(256)} %copy-done.8) | copy-start | bytes 3076
  28.3 3.4 %copy-start.11 = (s32[256]{0:T(256)S(1)}, s32[256]{0:T(256)}, u32[]{:S(2)}) copy-start(s32[256]{0:T(256)} %get-tuple-element.33) | copy-start | bytes 3076
  28.3 6.0 %copy-start.6 = (bf16[32,768]{1,0:T(8,128)(2,1)S(1)}, bf16[32,768]{1,0:T(8,128)(2,1)}, u32[]{:S(2)}) copy-start(bf16[32,768]{1,0:T(8,128)(2,1)} %param.24) | copy-start | bytes 147460
  28.3 6.6 %copy-start.7 = (bf16[32,768]{1,0:T(8,128)(2,1)S(1)}, bf16[32,768]{1,0:T(8,128)(2,1)}, u32[]{:S(2)}) copy-start(bf16[32,768]{1,0:T(8,128)(2,1)} %param.25) | copy-start | bytes 147460
  28.3 8.5 %slice-start = ((bf16[32,768]{1,0:T(8,128)(2,1)}), bf16[32,256]{1,0:T(8,128)(2,1)S(1)}, s32[]{:S(2)}) async-start(bf16[32,768]{1,0:T(8,128)(2,1)} %param.24), calls=%async_computation.2 | async-start | bytes 32768 | tf_op jit(solution)/shard_map/slice | solution.py:245
  28.3 8.5 %slice-start.1 = ((bf16[32,768]{1,0:T(8,128)(2,1)}), bf16[32,256]{1,0:T(8,128)(2,1)S(1)}, s32[]{:S(2)}) async-start(bf16[32,768]{1,0:T(8,128)(2,1)} %param.25), calls=%async_computation.3 | async-start | bytes 32768 | tf_op jit(solution)/shard_map/slice | solution.py:245
  135.4 33.4 %copy-start.10 = (f32[2048]{0:T(1024)S(1)}, f32[2048]{0:T(1024)}, u32[]{:S(2)}) copy-start(f32[2048]{0:T(1024)} %param.23) | copy-start | bytes 24580
  167.0 1.8 copy-start.2
  214.5 3.7 %copy-start.3 = (bf16[256,2048]{1,0:T(8,128)(2,1)S(1)}, bf16[256,2048]{1,0:T(8,128)(2,1)}, u32[]{:S(2)}) copy-start(bf16[256,2048]{1,0:T(8,128)(2,1)} %fusion.7) | copy-start | bytes 3145732
Sparse Core Ops, SparseCore 0:
  18.4 103.9 all-gather.4
  125.1 83.3 all-gather.6

commit v8 on v7

--- a/solution.py
+++ b/solution.py
@@ -79,10 +79,85 @@
         copy.wait()
 
 
+def tp_sum4_kernel(x_ref, out_ref, slots, relay, reduced, send_sem, recv_sem):
+    n = 4
+    me = lax.axis_index("tp")
+    row = lax.axis_index("seq")
+    cols = x_ref.shape[1] // n
+    half = cols // 2
+    right, left, far = lax.rem(me + 1, n), lax.rem(me + n - 1, n), lax.rem(me + 2, n)
+
+    barrier = pltpu.get_barrier_semaphore()
+    for k in range(1, n):
+        pl.semaphore_signal(barrier, inc=1, device_id=(row, lax.rem(me + k, n)), device_id_type=MESH)
+    pl.semaphore_wait(barrier, n - 1)
+
+    def block(ref, owner):
+        return ref.at[:, pl.ds(pl.multiple_of(owner * cols, cols), cols)]
+
+    def part(ref, lo):
+        return ref.at[:, lo : lo + half]
+
+    def copy(src, dst, index, device):
+        c = pltpu.make_async_remote_copy(
+            src_ref=src,
+            dst_ref=dst,
+            send_sem=send_sem.at[index],
+            recv_sem=recv_sem.at[index],
+            device_id=(row, device),
+            device_id_type=MESH,
+        )
+        c.start()
+        return c
+
+    def exchange(phase, src_of, dst_of, relay_base):
+        s = phase * 6
+        base = relay_base
+        direct = [
+            copy(src_of(right), dst_of(me, 1), s + 0, right),
+            copy(src_of(left), dst_of(me, 3), s + 1, left),
+        ]
+        first = [
+            copy(part(src_of(far), 0), relay.at[base + 0], s + 2, right),
+            copy(part(src_of(far), half), relay.at[base + 1], s + 3, left),
+        ]
+        for c in first:
+            c.wait()
+        second = [
+            copy(relay.at[base + 0], part(dst_of(left, 2), 0), s + 4, right),
+            copy(relay.at[base + 1], part(dst_of(right, 2), half), s + 5, left),
+        ]
+        for c in direct + second:
+            c.wait()
+
+    exchange(0, lambda peer: block(x_ref, peer), lambda origin, k: slots.at[k], 0)
+    total = block(x_ref, me)[...].astype(jnp.float32)
+    for k in range(1, n):
+        total = total + slots[k].astype(jnp.float32)
+    reduced[...] = total.astype(reduced.dtype)
+    block(out_ref, me)[...] = reduced[...]
+    exchange(1, lambda peer: reduced, lambda origin, k: block(out_ref, origin), 2)
+
+
 def tp_sum(x, collective_id):
     n = lax.axis_size("tp")
     rows, width = x.shape
     cols = width // n
+    if n == 4 and cols % 256 == 0:
+        return pl.pallas_call(
+            tp_sum4_kernel,
+            out_shape=jax.ShapeDtypeStruct((rows, width), x.dtype),
+            in_specs=[pl.BlockSpec(memory_space=pltpu.VMEM)],
+            out_specs=pl.BlockSpec(memory_space=pltpu.VMEM),
+            scratch_shapes=[
+                pltpu.VMEM((n, rows, cols), x.dtype),
+                pltpu.VMEM((4, rows, cols // 2), x.dtype),
+                pltpu.VMEM((rows, cols), x.dtype),
+                pltpu.SemaphoreType.DMA((12,)),
+                pltpu.SemaphoreType.DMA((12,)),
+            ],
+            compiler_params=pltpu.CompilerParams(collective_id=collective_id, has_side_effects=True),
+        )(x)
     return pl.pallas_call(
         functools.partial(tp_sum_kernel, n),
         out_shape=jax.ShapeDtypeStruct((rows, width), x.dtype),

time: 272 us -> 275 us (1.011)
  transfers between devices with their start and end apart: 2 -> 2, of which waited for: 2 -> 2; matrix products, arithmetic and copies ran while one was open for 10% -> 10% of each run, Pallas kernels for 14% -> 15%
where the time goes in v8:
time: 275 us; the launch traced here: 273 us
  waiting for transfers between devices  120 us (44%)
  Pallas kernels  72.6 us (26%)
  local copies, waits for them, and re-layouts  22.9 us (8%)
  matrix products  22.6 us (8%)
  other arithmetic  18 us (7%)
  between operations  16.9 us (6%)
    all_gather x1, waiting for transfers between devices, body(): kv_gathered = lax.all_gather(kv_packed, 'seq', axis=0, tiled=False)  82.5 us
    pallas_call x2, Pallas kernels, tp_sum(): pl.pallas_call(tp_sum4_kernel, out_shape=jax.ShapeDtypeStruct((rows, widt...  65.3 us
    all_gather x1, waiting for transfers between devices, body(): w_gathered = lax.all_gather(weights_packed, 'seq', axis=0, tiled=False)  37.2 us
    dot_general x2, matrix products, ffn_piece(): lax.dot_general(act, down_w, (((1,), (1,)), ((), ())), preferred_element_...  10.1 us
    slice x2, local copies, waits for them, and re-layouts, weight_part(): w_gathered[:, top:top + ff_rows, lo:hi].reshape(shards * ff_rows, hi - lo)  9.68 us
    pallas_call x1, Pallas kernels, attention(): pl.pallas_call(attention_kernel, out_shape=jax.ShapeDtypeStruct((rows, ou...  7.26 us
  transfers between devices with their start and end apart: 2, of which 2 were waited for; matrix products, arithmetic and copies ran while one was open for 10% of the time, Pallas kernels for 15%

profile of v8, /device:TPU:1, one launch (start us, length us, event | category | flops | bytes accessed | tf_op | source)
XLA Modules:
  0.0 272.9 jit_solution(8136834317440060979)
XLA Ops:
  7.3 1.6 fusion.1
  8.9 3.0 %multiply_reduce_fusion.1 = (f32[256,2]{0,1:T(2,128)S(1)}, f32[256,256]{0,1:T(8,128)}) fusion(bf16[2048,256]{1,0:T(8,128)(2,1)} %param.17, bf16[256,2048]{1,0:T(8,128)(2,1)} %param.14, f32[2048]{0:T(1024)} %param.15, f32[256]{0:T(256)S(1)} %add_rsqrt_fusion.3), kind=kOutput, calls=%fused_computation.41 | convolution fusion | flops 270663168 | bytes 2370560 | tf_op jit(solution)/shard_map/dot_general | solution.py:300
  15.1 1.8 convolution_convert_fusion.1
  21.6 3.2 %fusion.27 = f32[256,512]{1,0:T(8,128)} fusion(bf16[2048,512]{1,0:T(8,128)(2,1)} %param.16, bf16[256,2048]{1,0:T(8,128)(2,1)S(1)} %copy-done.1, f32[2048]{0:T(1024)} %param.15, f32[256]{0:T(256)S(1)} %add_rsqrt_fusion.3), kind=kOutput, calls=%fused_computation.65 | convolution fusion | flops 538968064 | bytes 3679232 | tf_op jit(solution)/shard_map/dot_general | solution.py:296
  24.8 2.0 reshape.133
  26.8 1.4 multiply_reduce_fusion
  28.3 1.4 multiply_multiply_fusion
  38.0 1.8 pad_maximum_fusion.1
  39.8 82.5 %all-gather.5.cloned.1.call-done = bf16[32768,256]{1,0:T(8,128)(2,1)} async-done(((bf16[512,256]{1,0:T(8,128)(2,1)}), bf16[32768,256]{1,0:T(8,128)(2,1)}) %all-gather.5.cloned.1.call-update) | async-done | bytes 16777232 | tf_op jit(solution)/shard_map/all_gather | solution.py:314
  122.4 1.5 copy.43.q_last_ref
  123.9 1.5 copy.44.q_first_ref
  125.5 7.3 %shard_map.148 = bf16[256,512]{1,0:T(8,128)(2,1)} custom-call(s32[4]{0:T(128)} %pad_add_fusion.info, bf16[2,512,128]{2,1,0:T(8,128)(2,1)} %bitcast.56, s32[512,1]{1,0:T(8,128)} %copy.43.q_last_ref, s32[512,1]{1,0:T(8,128)} %copy.44.q_first_ref, bf16[64,512,256]{2,1,0:T(8,128)(2,1)} %bitcast.47), custom_call_target="tpu_custom_call" | custom-call | tf_op jit(solution)/shard_map/pallas_call | solution.py:262
  132.7 2.6 convolution_convert_fusion.x_ref
  135.4 32.6 %shard_map.149 = bf16[256,2048]{1,0:T(8,128)(2,1)} custom-call(bf16[256,2048]{1,0:T(8,128)(2,1)} %convolution_convert_fusion.x_ref), custom_call_target="tpu_custom_call" | custom-call | tf_op jit(solution)/shard_map/pallas_call | solution.py:147
  168.0 1.7 fusion.5
  169.8 1.6 fusion.7
  171.4 37.2 %all-gather.7.cloned.1.call-done = bf16[10240,512]{1,0:T(8,128)(2,1)} async-done(((bf16[160,512]{1,0:T(8,128)(2,1)}), bf16[10240,512]{1,0:T(8,128)(2,1)}) %all-gather.7.cloned.1.call-update) | async-done | bytes 10485776 | tf_op jit(solution)/shard_map/all_gather | solution.py:355
  208.5 5.9 %fusion.32 = (bf16[64,32,512]{2,1,0:T(8,128)(2,1)S(1)}, bf16[64,32,512]{2,1,0:T(8,128)(2,1)}, bf16[64,32,512]{2,1,0:T(8,128)(2,1)}) fusion(bf16[64,160,512]{2,1,0:T(8,128)(2,1)} %bitcast.48), kind=kLoop, calls=%fused_computation.67 | loop fusion | bytes 12582912 | tf_op jit(solution)/shard_map/slice | solution.py:331
  214.5 3.7 %fusion.33 = (bf16[64,32,256]{2,1,0:T(8,128)(2,1)S(1)}, bf16[64,32,256]{2,1,0:T(8,128)(2,1)}, bf16[64,32,256]{2,1,0:T(8,128)(2,1)}) fusion(bf16[64,160,512]{2,1,0:T(8,128)(2,1)} %bitcast.49), kind=kLoop, calls=%fused_computation.68 | loop fusion | bytes 6291456 | tf_op jit(solution)/shard_map/slice | solution.py:331
  218.2 1.5 fusion.35
  220.2 4.5 %fusion.11 = f32[256,2048]{1,0:T(8,128)} fusion(bf16[2048,256]{1,0:T(8,128)(2,1)} %bitcast.51, bf16[256,2048]{1,0:T(8,128)(2,1)} %fusion.7, bf16[2048,256]{1,0:T(8,128)(2,1)} %bitcast.52, f32[256,256]{1,0:T(8,128)S(1)} %fusion.36), kind=kOutput, calls=%fused_computation.22 | convolution fusion | flops 537264128 | bytes 5505024 | tf_op jit(solution)/shard_map/dot_general | solution.py:372
  224.7 5.6 %fusion.x_ref = bf16[256,2048]{1,0:T(8,128)(2,1)} fusion(f32[256,2048]{1,0:T(8,128)} %fusion.11, bf16[2048,512]{1,0:T(8,128)(2,1)} %bitcast.53, bf16[256,2048]{1,0:T(8,128)(2,1)} %fusion.7, bf16[2048,512]{1,0:T(8,128)(2,1)} %bitcast.54, f32[256,512]{1,0:T(8,128)} %fusion.35), kind=kOutput, calls=%fused_computation.7 | convolution fusion | flops 1075576832 | bytes 8912896 | tf_op jit(solution)/shard_map/dot_general | solution.py:372
  230.3 32.7 %shard_map.150 = bf16[256,2048]{1,0:T(8,128)(2,1)} custom-call(bf16[256,2048]{1,0:T(8,128)(2,1)} %fusion.x_ref), custom_call_target="tpu_custom_call" | custom-call | tf_op jit(solution)/shard_map/pallas_call | solution.py:147
  263.0 3.1 %fusion.8 = bf16[256,2048]{1,0:T(8,128)(2,1)} fusion(bf16[256,2048]{1,0:T(8,128)(2,1)} %shard_map.150, bf16[256,2048]{1,0:T(8,128)(2,1)} %shard_map.149, bf16[256,2048]{1,0:T(8,128)(2,1)S(1)} %copy-done.1), kind=kLoop, calls=%fused_computation.16 | loop fusion | flops 4194304 | bytes 4194304 | tf_op jit(solution)/shard_map/convert_element_type | solution.py:378
  (68 shorter events, 14.1 us)
Async XLA Ops:
  7.2 125.6 %copy-start = (bf16[512,2048]{1,0:T(8,128)(2,1)S(1)}, bf16[512,2048]{1,0:T(8,128)(2,1)}, u32[]{:S(2)}) copy-start(bf16[512,2048]{1,0:T(8,128)(2,1)} %param.19) | copy-start | bytes 6291460
  7.2 4.8 %copy-start.12 = (s32[256]{0:T(256)S(1)}, s32[256]{0:T(256)}, u32[]{:S(2)}) copy-start(s32[256]{0:T(256)} %param.22) | copy-start | bytes 3076
  7.2 115.2 %all-gather.5.cloned.1.call-start = ((), (), s32[]{:S(2)}) async-start(), calls=%async_computation | async-start | bytes 17039360 | tf_op jit(solution)/shard_map/all_gather | solution.py:314
  8.9 4.3 %copy-start.13 = (f32[128]{0:T(128)S(1)}, f32[128]{0:T(128)}, u32[]{:S(2)}) copy-start(f32[128]{0:T(128)} %param.21) | copy-start | bytes 1540
  8.9 6.2 %copy-start.1 = (bf16[256,2048]{1,0:T(8,128)(2,1)S(1)}, bf16[256,2048]{1,0:T(8,128)(2,1)}, u32[]{:S(2)}) copy-start(bf16[256,2048]{1,0:T(8,128)(2,1)} %param.14) | copy-start | bytes 3145732
  12.5 5.8 %copy-start.8 = (s32[256]{0:T(256)}, s32[256]{0:T(256)S(1)}, u32[]{:S(2)}) copy-start(s32[256]{0:T(256)S(1)} %get-tuple-element.29) | copy-start | bytes 3076
  15.1 2.4 copy-start.4
  16.9 0.7 copy-start.5
  18.3 190.2 %all-gather.7.cloned.1.call-start = ((), (), s32[]{:S(2)}) async-start(), calls=%async_computation.1 | async-start | bytes 10649600 | tf_op jit(solution)/shard_map/all_gather | solution.py:355
  21.6 6.6 %copy-start.14 = (f32[128]{0:T(128)S(1)}, f32[128]{0:T(128)}, u32[]{:S(2)}) copy-start(f32[128]{0:T(128)} %param.20) | copy-start | bytes 1540
  28.3 2.8 %copy-start.9 = (s32[256]{0:T(256)S(1)}, s32[256]{0:T(256)}, u32[]{:S(2)}) copy-start(s32[256]{0:T(256)} %copy-done.8) | copy-start | bytes 3076
  28.3 3.4 %copy-start.11 = (s32[256]{0:T(256)S(1)}, s32[256]{0:T(256)}, u32[]{:S(2)}) copy-start(s32[256]{0:T(256)} %get-tuple-element.33) | copy-start | bytes 3076
  28.3 6.0 %copy-start.6 = (bf16[32,768]{1,0:T(8,128)(2,1)S(1)}, bf16[32,768]{1,0:T(8,128)(2,1)}, u32[]{:S(2)}) copy-start(bf16[32,768]{1,0:T(8,128)(2,1)} %param.24) | copy-start | bytes 147460
  28.3 6.6 %copy-start.7 = (bf16[32,768]{1,0:T(8,128)(2,1)S(1)}, bf16[32,768]{1,0:T(8,128)(2,1)}, u32[]{:S(2)}) copy-start(bf16[32,768]{1,0:T(8,128)(2,1)} %param.25) | copy-start | bytes 147460
  28.3 8.5 %slice-start = ((bf16[32,768]{1,0:T(8,128)(2,1)}), bf16[32,256]{1,0:T(8,128)(2,1)S(1)}, s32[]{:S(2)}) async-start(bf16[32,768]{1,0:T(8,128)(2,1)} %param.24), calls=%async_computation.2 | async-start | bytes 32768 | tf_op jit(solution)/shard_map/slice | solution.py:320
  28.3 8.5 %slice-start.1 = ((bf16[32,768]{1,0:T(8,128)(2,1)}), bf16[32,256]{1,0:T(8,128)(2,1)S(1)}, s32[]{:S(2)}) async-start(bf16[32,768]{1,0:T(8,128)(2,1)} %param.25), calls=%async_computation.3 | async-start | bytes 32768 | tf_op jit(solution)/shard_map/slice | solution.py:320
  135.4 34.4 %copy-start.10 = (f32[2048]{0:T(1024)S(1)}, f32[2048]{0:T(1024)}, u32[]{:S(2)}) copy-start(f32[2048]{0:T(1024)} %param.23) | copy-start | bytes 24580
  168.0 1.8 copy-start.2
  214.5 3.7 %copy-start.3 = (bf16[256,2048]{1,0:T(8,128)(2,1)S(1)}, bf16[256,2048]{1,0:T(8,128)(2,1)}, u32[]{:S(2)}) copy-start(bf16[256,2048]{1,0:T(8,128)(2,1)} %fusion.7) | copy-start | bytes 3145732
Sparse Core Ops, SparseCore 0:
  18.4 103.9 all-gather.4
  125.1 83.3 all-gather.6

commit v9 on v7

--- a/solution.py
+++ b/solution.py
@@ -237,24 +237,10 @@
     down_t = w_down.T
     kv_packed = jnp.concatenate([key_cache, value_cache], axis=0)
     kv_gathered = lax.all_gather(kv_packed, "seq", axis=0, tiled=False)
+    pad = -(3 * ff_local) % width_all
     weights_packed = jnp.concatenate(
-        [
-            w_gate[:, :width_all],
-            w_up[:, :width_all],
-            down_t[:, :width_all],
-            jnp.concatenate([w_gate[:, width_all:], w_up[:, width_all:]], axis=1),
-            jnp.concatenate(
-                [down_t[:, width_all:], jnp.zeros((ff_rows, 2 * width_all - ff_local), down_t.dtype)],
-                axis=1,
-            ),
-        ],
-        axis=0,
-    )
-
-    def weight_part(k, lo, hi):
-        top = k * ff_rows
-        return w_gathered[:, top : top + ff_rows, lo:hi].reshape(shards * ff_rows, hi - lo)
-
+        [w_gate, w_up, down_t, jnp.zeros((ff_rows, pad), down_t.dtype)], axis=1
+    )
 
     me = lax.axis_index("seq")
     first = me * rows
@@ -277,28 +263,23 @@
     kv_gathered, weights_packed, q_grouped, q_last, q_first, info = lax.optimization_barrier(
         (kv_gathered, weights_packed, q_grouped, q_last, q_first, info)
     )
-    w_gathered = lax.all_gather(weights_packed, "seq", axis=0, tiled=False)
-    gate_a = weight_part(0, 0, width_all)
-    up_a = weight_part(1, 0, width_all)
-    down_a = weight_part(2, 0, width_all)
-    gate_b = weight_part(3, 0, rest)
-    up_b = weight_part(3, rest, 2 * rest)
-    down_b = weight_part(4, 0, rest)
+    w_gathered = lax.all_gather(weights_packed, "seq", axis=0, tiled=False).reshape(
+        shards * ff_rows, weights_packed.shape[1]
+    )
     attended = attention(q_grouped, q_last, q_first, kv_gathered, info, rows, 2 * rows, shards_per)
     partial_out = jnp.dot(attended, w_out, preferred_element_type=jnp.float32)
     summed = tp_sum(partial_out.astype(jnp.bfloat16), 0).astype(jnp.float32)
     mid = (xf + summed).astype(jnp.bfloat16)
     mid_f = mid.astype(jnp.float32)
     post_normed = rms(mid_f, post_gain).astype(jnp.bfloat16)
-    def ffn_piece(gate_w, up_w, down_w):
-        gate = jnp.dot(post_normed, gate_w, preferred_element_type=jnp.float32)
-        up = jnp.dot(post_normed, up_w, preferred_element_type=jnp.float32)
-        act = (jax.nn.silu(gate) * up).astype(jnp.bfloat16)
-        return lax.dot_general(
-            act, down_w, (((1,), (1,)), ((), ())), preferred_element_type=jnp.float32
-        )
-
-    terms = ffn_piece(gate_a, up_a, down_a) + ffn_piece(gate_b, up_b, down_b)
+    gate_up = jnp.dot(post_normed, w_gathered[:, : 2 * ff_local], preferred_element_type=jnp.float32)
+    act = (jax.nn.silu(gate_up[:, :ff_local]) * gate_up[:, ff_local:]).astype(jnp.bfloat16)
+    terms = lax.dot_general(
+        act,
+        w_gathered[:, 2 * ff_local : 3 * ff_local],
+        (((1,), (1,)), ((), ())),
+        preferred_element_type=jnp.float32,
+    )
     ffn_total = tp_sum(terms.astype(jnp.bfloat16), 1).astype(jnp.float32)
     hidden = (mid_f + ffn_total).astype(jnp.bfloat16)
     return (hidden, key_cache, value_cache)

time: 272 us -> 260 us (0.956)
  local copies, waits for them, and re-layouts: 22.9 us -> 9.33 us
  waiting for transfers between devices: 121 us -> 126 us
  matrix products: 22.6 us -> 19.4 us
    slice x7 -> x0, local copies, waits for them, and re-layouts: 10.4 us -> none  [the longest x2 9.68 us: weight_part(): w_gathered[:, top:top + ff_rows, lo:hi].reshape(shards * ff_rows, hi - lo)]
    all_gather x1, waiting for transfers between devices: 82.5 us -> 86.6 us  [body(): kv_gathered = lax.all_gather(kv_packed, 'seq', axis=0, tiled=False)]
    dot_general x4 -> x2, matrix products: 12.1 us -> 8.84 us  [the longest x1 4.96 us: body(): jnp.dot(post_normed, w_gathered[:, :2 * ff_local], preferred_element_type...]
  transfers between devices with their start and end apart: 2 -> 2, of which waited for: 2 -> 2; matrix products, arithmetic and copies ran while one was open for 10% -> 9% of each run, Pallas kernels for 14% -> 15%
where the time goes in v9:
time: 260 us; the launch traced here: 259 us
  waiting for transfers between devices  126 us (48%)
  Pallas kernels  70.4 us (27%)
  matrix products  19.4 us (7%)
  between operations  16.9 us (6%)
  other arithmetic  16.5 us (6%)
  local copies, waits for them, and re-layouts  9.33 us (4%)
    all_gather x1, waiting for transfers between devices, body(): kv_gathered = lax.all_gather(kv_packed, 'seq', axis=0, tiled=False)  86.6 us
    pallas_call x2, Pallas kernels, tp_sum(): pl.pallas_call(functools.partial(tp_sum_kernel, n), out_shape=jax.ShapeDt...  62.9 us
    all_gather x1, waiting for transfers between devices, body(): lax.all_gather(weights_packed, 'seq', axis=0, tiled=False)  39.7 us
    pallas_call x1, Pallas kernels, attention(): pl.pallas_call(attention_kernel, out_shape=jax.ShapeDtypeStruct((rows, ou...  7.46 us
  transfers between devices with their start and end apart: 2, of which 2 were waited for; matrix products, arithmetic and copies ran while one was open for 9% of the time, Pallas kernels for 15%

profile of v9, /device:TPU:1, one launch (start us, length us, event | category | flops | bytes accessed | tf_op | source)
XLA Modules:
  0.0 258.9 jit_solution(2640346833935403914)
XLA Ops:
  7.3 1.6 fusion.7
  8.9 3.0 %multiply_reduce_fusion.1 = (f32[256,2]{0,1:T(2,128)S(1)}, f32[256,256]{0,1:T(8,128)}) fusion(bf16[2048,256]{1,0:T(8,128)(2,1)} %param.17, bf16[256,2048]{1,0:T(8,128)(2,1)} %param.14, f32[2048]{0:T(1024)} %param.15, f32[256]{0:T(256)S(1)} %add_rsqrt_fusion.3), kind=kOutput, calls=%fused_computation.33 | convolution fusion | flops 270663168 | bytes 2370560 | tf_op jit(solution)/shard_map/dot_general | solution.py:225
  13.3 1.0 multiply_multiply_fusion.1
  14.4 0.8 copy.45
  15.1 1.8 convolution_convert_fusion.1
  17.6 0.7 pad_maximum_fusion
  21.6 3.2 %fusion.24 = f32[256,512]{1,0:T(8,128)} fusion(bf16[2048,512]{1,0:T(8,128)(2,1)} %param.16, bf16[256,2048]{1,0:T(8,128)(2,1)S(1)} %copy-done.1, f32[2048]{0:T(1024)} %param.15, f32[256]{0:T(256)S(1)} %add_rsqrt_fusion.3), kind=kOutput, calls=%fused_computation.51 | convolution fusion | flops 538968064 | bytes 3679232 | tf_op jit(solution)/shard_map/dot_general | solution.py:221
  24.8 2.0 reshape.118
  26.8 1.4 multiply_reduce_fusion
  28.3 1.4 multiply_multiply_fusion
  32.2 1.3 pad_add_fusion.info
  33.5 1.8 pad_maximum_fusion.1
  36.0 86.6 %all-gather.5.cloned.1.call-done = bf16[32768,256]{1,0:T(8,128)(2,1)} async-done(((bf16[512,256]{1,0:T(8,128)(2,1)}), bf16[32768,256]{1,0:T(8,128)(2,1)}) %all-gather.5.cloned.1.call-update) | async-done | bytes 16777232 | tf_op jit(solution)/shard_map/all_gather | solution.py:239
  122.6 1.5 copy.43.q_last_ref
  124.2 1.6 copy.44.q_first_ref
  125.7 7.5 %shard_map.148 = bf16[256,512]{1,0:T(8,128)(2,1)} custom-call(s32[4]{0:T(128)} %pad_add_fusion.info, bf16[2,512,128]{2,1,0:T(8,128)(2,1)} %bitcast.31, s32[512,1]{1,0:T(8,128)} %copy.43.q_last_ref, s32[512,1]{1,0:T(8,128)} %copy.44.q_first_ref, bf16[64,512,256]{2,1,0:T(8,128)(2,1)} %bitcast.30), custom_call_target="tpu_custom_call" | custom-call | tf_op jit(solution)/shard_map/pallas_call | solution.py:187
  133.2 2.6 %convolution_convert_fusion.x_ref = bf16[256,2048]{1,0:T(8,128)(2,1)} fusion(bf16[256,512]{1,0:T(8,128)(2,1)} %shard_map.148, bf16[512,2048]{1,0:T(8,128)(2,1)S(1)} %copy-done), kind=kOutput, calls=%fused_computation.10 | convolution fusion | flops 537395200 | bytes 3407872 | tf_op jit(solution)/shard_map/dot_general | solution.py:270
  135.8 31.6 %shard_map.149 = bf16[256,2048]{1,0:T(8,128)(2,1)} custom-call(bf16[256,2048]{1,0:T(8,128)(2,1)} %convolution_convert_fusion.x_ref), custom_call_target="tpu_custom_call" | custom-call | tf_op jit(solution)/shard_map/pallas_call | solution.py:86
  167.4 1.6 fusion.11
  169.1 39.7 %all-gather.7.cloned.1.call-done = bf16[2048,2560]{1,0:T(8,128)(2,1)} async-done(((bf16[32,2560]{1,0:T(8,128)(2,1)}), bf16[2048,2560]{1,0:T(8,128)(2,1)}) %all-gather.7.cloned.1.call-update) | async-done | bytes 10485776 | tf_op jit(solution)/shard_map/all_gather | solution.py:266
  208.7 5.0 %fusion = f32[256,1536]{1,0:T(8,128)S(1)} fusion(bf16[2048,2560]{1,0:T(8,128)(2,1)} %all-gather.7.cloned.1.call-done, f32[2048]{0:T(1024)S(1)} %copy-done.13, f32[256]{0:T(256)S(1)} %add_rsqrt_fusion.2, bf16[256,2048]{1,0:T(8,128)(2,1)S(1)} %copy-done.1, bf16[256,2048]{1,0:T(8,128)(2,1)} %shard_map.149), kind=kOutput, calls=%fused_computation | convolution fusion | flops 1614807040 | bytes 9970688 | tf_op jit(solution)/shard_map/dot_general | solution.py:275
  213.7 3.9 %fusion.4.x_ref = bf16[256,2048]{1,0:T(8,128)(2,1)} fusion(bf16[2048,2560]{1,0:T(8,128)(2,1)} %all-gather.7.cloned.1.call-done, f32[256,1536]{1,0:T(8,128)S(1)} %fusion), kind=kOutput, calls=%fused_computation.11 | convolution fusion | flops 807010304 | bytes 5767168 | tf_op jit(solution)/shard_map/dot_general | solution.py:277
  217.6 31.3 %shard_map.150 = bf16[256,2048]{1,0:T(8,128)(2,1)} custom-call(bf16[256,2048]{1,0:T(8,128)(2,1)} %fusion.4.x_ref), custom_call_target="tpu_custom_call" | custom-call | tf_op jit(solution)/shard_map/pallas_call | solution.py:86
  248.9 3.1 %fusion.14 = bf16[256,2048]{1,0:T(8,128)(2,1)} fusion(bf16[256,2048]{1,0:T(8,128)(2,1)} %shard_map.150, bf16[256,2048]{1,0:T(8,128)(2,1)} %shard_map.149, bf16[256,2048]{1,0:T(8,128)(2,1)S(1)} %copy-done.1), kind=kLoop, calls=%fused_computation.19 | loop fusion | flops 4194304 | bytes 4194304 | tf_op jit(solution)/shard_map/convert_element_type | solution.py:284
  (54 shorter events, 6.0 us)
Async XLA Ops:
  7.2 126.0 %copy-start = (bf16[512,2048]{1,0:T(8,128)(2,1)S(1)}, bf16[512,2048]{1,0:T(8,128)(2,1)}, u32[]{:S(2)}) copy-start(bf16[512,2048]{1,0:T(8,128)(2,1)} %param.19) | copy-start | bytes 6291460
  7.2 4.8 %copy-start.10 = (s32[256]{0:T(256)S(1)}, s32[256]{0:T(256)}, u32[]{:S(2)}) copy-start(s32[256]{0:T(256)} %param.22) | copy-start | bytes 3076
  7.2 115.4 %all-gather.5.cloned.1.call-start = ((), (), s32[]{:S(2)}) async-start(), calls=%async_computation | async-start | bytes 17039360 | tf_op jit(solution)/shard_map/all_gather | solution.py:239
  8.9 4.4 %copy-start.11 = (f32[128]{0:T(128)S(1)}, f32[128]{0:T(128)}, u32[]{:S(2)}) copy-start(f32[128]{0:T(128)} %param.21) | copy-start | bytes 1540
  8.9 6.2 %copy-start.1 = (bf16[256,2048]{1,0:T(8,128)(2,1)S(1)}, bf16[256,2048]{1,0:T(8,128)(2,1)}, u32[]{:S(2)}) copy-start(bf16[256,2048]{1,0:T(8,128)(2,1)} %param.14) | copy-start | bytes 3145732
  12.5 5.9 %copy-start.7 = (s32[256]{0:T(256)}, s32[256]{0:T(256)S(1)}, u32[]{:S(2)}) copy-start(s32[256]{0:T(256)S(1)} %get-tuple-element.23) | copy-start | bytes 3076
  15.1 2.4 copy-start.2
  16.9 0.7 copy-start.3
  18.3 190.4 %all-gather.7.cloned.1.call-start = ((), (), s32[]{:S(2)}) async-start(), calls=%async_computation.1 | async-start | bytes 10649600 | tf_op jit(solution)/shard_map/all_gather | solution.py:266
  21.6 6.6 %copy-start.12 = (f32[128]{0:T(128)S(1)}, f32[128]{0:T(128)}, u32[]{:S(2)}) copy-start(f32[128]{0:T(128)} %param.20) | copy-start | bytes 1540
  28.2 2.7 %copy-start.8 = (s32[256]{0:T(256)S(1)}, s32[256]{0:T(256)}, u32[]{:S(2)}) copy-start(s32[256]{0:T(256)} %copy-done.7) | copy-start | bytes 3076
  28.2 3.3 %copy-start.9 = (s32[256]{0:T(256)S(1)}, s32[256]{0:T(256)}, u32[]{:S(2)}) copy-start(s32[256]{0:T(256)} %get-tuple-element.27) | copy-start | bytes 3076
  29.6 5.6 %copy-start.4 = (bf16[768,32]{0,1:T(8,128)(2,1)S(1)}, bf16[768,32]{0,1:T(8,128)(2,1)}, u32[]{:S(2)}) copy-start(bf16[768,32]{0,1:T(8,128)(2,1)} %param.26) | copy-start | bytes 147460
  29.6 5.6 %copy-start.5 = (bf16[32,768]{1,0:T(8,128)(2,1)S(1)}, bf16[32,768]{1,0:T(8,128)(2,1)}, u32[]{:S(2)}) copy-start(bf16[32,768]{1,0:T(8,128)(2,1)} %param.25) | copy-start | bytes 147460
  29.7 5.6 %copy-start.6 = (bf16[32,768]{1,0:T(8,128)(2,1)S(1)}, bf16[32,768]{1,0:T(8,128)(2,1)}, u32[]{:S(2)}) copy-start(bf16[32,768]{1,0:T(8,128)(2,1)} %param.24) | copy-start | bytes 147460
  135.8 72.9 %copy-start.13 = (f32[2048]{0:T(1024)S(1)}, f32[2048]{0:T(1024)}, u32[]{:S(2)}) copy-start(f32[2048]{0:T(1024)} %param.23) | copy-start | bytes 24580
Sparse Core Ops, SparseCore 0:
  18.5 104.0 all-gather.4
  125.3 83.3 all-gather.6

commit v10 on v9

--- a/solution.py
+++ b/solution.py
@@ -128,7 +128,7 @@
             s = lax.dot_general(q, k, (((1,), (1,)), ((), ())), preferred_element_type=jnp.float32) * scale
             if masked:
                 k_index = offset + lax.broadcasted_iota(jnp.int32, s.shape, 1)
-                allowed = (k_index <= q_last_ref[...]) & (k_index >= q_first_ref[...])
+                allowed = (k_index <= q_last_ref[:, :1]) & (k_index >= q_first_ref[:, :1])
                 s = jnp.where(allowed, s, -1e30)
             top = top_ref[g]
             new_top = jnp.maximum(top, jnp.max(s, axis=-1, keepdims=True))
@@ -173,8 +173,8 @@
         grid=(blocks,),
         in_specs=[
             pl.BlockSpec((groups, rows_all, head_size), lambda j, info: (0, 0, 0)),
-            pl.BlockSpec((rows_all, 1), lambda j, info: (0, 0)),
-            pl.BlockSpec((rows_all, 1), lambda j, info: (0, 0)),
+            pl.BlockSpec(q_last.shape, lambda j, info: (0, 0)),
+            pl.BlockSpec(q_first.shape, lambda j, info: (0, 0)),
             pl.BlockSpec((shards_per, kv_rows_per_shard, width_all), kv_map),
         ],
         out_specs=pl.BlockSpec((rows, out_cols), lambda j, info: (0, 0)),
@@ -237,10 +237,7 @@
     down_t = w_down.T
     kv_packed = jnp.concatenate([key_cache, value_cache], axis=0)
     kv_gathered = lax.all_gather(kv_packed, "seq", axis=0, tiled=False)
-    pad = -(3 * ff_local) % width_all
-    weights_packed = jnp.concatenate(
-        [w_gate, w_up, down_t, jnp.zeros((ff_rows, pad), down_t.dtype)], axis=1
-    )
+    weights_packed = jnp.concatenate([w_gate, w_up, down_t], axis=1)
 
     me = lax.axis_index("seq")
     first = me * rows
@@ -258,8 +255,9 @@
         .transpose(1, 2, 0, 3)
         .reshape(kv_local, head_group * rows, head_size)
     )
-    q_last = jnp.tile(q_index, head_group).reshape(head_group * rows, 1)
-    q_first = jnp.tile(q_start, head_group).reshape(head_group * rows, 1)
+    lanes = 128
+    q_last = jnp.broadcast_to(jnp.tile(q_index, head_group)[:, None], (head_group * rows, lanes))
+    q_first = jnp.broadcast_to(jnp.tile(q_start, head_group)[:, None], (head_group * rows, lanes))
     kv_gathered, weights_packed, q_grouped, q_last, q_first, info = lax.optimization_barrier(
         (kv_gathered, weights_packed, q_grouped, q_last, q_first, info)
     )

time: 260 us -> 258 us (level)
    optimization_barrier x2 -> x0, local copies, waits for them, and re-layouts: 3.09 us -> none  [body(): lax.optimization_barrier((kv_gathered, weights_packed, q_grouped, q_last,...]
    broadcast_in_dim x1 -> x2, local copies, waits for them, and re-layouts: 0.01 us -> 2.96 us  [the longest x1 1.51 us: body(): jnp.broadcast_to(jnp.tile(q_start, head_group)[:, None], (head_group * ro...]
  transfers between devices with their start and end apart: 2 -> 2, of which waited for: 2 -> 2; matrix products, arithmetic and copies ran while one was open for 9% -> 7% of each run, Pallas kernels for 15% -> 15%
where the time goes in v10:
time: 258 us
  waiting for transfers between devices  125 us (48%)
  Pallas kernels  70.2 us (27%)
  matrix products  19.4 us (8%)
  between operations  16.9 us (7%)
  other arithmetic  16.4 us (6%)
  local copies, waits for them, and re-layouts  9.16 us (4%)
    all_gather x1, waiting for transfers between devices, body(): kv_gathered = lax.all_gather(kv_packed, 'seq', axis=0, tiled=False)  86.5 us
    pallas_call x2, Pallas kernels, tp_sum(): pl.pallas_call(functools.partial(tp_sum_kernel, n), out_shape=jax.ShapeDt...  62.7 us
    all_gather x1, waiting for transfers between devices, body(): lax.all_gather(weights_packed, 'seq', axis=0, tiled=False)  38.9 us
    pallas_call x1, Pallas kernels, attention(): pl.pallas_call(attention_kernel, out_shape=jax.ShapeDtypeStruct((rows, ou...  7.46 us
  transfers between devices with their start and end apart: 2, of which 2 were waited for; matrix products, arithmetic and copies ran while one was open for 7% of the time, Pallas kernels for 15%

profile of v10, /device:TPU:1, one launch (start us, length us, event | category | flops | bytes accessed | tf_op | source)
XLA Modules:
  0.0 257.6 jit_solution(11733602447371293690)
XLA Ops:
  7.3 1.6 fusion.7
  8.9 3.0 %multiply_reduce_fusion.1 = (f32[256,2]{0,1:T(2,128)S(1)}, f32[256,256]{0,1:T(8,128)}) fusion(bf16[2048,256]{1,0:T(8,128)(2,1)} %param.17, bf16[256,2048]{1,0:T(8,128)(2,1)} %param.14, f32[2048]{0:T(1024)} %param.15, f32[256]{0:T(256)S(1)} %add_rsqrt_fusion.3), kind=kOutput, calls=%fused_computation.33 | convolution fusion | flops 270663168 | bytes 2370560 | tf_op jit(solution)/shard_map/dot_general | solution.py:225
  13.3 1.0 multiply_multiply_fusion.1
  14.4 0.8 copy.34
  15.1 1.8 convolution_convert_fusion.1
  17.6 0.7 pad_maximum_fusion
  21.7 3.2 %fusion.24 = f32[256,512]{1,0:T(8,128)} fusion(bf16[2048,512]{1,0:T(8,128)(2,1)} %param.16, bf16[256,2048]{1,0:T(8,128)(2,1)S(1)} %copy-done.1, f32[2048]{0:T(1024)} %param.15, f32[256]{0:T(256)S(1)} %add_rsqrt_fusion.3), kind=kOutput, calls=%fused_computation.51 | convolution fusion | flops 538968064 | bytes 3679232 | tf_op jit(solution)/shard_map/dot_general | solution.py:221
  24.8 2.0 reshape.120
  26.8 1.4 multiply_reduce_fusion
  28.3 1.4 multiply_multiply_fusion
  32.2 1.2 pad_add_fusion.info
  33.4 1.8 pad_maximum_fusion.1
  35.9 86.5 %all-gather.5.cloned.1.call-done = bf16[32768,256]{1,0:T(8,128)(2,1)} async-done(((bf16[512,256]{1,0:T(8,128)(2,1)}), bf16[32768,256]{1,0:T(8,128)(2,1)}) %all-gather.5.cloned.1.call-update) | async-done | bytes 16777232 | tf_op jit(solution)/shard_map/all_gather | solution.py:239
  122.4 1.5 broadcast_in_dim.11.q_first_ref
  123.9 1.5 broadcast_in_dim.9.q_last_ref
  125.4 7.5 %shard_map.148 = bf16[256,512]{1,0:T(8,128)(2,1)} custom-call(s32[4]{0:T(128)} %pad_add_fusion.info, bf16[2,512,128]{2,1,0:T(8,128)(2,1)} %bitcast.27, s32[512,128]{1,0:T(8,128)} %broadcast_in_dim.9.q_last_ref, s32[512,128]{1,0:T(8,128)} %broadcast_in_dim.11.q_first_ref, bf16[64,512,256]{2,1,0:T(8,128)(2,1)} %bitcast.26), custom_call_target="tpu_custom_call" | custom-call | tf_op jit(solution)/shard_map/pallas_call | solution.py:187
  132.9 2.6 %convolution_convert_fusion.x_ref = bf16[256,2048]{1,0:T(8,128)(2,1)} fusion(bf16[256,512]{1,0:T(8,128)(2,1)} %shard_map.148, bf16[512,2048]{1,0:T(8,128)(2,1)S(1)} %copy-done), kind=kOutput, calls=%fused_computation.10 | convolution fusion | flops 537395200 | bytes 3407872 | tf_op jit(solution)/shard_map/dot_general | solution.py:268
  135.5 31.3 %shard_map.149 = bf16[256,2048]{1,0:T(8,128)(2,1)} custom-call(bf16[256,2048]{1,0:T(8,128)(2,1)} %convolution_convert_fusion.x_ref), custom_call_target="tpu_custom_call" | custom-call | tf_op jit(solution)/shard_map/pallas_call | solution.py:86
  166.9 1.6 fusion.11
  168.5 38.9 %all-gather.7.cloned.1.call-done = bf16[2048,2304]{1,0:T(8,128)(2,1)} async-done(((bf16[32,2304]{1,0:T(8,128)(2,1)}), bf16[2048,2304]{1,0:T(8,128)(2,1)}) %all-gather.7.cloned.1.call-update) | async-done | bytes 9437200 | tf_op jit(solution)/shard_map/all_gather | solution.py:264
  207.4 5.0 %fusion = f32[256,1536]{1,0:T(8,128)S(1)} fusion(bf16[2048,2304]{1,0:T(8,128)(2,1)} %all-gather.7.cloned.1.call-done, f32[2048]{0:T(1024)S(1)} %copy-done.13, f32[256]{0:T(256)S(1)} %add_rsqrt_fusion.2, bf16[256,2048]{1,0:T(8,128)(2,1)S(1)} %copy-done.1, bf16[256,2048]{1,0:T(8,128)(2,1)} %shard_map.149), kind=kOutput, calls=%fused_computation | convolution fusion | flops 1614807040 | bytes 9970688 | tf_op jit(solution)/shard_map/dot_general | solution.py:273
  212.4 3.9 %fusion.4.x_ref = bf16[256,2048]{1,0:T(8,128)(2,1)} fusion(bf16[2048,2304]{1,0:T(8,128)(2,1)} %all-gather.7.cloned.1.call-done, f32[256,1536]{1,0:T(8,128)S(1)} %fusion), kind=kOutput, calls=%fused_computation.11 | convolution fusion | flops 807010304 | bytes 5767168 | tf_op jit(solution)/shard_map/dot_general | solution.py:275
  216.3 31.4 %shard_map.150 = bf16[256,2048]{1,0:T(8,128)(2,1)} custom-call(bf16[256,2048]{1,0:T(8,128)(2,1)} %fusion.4.x_ref), custom_call_target="tpu_custom_call" | custom-call | tf_op jit(solution)/shard_map/pallas_call | solution.py:86
  247.7 3.1 %fusion.14 = bf16[256,2048]{1,0:T(8,128)(2,1)} fusion(bf16[256,2048]{1,0:T(8,128)(2,1)} %shard_map.150, bf16[256,2048]{1,0:T(8,128)(2,1)} %shard_map.149, bf16[256,2048]{1,0:T(8,128)(2,1)S(1)} %copy-done.1), kind=kLoop, calls=%fused_computation.19 | loop fusion | flops 4194304 | bytes 4194304 | tf_op jit(solution)/shard_map/convert_element_type | solution.py:282
  (52 shorter events, 6.0 us)
Async XLA Ops:
  7.2 125.7 %copy-start = (bf16[512,2048]{1,0:T(8,128)(2,1)S(1)}, bf16[512,2048]{1,0:T(8,128)(2,1)}, u32[]{:S(2)}) copy-start(bf16[512,2048]{1,0:T(8,128)(2,1)} %param.19) | copy-start | bytes 6291460
  7.2 4.8 %copy-start.10 = (s32[256]{0:T(256)S(1)}, s32[256]{0:T(256)}, u32[]{:S(2)}) copy-start(s32[256]{0:T(256)} %param.22) | copy-start | bytes 3076
  7.2 115.2 %all-gather.5.cloned.1.call-start = ((), (), s32[]{:S(2)}) async-start(), calls=%async_computation | async-start | bytes 17039360 | tf_op jit(solution)/shard_map/all_gather | solution.py:239
  8.9 4.4 %copy-start.11 = (f32[128]{0:T(128)S(1)}, f32[128]{0:T(128)}, u32[]{:S(2)}) copy-start(f32[128]{0:T(128)} %param.21) | copy-start | bytes 1540
  8.9 6.2 %copy-start.1 = (bf16[256,2048]{1,0:T(8,128)(2,1)S(1)}, bf16[256,2048]{1,0:T(8,128)(2,1)}, u32[]{:S(2)}) copy-start(bf16[256,2048]{1,0:T(8,128)(2,1)} %param.14) | copy-start | bytes 3145732
  12.5 5.9 %copy-start.7 = (s32[256]{0:T(256)}, s32[256]{0:T(256)S(1)}, u32[]{:S(2)}) copy-start(s32[256]{0:T(256)S(1)} %get-tuple-element.23) | copy-start | bytes 3076
  15.1 2.4 copy-start.2
  16.9 0.7 copy-start.3
  18.3 189.1 %all-gather.7.cloned.1.call-start = ((), (), s32[]{:S(2)}) async-start(), calls=%async_computation.1 | async-start | bytes 9584640 | tf_op jit(solution)/shard_map/all_gather | solution.py:264
  21.7 6.6 %copy-start.12 = (f32[128]{0:T(128)S(1)}, f32[128]{0:T(128)}, u32[]{:S(2)}) copy-start(f32[128]{0:T(128)} %param.20) | copy-start | bytes 1540
  28.3 2.7 %copy-start.8 = (s32[256]{0:T(256)S(1)}, s32[256]{0:T(256)}, u32[]{:S(2)}) copy-start(s32[256]{0:T(256)} %copy-done.7) | copy-start | bytes 3076
  28.3 3.3 %copy-start.9 = (s32[256]{0:T(256)S(1)}, s32[256]{0:T(256)}, u32[]{:S(2)}) copy-start(s32[256]{0:T(256)} %get-tuple-element.27) | copy-start | bytes 3076
  29.7 5.5 %copy-start.4 = (bf16[768,32]{0,1:T(8,128)(2,1)S(1)}, bf16[768,32]{0,1:T(8,128)(2,1)}, u32[]{:S(2)}) copy-start(bf16[768,32]{0,1:T(8,128)(2,1)} %param.26) | copy-start | bytes 147460
  29.7 5.5 %copy-start.5 = (bf16[32,768]{1,0:T(8,128)(2,1)S(1)}, bf16[32,768]{1,0:T(8,128)(2,1)}, u32[]{:S(2)}) copy-start(bf16[32,768]{1,0:T(8,128)(2,1)} %param.25) | copy-start | bytes 147460
  29.7 5.5 %copy-start.6 = (bf16[32,768]{1,0:T(8,128)(2,1)S(1)}, bf16[32,768]{1,0:T(8,128)(2,1)}, u32[]{:S(2)}) copy-start(bf16[32,768]{1,0:T(8,128)(2,1)} %param.24) | copy-start | bytes 147460
  135.5 71.9 %copy-start.13 = (f32[2048]{0:T(1024)S(1)}, f32[2048]{0:T(1024)}, u32[]{:S(2)}) copy-start(f32[2048]{0:T(1024)} %param.23) | copy-start | bytes 24580
Sparse Core Ops, SparseCore 0:
  18.5 103.9 all-gather.4
  125.5 81.8 all-gather.6

commit v11 on v10

--- a/solution.py
+++ b/solution.py
@@ -28,7 +28,11 @@
     )
 
 
-def tp_sum_kernel(n, x_ref, out_ref, slots, reduced, send1, recv1, send2, recv2):
+def tp_sum_kernel(n, with_base, *refs):
+    if with_base:
+        x_ref, base_ref, out_ref, slots, reduced, send1, recv1, send2, recv2 = refs
+    else:
+        x_ref, out_ref, slots, reduced, send1, recv1, send2, recv2 = refs
     me = lax.axis_index("tp")
     row = lax.axis_index("seq")
     cols = x_ref.shape[1] // n
@@ -77,16 +81,21 @@
         second.append(copy)
     for copy in second:
         copy.wait()
-
-
-def tp_sum(x, collective_id):
+    if with_base:
+        out_ref[...] = (base_ref[...].astype(jnp.float32) + out_ref[...].astype(jnp.float32)).astype(
+            out_ref.dtype
+        )
+
+
+def tp_sum(x, collective_id, base=None):
     n = lax.axis_size("tp")
     rows, width = x.shape
     cols = width // n
+    operands = (x,) if base is None else (x, base)
     return pl.pallas_call(
-        functools.partial(tp_sum_kernel, n),
+        functools.partial(tp_sum_kernel, n, base is not None),
         out_shape=jax.ShapeDtypeStruct((rows, width), x.dtype),
-        in_specs=[pl.BlockSpec(memory_space=pltpu.VMEM)],
+        in_specs=[pl.BlockSpec(memory_space=pltpu.VMEM)] * len(operands),
         out_specs=pl.BlockSpec(memory_space=pltpu.VMEM),
         scratch_shapes=[
             pltpu.VMEM((n, rows, cols), x.dtype),
@@ -97,7 +106,7 @@
             pltpu.SemaphoreType.DMA((n,)),
         ],
         compiler_params=pltpu.CompilerParams(collective_id=collective_id, has_side_effects=True),
-    )(x)
+    )(*operands)
 
 
 def attention_kernel(info, q_ref, q_last_ref, q_first_ref, kv_ref, o_ref, top_ref, total_ref, acc_ref):
@@ -278,8 +287,7 @@
         (((1,), (1,)), ((), ())),
         preferred_element_type=jnp.float32,
     )
-    ffn_total = tp_sum(terms.astype(jnp.bfloat16), 1).astype(jnp.float32)
-    hidden = (mid_f + ffn_total).astype(jnp.bfloat16)
+    hidden = tp_sum(terms.astype(jnp.bfloat16), 1, mid)
     return (hidden, key_cache, value_cache)
 
 

time: 258 us -> 257 us (level)
  waiting for transfers between devices: 125 us -> 132 us
  other arithmetic: 16.4 us -> 10.6 us
    all_gather x1, waiting for transfers between devices: 86.5 us -> 92.1 us  [body(): kv_gathered = lax.all_gather(kv_packed, 'seq', axis=0, tiled=False)]
    convert_element_type x1 -> x0, other arithmetic: 3.1 us -> none  [body(): hidden = (mid_f + ffn_total).astype(jnp.bfloat16)]
  transfers between devices with their start and end apart: 2 -> 2, of which waited for: 2 -> 2; matrix products, arithmetic and copies ran while one was open for 7% -> 5% of each run, Pallas kernels for 15% -> 15%
where the time goes in v11:
time: 257 us
  waiting for transfers between devices  132 us (51%)
  Pallas kernels  70.8 us (28%)
  matrix products  19.1 us (7%)
  between operations  17 us (7%)
  other arithmetic  10.6 us (4%)
  local copies, waits for them, and re-layouts  7.57 us (3%)
    all_gather x1, waiting for transfers between devices, body(): kv_gathered = lax.all_gather(kv_packed, 'seq', axis=0, tiled=False)  92.1 us
    pallas_call x2, Pallas kernels, tp_sum(): pl.pallas_call(functools.partial(tp_sum_kernel, n, base is not None), out...  63.3 us
    all_gather x1, waiting for transfers between devices, body(): lax.all_gather(weights_packed, 'seq', axis=0, tiled=False)  39.4 us
    pallas_call x1, Pallas kernels, attention(): pl.pallas_call(attention_kernel, out_shape=jax.ShapeDtypeStruct((rows, ou...  7.45 us
  transfers between devices with their start and end apart: 2, of which 2 were waited for; matrix products, arithmetic and copies ran while one was open for 5% of the time, Pallas kernels for 15%

profile of v11, /device:TPU:1, one launch (start us, length us, event | category | flops | bytes accessed | tf_op | source)
XLA Modules:
  0.0 256.6 jit_solution(15169984874910136958)
XLA Ops:
  7.3 1.6 fusion.10
  8.9 3.0 %multiply_reduce_fusion.1 = (f32[256,2]{0,1:T(2,128)S(1)}, f32[256,256]{0,1:T(8,128)}) fusion(bf16[2048,256]{1,0:T(8,128)(2,1)} %param.17, bf16[256,2048]{1,0:T(8,128)(2,1)} %param.14, f32[2048]{0:T(1024)} %param.15, f32[256]{0:T(256)S(1)} %add_rsqrt_fusion.3), kind=kOutput, calls=%fused_computation.31 | convolution fusion | flops 270663168 | bytes 2370560 | tf_op jit(solution)/shard_map/dot_general | solution.py:234
  13.3 1.0 multiply_multiply_fusion.1
  14.4 0.8 copy.34
  15.1 1.8 convolution_convert_fusion.1
  17.6 0.7 pad_maximum_fusion
  18.4 0.6 fusion.28
  21.6 3.2 %fusion.22 = f32[256,512]{1,0:T(8,128)} fusion(bf16[2048,512]{1,0:T(8,128)(2,1)} %param.16, bf16[256,2048]{1,0:T(8,128)(2,1)S(1)} %copy-done.2, f32[2048]{0:T(1024)} %param.15, f32[256]{0:T(256)S(1)} %add_rsqrt_fusion.3), kind=kOutput, calls=%fused_computation.49 | convolution fusion | flops 538968064 | bytes 3679232 | tf_op jit(solution)/shard_map/dot_general | solution.py:230
  24.8 1.2 reshape.120
  27.4 1.3 pad_add_fusion.info
  28.7 0.8 pad_maximum_fusion.1
  29.6 0.7 pad_maximum_fusion.2
  30.3 92.1 %all-gather.5.cloned.1.call-done = bf16[32768,256]{1,0:T(8,128)(2,1)} async-done(((bf16[512,256]{1,0:T(8,128)(2,1)}), bf16[32768,256]{1,0:T(8,128)(2,1)}) %all-gather.5.cloned.1.call-update) | async-done | bytes 16777232 | tf_op jit(solution)/shard_map/all_gather | solution.py:248
  122.4 0.8 broadcast_in_dim.11.q_first_ref
  123.2 0.8 broadcast_in_dim.9.q_last_ref
  124.1 7.5 %shard_map.148 = bf16[256,512]{1,0:T(8,128)(2,1)} custom-call(s32[4]{0:T(128)} %pad_add_fusion.info, bf16[2,512,128]{2,1,0:T(8,128)(2,1)} %bitcast.27, s32[512,128]{1,0:T(8,128)} %broadcast_in_dim.9.q_last_ref, s32[512,128]{1,0:T(8,128)} %broadcast_in_dim.11.q_first_ref, bf16[64,512,256]{2,1,0:T(8,128)(2,1)} %bitcast.26), custom_call_target="tpu_custom_call" | custom-call | tf_op jit(solution)/shard_map/pallas_call | solution.py:196
  131.6 2.6 %convolution_convert_fusion.refs_0_ = bf16[256,2048]{1,0:T(8,128)(2,1)} fusion(bf16[256,512]{1,0:T(8,128)(2,1)} %shard_map.148, bf16[512,2048]{1,0:T(8,128)(2,1)S(1)} %copy-done), kind=kOutput, calls=%fused_computation.9 | convolution fusion | flops 537395200 | bytes 3407872 | tf_op jit(solution)/shard_map/dot_general | solution.py:277
  134.2 31.4 %shard_map.149 = bf16[256,2048]{1,0:T(8,128)(2,1)} custom-call(bf16[256,2048]{1,0:T(8,128)(2,1)} %convolution_convert_fusion.refs_0_), custom_call_target="tpu_custom_call" | custom-call | tf_op jit(solution)/shard_map/pallas_call | solution.py:95
  165.6 2.1 fusion.7
  167.7 39.4 %all-gather.7.cloned.1.call-done = bf16[2048,2304]{1,0:T(8,128)(2,1)} async-done(((bf16[32,2304]{1,0:T(8,128)(2,1)}), bf16[2048,2304]{1,0:T(8,128)(2,1)}) %all-gather.7.cloned.1.call-update) | async-done | bytes 9437200 | tf_op jit(solution)/shard_map/all_gather | solution.py:273
  207.0 4.6 %fusion = f32[256,1536]{1,0:T(8,128)S(1)} fusion(bf16[2048,2304]{1,0:T(8,128)(2,1)} %all-gather.7.cloned.1.call-done, bf16[256,2048]{1,0:T(8,128)(2,1)S(1)} %get-tuple-element.16.refs_1_, f32[2048]{0:T(1024)S(1)} %copy-done.14, f32[256]{0:T(256)S(1)} %add_rsqrt_fusion.2), kind=kOutput, calls=%fused_computation | convolution fusion | flops 1612709888 | bytes 8922112 | tf_op jit(solution)/shard_map/dot_general | solution.py:282
  211.7 3.9 %fusion.4.refs_0_ = bf16[256,2048]{1,0:T(8,128)(2,1)} fusion(bf16[2048,2304]{1,0:T(8,128)(2,1)} %all-gather.7.cloned.1.call-done, f32[256,1536]{1,0:T(8,128)S(1)} %fusion), kind=kOutput, calls=%fused_computation.10 | convolution fusion | flops 807010304 | bytes 5767168 | tf_op jit(solution)/shard_map/dot_general | solution.py:284
  215.6 31.9 %shard_map.150 = bf16[256,2048]{1,0:T(8,128)(2,1)} custom-call(bf16[256,2048]{1,0:T(8,128)(2,1)} %fusion.4.refs_0_, bf16[256,2048]{1,0:T(8,128)(2,1)} %copy-done.1), custom_call_target="tpu_custom_call" | custom-call | tf_op jit(solution)/shard_map/pallas_call | solution.py:95
  247.5 2.3 copy.39
  (54 shorter events, 3.5 us)
Async XLA Ops:
  7.2 124.4 %copy-start = (bf16[512,2048]{1,0:T(8,128)(2,1)S(1)}, bf16[512,2048]{1,0:T(8,128)(2,1)}, u32[]{:S(2)}) copy-start(bf16[512,2048]{1,0:T(8,128)(2,1)} %param.19) | copy-start | bytes 6291460
  7.2 4.8 %copy-start.11 = (s32[256]{0:T(256)S(1)}, s32[256]{0:T(256)}, u32[]{:S(2)}) copy-start(s32[256]{0:T(256)} %param.22) | copy-start | bytes 3076
  7.2 115.2 %all-gather.5.cloned.1.call-start = ((), (), s32[]{:S(2)}) async-start(), calls=%async_computation | async-start | bytes 17039360 | tf_op jit(solution)/shard_map/all_gather | solution.py:248
  8.9 4.4 %copy-start.12 = (f32[128]{0:T(128)S(1)}, f32[128]{0:T(128)}, u32[]{:S(2)}) copy-start(f32[128]{0:T(128)} %param.21) | copy-start | bytes 1540
  8.9 6.2 %copy-start.2 = (bf16[256,2048]{1,0:T(8,128)(2,1)S(1)}, bf16[256,2048]{1,0:T(8,128)(2,1)}, u32[]{:S(2)}) copy-start(bf16[256,2048]{1,0:T(8,128)(2,1)} %param.14) | copy-start | bytes 3145732
  12.6 5.8 %copy-start.8 = (s32[256]{0:T(256)}, s32[256]{0:T(256)S(1)}, u32[]{:S(2)}) copy-start(s32[256]{0:T(256)S(1)} %get-tuple-element.25) | copy-start | bytes 3076
  15.1 2.4 copy-start.3
  16.9 0.7 copy-start.4
  18.3 188.7 %all-gather.7.cloned.1.call-start = ((), (), s32[]{:S(2)}) async-start(), calls=%async_computation.1 | async-start | bytes 9584640 | tf_op jit(solution)/shard_map/all_gather | solution.py:273
  21.6 4.8 %copy-start.13 = (f32[128]{0:T(128)S(1)}, f32[128]{0:T(128)}, u32[]{:S(2)}) copy-start(f32[128]{0:T(128)} %param.20) | copy-start | bytes 1540
  26.4 1.0 copy-start.9
  26.4 1.0 copy-start.10
  26.8 2.8 %copy-start.5 = (bf16[768,32]{0,1:T(8,128)(2,1)S(1)}, bf16[768,32]{0,1:T(8,128)(2,1)}, u32[]{:S(2)}) copy-start(bf16[768,32]{0,1:T(8,128)(2,1)} %param.26) | copy-start | bytes 147460
  26.8 2.8 %copy-start.6 = (bf16[32,768]{1,0:T(8,128)(2,1)S(1)}, bf16[32,768]{1,0:T(8,128)(2,1)}, u32[]{:S(2)}) copy-start(bf16[32,768]{1,0:T(8,128)(2,1)} %param.25) | copy-start | bytes 147460
  26.8 2.8 %copy-start.7 = (bf16[32,768]{1,0:T(8,128)(2,1)S(1)}, bf16[32,768]{1,0:T(8,128)(2,1)}, u32[]{:S(2)}) copy-start(bf16[32,768]{1,0:T(8,128)(2,1)} %param.24) | copy-start | bytes 147460
  165.6 41.5 %copy-start.14 = (f32[2048]{0:T(1024)S(1)}, f32[2048]{0:T(1024)}, u32[]{:S(2)}) copy-start(f32[2048]{0:T(1024)} %param.23) | copy-start | bytes 24580
  167.6 44.0 %copy-start.1 = (bf16[256,2048]{1,0:T(8,128)(2,1)}, bf16[256,2048]{1,0:T(8,128)(2,1)S(1)}, u32[]{:S(2)}) copy-start(bf16[256,2048]{1,0:T(8,128)(2,1)S(1)} %get-tuple-element.16.refs_1_) | copy-start | bytes 3145732
Sparse Core Ops, SparseCore 0:
  18.4 103.8 all-gather.4
  125.1 81.8 all-gather.6

commit v12 on v11

--- a/solution.py
+++ b/solution.py
@@ -278,7 +278,7 @@
     summed = tp_sum(partial_out.astype(jnp.bfloat16), 0).astype(jnp.float32)
     mid = (xf + summed).astype(jnp.bfloat16)
     mid_f = mid.astype(jnp.float32)
-    post_normed = rms(mid_f, post_gain).astype(jnp.bfloat16)
+    post_normed = lax.optimization_barrier(rms(mid_f, post_gain).astype(jnp.bfloat16))
     gate_up = jnp.dot(post_normed, w_gathered[:, : 2 * ff_local], preferred_element_type=jnp.float32)
     act = (jax.nn.silu(gate_up[:, :ff_local]) * gate_up[:, ff_local:]).astype(jnp.bfloat16)
     terms = lax.dot_general(

time: 257 us -> 257 us (level)
  transfers between devices with their start and end apart: 2 -> 2, of which waited for: 2 -> 2; matrix products, arithmetic and copies ran while one was open for 5% -> 6% of each run, Pallas kernels for 15% -> 15%
where the time goes in v12:
time: 257 us
  waiting for transfers between devices  130 us (51%)
  Pallas kernels  70.8 us (28%)
  matrix products  19.4 us (8%)
  between operations  17 us (7%)
  other arithmetic  11.9 us (5%)
  local copies, waits for them, and re-layouts  7.57 us (3%)
    all_gather x1, waiting for transfers between devices, body(): kv_gathered = lax.all_gather(kv_packed, 'seq', axis=0, tiled=False)  92.1 us
    pallas_call x2, Pallas kernels, tp_sum(): pl.pallas_call(functools.partial(tp_sum_kernel, n, base is not None), out...  63.3 us
    all_gather x1, waiting for transfers between devices, body(): lax.all_gather(weights_packed, 'seq', axis=0, tiled=False)  38.1 us
    pallas_call x1, Pallas kernels, attention(): pl.pallas_call(attention_kernel, out_shape=jax.ShapeDtypeStruct((rows, ou...  7.45 us
  transfers between devices with their start and end apart: 2, of which 2 were waited for; matrix products, arithmetic and copies ran while one was open for 6% of the time, Pallas kernels for 15%

profile of v12, /device:TPU:1, one launch (start us, length us, event | category | flops | bytes accessed | tf_op | source)
XLA Modules:
  0.0 257.0 jit_solution(15901849324458016592)
XLA Ops:
  7.3 1.6 fusion.10
  8.9 3.0 %multiply_reduce_fusion.1 = (f32[256,2]{0,1:T(2,128)S(1)}, f32[256,256]{0,1:T(8,128)}) fusion(bf16[2048,256]{1,0:T(8,128)(2,1)} %param.17, bf16[256,2048]{1,0:T(8,128)(2,1)} %param.14, f32[2048]{0:T(1024)} %param.15, f32[256]{0:T(256)S(1)} %add_rsqrt_fusion.3), kind=kOutput, calls=%fused_computation.29 | convolution fusion | flops 270663168 | bytes 2370560 | tf_op jit(solution)/shard_map/dot_general | solution.py:234
  13.3 1.0 multiply_multiply_fusion.1
  14.4 0.8 copy.34
  15.1 1.8 convolution_convert_fusion.1
  17.6 0.7 pad_maximum_fusion
  21.6 3.2 %fusion.19 = f32[256,512]{1,0:T(8,128)} fusion(bf16[2048,512]{1,0:T(8,128)(2,1)} %param.16, bf16[256,2048]{1,0:T(8,128)(2,1)S(1)} %copy-done.2, f32[2048]{0:T(1024)} %param.15, f32[256]{0:T(256)S(1)} %add_rsqrt_fusion.3), kind=kOutput, calls=%fused_computation.47 | convolution fusion | flops 538968064 | bytes 3679232 | tf_op jit(solution)/shard_map/dot_general | solution.py:230
  24.8 1.2 reshape.120
  27.4 1.3 pad_add_fusion.info
  28.7 0.8 pad_maximum_fusion.1
  29.6 0.7 pad_maximum_fusion.2
  30.3 92.1 %all-gather.5.cloned.1.call-done = bf16[32768,256]{1,0:T(8,128)(2,1)} async-done(((bf16[512,256]{1,0:T(8,128)(2,1)}), bf16[32768,256]{1,0:T(8,128)(2,1)}) %all-gather.5.cloned.1.call-update) | async-done | bytes 16777232 | tf_op jit(solution)/shard_map/all_gather | solution.py:248
  122.4 0.8 broadcast_in_dim.11.q_first_ref
  123.2 0.8 broadcast_in_dim.9.q_last_ref
  124.1 7.5 %shard_map.148 = bf16[256,512]{1,0:T(8,128)(2,1)} custom-call(s32[4]{0:T(128)} %pad_add_fusion.info, bf16[2,512,128]{2,1,0:T(8,128)(2,1)} %bitcast.28, s32[512,128]{1,0:T(8,128)} %broadcast_in_dim.9.q_last_ref, s32[512,128]{1,0:T(8,128)} %broadcast_in_dim.11.q_first_ref, bf16[64,512,256]{2,1,0:T(8,128)(2,1)} %bitcast.27), custom_call_target="tpu_custom_call" | custom-call | tf_op jit(solution)/shard_map/pallas_call | solution.py:196
  131.6 2.6 %convolution_convert_fusion.refs_0_ = bf16[256,2048]{1,0:T(8,128)(2,1)} fusion(bf16[256,512]{1,0:T(8,128)(2,1)} %shard_map.148, bf16[512,2048]{1,0:T(8,128)(2,1)S(1)} %copy-done), kind=kOutput, calls=%fused_computation.9 | convolution fusion | flops 537395200 | bytes 3407872 | tf_op jit(solution)/shard_map/dot_general | solution.py:277
  134.2 31.4 %shard_map.149 = bf16[256,2048]{1,0:T(8,128)(2,1)} custom-call(bf16[256,2048]{1,0:T(8,128)(2,1)} %convolution_convert_fusion.refs_0_), custom_call_target="tpu_custom_call" | custom-call | tf_op jit(solution)/shard_map/pallas_call | solution.py:95
  165.6 2.1 fusion.7
  167.7 1.3 fusion.9
  169.0 38.1 %all-gather.7.cloned.1.call-done = bf16[2048,2304]{1,0:T(8,128)(2,1)} async-done(((bf16[32,2304]{1,0:T(8,128)(2,1)}), bf16[2048,2304]{1,0:T(8,128)(2,1)}) %all-gather.7.cloned.1.call-update) | async-done | bytes 9437200 | tf_op jit(solution)/shard_map/all_gather | solution.py:273
  207.1 4.9 %fusion = f32[256,1536]{1,0:T(8,128)S(1)} fusion(bf16[256,2048]{1,0:T(8,128)(2,1)} %fusion.9, bf16[2048,2304]{1,0:T(8,128)(2,1)} %all-gather.7.cloned.1.call-done), kind=kOutput, calls=%fused_computation | convolution fusion | flops 1610612736 | bytes 8912896 | tf_op jit(solution)/shard_map/dot_general | solution.py:282
  212.0 3.9 %fusion.4.refs_0_ = bf16[256,2048]{1,0:T(8,128)(2,1)} fusion(bf16[2048,2304]{1,0:T(8,128)(2,1)} %all-gather.7.cloned.1.call-done, f32[256,1536]{1,0:T(8,128)S(1)} %fusion), kind=kOutput, calls=%fused_computation.10 | convolution fusion | flops 807010304 | bytes 5767168 | tf_op jit(solution)/shard_map/dot_general | solution.py:284
  215.9 31.9 %shard_map.150 = bf16[256,2048]{1,0:T(8,128)(2,1)} custom-call(bf16[256,2048]{1,0:T(8,128)(2,1)} %fusion.4.refs_0_, bf16[256,2048]{1,0:T(8,128)(2,1)} %copy-done.1), custom_call_target="tpu_custom_call" | custom-call | tf_op jit(solution)/shard_map/pallas_call | solution.py:95
  247.8 2.3 copy.39
  (55 shorter events, 4.1 us)
Async XLA Ops:
  7.2 124.4 %copy-start = (bf16[512,2048]{1,0:T(8,128)(2,1)S(1)}, bf16[512,2048]{1,0:T(8,128)(2,1)}, u32[]{:S(2)}) copy-start(bf16[512,2048]{1,0:T(8,128)(2,1)} %param.19) | copy-start | bytes 6291460
  7.2 4.8 %copy-start.12 = (s32[256]{0:T(256)S(1)}, s32[256]{0:T(256)}, u32[]{:S(2)}) copy-start(s32[256]{0:T(256)} %param.22) | copy-start | bytes 3076
  7.2 115.2 %all-gather.5.cloned.1.call-start = ((), (), s32[]{:S(2)}) async-start(), calls=%async_computation | async-start | bytes 17039360 | tf_op jit(solution)/shard_map/all_gather | solution.py:248
  8.9 4.4 %copy-start.13 = (f32[128]{0:T(128)S(1)}, f32[128]{0:T(128)}, u32[]{:S(2)}) copy-start(f32[128]{0:T(128)} %param.21) | copy-start | bytes 1540
  8.9 6.2 %copy-start.2 = (bf16[256,2048]{1,0:T(8,128)(2,1)S(1)}, bf16[256,2048]{1,0:T(8,128)(2,1)}, u32[]{:S(2)}) copy-start(bf16[256,2048]{1,0:T(8,128)(2,1)} %param.14) | copy-start | bytes 3145732
  12.6 5.8 %copy-start.8 = (s32[256]{0:T(256)}, s32[256]{0:T(256)S(1)}, u32[]{:S(2)}) copy-start(s32[256]{0:T(256)S(1)} %get-tuple-element.25) | copy-start | bytes 3076
  15.1 2.4 copy-start.3
  16.9 0.7 copy-start.4
  18.3 188.7 %all-gather.7.cloned.1.call-start = ((), (), s32[]{:S(2)}) async-start(), calls=%async_computation.1 | async-start | bytes 9584640 | tf_op jit(solution)/shard_map/all_gather | solution.py:273
  21.6 4.8 %copy-start.14 = (f32[128]{0:T(128)S(1)}, f32[128]{0:T(128)}, u32[]{:S(2)}) copy-start(f32[128]{0:T(128)} %param.20) | copy-start | bytes 1540
  26.4 1.0 copy-start.9
  26.4 1.0 copy-start.11
  26.8 2.8 %copy-start.5 = (bf16[768,32]{0,1:T(8,128)(2,1)S(1)}, bf16[768,32]{0,1:T(8,128)(2,1)}, u32[]{:S(2)}) copy-start(bf16[768,32]{0,1:T(8,128)(2,1)} %param.26) | copy-start | bytes 147460
  26.8 2.8 %copy-start.6 = (bf16[32,768]{1,0:T(8,128)(2,1)S(1)}, bf16[32,768]{1,0:T(8,128)(2,1)}, u32[]{:S(2)}) copy-start(bf16[32,768]{1,0:T(8,128)(2,1)} %param.25) | copy-start | bytes 147460
  26.8 2.8 %copy-start.7 = (bf16[32,768]{1,0:T(8,128)(2,1)S(1)}, bf16[32,768]{1,0:T(8,128)(2,1)}, u32[]{:S(2)}) copy-start(bf16[32,768]{1,0:T(8,128)(2,1)} %param.24) | copy-start | bytes 147460
  165.6 2.1 copy-start.10
  167.6 44.3 %copy-start.1 = (bf16[256,2048]{1,0:T(8,128)(2,1)}, bf16[256,2048]{1,0:T(8,128)(2,1)S(1)}, u32[]{:S(2)}) copy-start(bf16[256,2048]{1,0:T(8,128)(2,1)S(1)} %get-tuple-element.16.refs_1_) | copy-start | bytes 3145732
Sparse Core Ops, SparseCore 0:
  18.4 103.8 all-gather.4
  125.1 81.8 all-gather.6

commit v13 on v12

--- a/solution.py
+++ b/solution.py
@@ -28,7 +28,7 @@
     )
 
 
-def tp_sum_kernel(n, with_base, *refs):
+def tp_sum_kernel(n, parts, with_base, *refs):
     if with_base:
         x_ref, base_ref, out_ref, slots, reduced, send1, recv1, send2, recv2 = refs
     else:
@@ -36,49 +36,57 @@
     me = lax.axis_index("tp")
     row = lax.axis_index("seq")
     cols = x_ref.shape[1] // n
+    rows_p = x_ref.shape[0] // parts
 
     barrier = pltpu.get_barrier_semaphore()
     for k in range(1, n):
         pl.semaphore_signal(barrier, inc=1, device_id=(row, lax.rem(me + k, n)), device_id_type=MESH)
     pl.semaphore_wait(barrier, n - 1)
 
-    def block(ref, owner):
-        return ref.at[:, pl.ds(pl.multiple_of(owner * cols, cols), cols)]
+    def cols_of(owner):
+        return pl.ds(pl.multiple_of(owner * cols, cols), cols)
+
+    def rows_of(c):
+        return pl.ds(c * rows_p, rows_p)
 
     first = []
-    for k in range(1, n):
-        peer = lax.rem(me + k, n)
-        copy = pltpu.make_async_remote_copy(
-            src_ref=block(x_ref, peer),
-            dst_ref=slots.at[k],
-            send_sem=send1.at[k],
-            recv_sem=recv1.at[k],
-            device_id=(row, peer),
-            device_id_type=MESH,
-        )
-        copy.start()
-        first.append(copy)
-    for copy in first:
-        copy.wait()
-    total = block(x_ref, me)[...].astype(jnp.float32)
-    for k in range(1, n):
-        total = total + slots[k].astype(jnp.float32)
-    reduced[...] = total.astype(reduced.dtype)
-    block(out_ref, me)[...] = reduced[...]
+    for c in range(parts):
+        part = []
+        for k in range(1, n):
+            peer = lax.rem(me + k, n)
+            copy = pltpu.make_async_remote_copy(
+                src_ref=x_ref.at[rows_of(c), cols_of(peer)],
+                dst_ref=slots.at[k, rows_of(c)],
+                send_sem=send1.at[c, k],
+                recv_sem=recv1.at[c, k],
+                device_id=(row, peer),
+                device_id_type=MESH,
+            )
+            copy.start()
+            part.append(copy)
+        first.append(part)
 
     second = []
-    for k in range(1, n):
-        peer = lax.rem(me + k, n)
-        copy = pltpu.make_async_remote_copy(
-            src_ref=reduced,
-            dst_ref=block(out_ref, me),
-            send_sem=send2.at[k],
-            recv_sem=recv2.at[k],
-            device_id=(row, peer),
-            device_id_type=MESH,
-        )
-        copy.start()
-        second.append(copy)
+    for c in range(parts):
+        for copy in first[c]:
+            copy.wait()
+        total = x_ref[rows_of(c), cols_of(me)].astype(jnp.float32)
+        for k in range(1, n):
+            total = total + slots[k, rows_of(c)].astype(jnp.float32)
+        reduced[rows_of(c)] = total.astype(reduced.dtype)
+        out_ref[rows_of(c), cols_of(me)] = reduced[rows_of(c)]
+        for k in range(1, n):
+            peer = lax.rem(me + k, n)
+            copy = pltpu.make_async_remote_copy(
+                src_ref=reduced.at[rows_of(c)],
+                dst_ref=out_ref.at[rows_of(c), cols_of(me)],
+                send_sem=send2.at[c, k],
+                recv_sem=recv2.at[c, k],
+                device_id=(row, peer),
+                device_id_type=MESH,
+            )
+            copy.start()
+            second.append(copy)
     for copy in second:
         copy.wait()
     if with_base:
@@ -92,18 +100,19 @@
     rows, width = x.shape
     cols = width // n
     operands = (x,) if base is None else (x, base)
+    parts = 2 if rows % 32 == 0 else 1
     return pl.pallas_call(
-        functools.partial(tp_sum_kernel, n, base is not None),
+        functools.partial(tp_sum_kernel, n, parts, base is not None),
         out_shape=jax.ShapeDtypeStruct((rows, width), x.dtype),
         in_specs=[pl.BlockSpec(memory_space=pltpu.VMEM)] * len(operands),
         out_specs=pl.BlockSpec(memory_space=pltpu.VMEM),
         scratch_shapes=[
             pltpu.VMEM((n, rows, cols), x.dtype),
             pltpu.VMEM((rows, cols), x.dtype),
-            pltpu.SemaphoreType.DMA((n,)),
-            pltpu.SemaphoreType.DMA((n,)),
-            pltpu.SemaphoreType.DMA((n,)),
-            pltpu.SemaphoreType.DMA((n,)),
+            pltpu.SemaphoreType.DMA((parts, n)),
+            pltpu.SemaphoreType.DMA((parts, n)),
+            pltpu.SemaphoreType.DMA((parts, n)),
+            pltpu.SemaphoreType.DMA((parts, n)),
         ],
         compiler_params=pltpu.CompilerParams(collective_id=collective_id, has_side_effects=True),
     )(*operands)

time: 257 us -> 255 us (level)
  Pallas kernels: 70.8 us -> 66.7 us
    pallas_call x2, Pallas kernels: 63.3 us -> 59.2 us  [tp_sum(): pl.pallas_call(functools.partial(tp_sum_kernel, n, parts, base is not Non...]
  transfers between devices with their start and end apart: 2 -> 2, of which waited for: 2 -> 2; matrix products, arithmetic and copies ran while one was open for 6% -> 6% of each run, Pallas kernels for 15% -> 14%
where the time goes in v13:
time: 255 us
  waiting for transfers between devices  132 us (52%)
  Pallas kernels  66.7 us (26%)
  matrix products  19.4 us (8%)
  between operations  17 us (7%)
  other arithmetic  11.9 us (5%)
  local copies, waits for them, and re-layouts  7.57 us (3%)
    all_gather x1, waiting for transfers between devices, body(): kv_gathered = lax.all_gather(kv_packed, 'seq', axis=0, tiled=False)  92.1 us
    pallas_call x2, Pallas kernels, tp_sum(): pl.pallas_call(functools.partial(tp_sum_kernel, n, parts, base is not Non...  59.2 us
    all_gather x1, waiting for transfers between devices, body(): lax.all_gather(weights_packed, 'seq', axis=0, tiled=False)  40.1 us
    pallas_call x1, Pallas kernels, attention(): pl.pallas_call(attention_kernel, out_shape=jax.ShapeDtypeStruct((rows, ou...  7.45 us
  transfers between devices with their start and end apart: 2, of which 2 were waited for; matrix products, arithmetic and copies ran while one was open for 6% of the time, Pallas kernels for 14%

profile of v13, /device:TPU:1, one launch (start us, length us, event | category | flops | bytes accessed | tf_op | source)
XLA Modules:
  0.0 254.9 jit_solution(13911911107909719108)
XLA Ops:
  7.3 1.6 fusion.10
  8.9 3.0 %multiply_reduce_fusion.1 = (f32[256,2]{0,1:T(2,128)S(1)}, f32[256,256]{0,1:T(8,128)}) fusion(bf16[2048,256]{1,0:T(8,128)(2,1)} %param.17, bf16[256,2048]{1,0:T(8,128)(2,1)} %param.14, f32[2048]{0:T(1024)} %param.15, f32[256]{0:T(256)S(1)} %add_rsqrt_fusion.3), kind=kOutput, calls=%fused_computation.29 | convolution fusion | flops 270663168 | bytes 2370560 | tf_op jit(solution)/shard_map/dot_general | solution.py:243
  13.3 1.0 multiply_multiply_fusion.1
  14.4 0.8 copy.34
  15.1 1.8 convolution_convert_fusion.1
  17.6 0.7 pad_maximum_fusion
  21.6 3.2 %fusion.19 = f32[256,512]{1,0:T(8,128)} fusion(bf16[2048,512]{1,0:T(8,128)(2,1)} %param.16, bf16[256,2048]{1,0:T(8,128)(2,1)S(1)} %copy-done.2, f32[2048]{0:T(1024)} %param.15, f32[256]{0:T(256)S(1)} %add_rsqrt_fusion.3), kind=kOutput, calls=%fused_computation.47 | convolution fusion | flops 538968064 | bytes 3679232 | tf_op jit(solution)/shard_map/dot_general | solution.py:239
  24.8 1.2 reshape.120
  27.4 1.3 pad_add_fusion.info
  28.7 0.8 pad_maximum_fusion.1
  29.6 0.7 pad_maximum_fusion.2
  30.3 92.1 %all-gather.5.cloned.1.call-done = bf16[32768,256]{1,0:T(8,128)(2,1)} async-done(((bf16[512,256]{1,0:T(8,128)(2,1)}), bf16[32768,256]{1,0:T(8,128)(2,1)}) %all-gather.5.cloned.1.call-update) | async-done | bytes 16777232 | tf_op jit(solution)/shard_map/all_gather | solution.py:257
  122.4 0.8 broadcast_in_dim.11.q_first_ref
  123.2 0.8 broadcast_in_dim.9.q_last_ref
  124.1 7.5 %shard_map.148 = bf16[256,512]{1,0:T(8,128)(2,1)} custom-call(s32[4]{0:T(128)} %pad_add_fusion.info, bf16[2,512,128]{2,1,0:T(8,128)(2,1)} %bitcast.28, s32[512,128]{1,0:T(8,128)} %broadcast_in_dim.9.q_last_ref, s32[512,128]{1,0:T(8,128)} %broadcast_in_dim.11.q_first_ref, bf16[64,512,256]{2,1,0:T(8,128)(2,1)} %bitcast.27), custom_call_target="tpu_custom_call" | custom-call | tf_op jit(solution)/shard_map/pallas_call | solution.py:205
  131.6 2.6 %convolution_convert_fusion.refs_0_ = bf16[256,2048]{1,0:T(8,128)(2,1)} fusion(bf16[256,512]{1,0:T(8,128)(2,1)} %shard_map.148, bf16[512,2048]{1,0:T(8,128)(2,1)S(1)} %copy-done), kind=kOutput, calls=%fused_computation.9 | convolution fusion | flops 537395200 | bytes 3407872 | tf_op jit(solution)/shard_map/dot_general | solution.py:286
  134.2 29.3 %shard_map.149 = bf16[256,2048]{1,0:T(8,128)(2,1)} custom-call(bf16[256,2048]{1,0:T(8,128)(2,1)} %convolution_convert_fusion.refs_0_), custom_call_target="tpu_custom_call" | custom-call | tf_op jit(solution)/shard_map/pallas_call | solution.py:104
  163.5 2.1 fusion.7
  165.6 1.3 fusion.9
  166.9 40.1 %all-gather.7.cloned.1.call-done = bf16[2048,2304]{1,0:T(8,128)(2,1)} async-done(((bf16[32,2304]{1,0:T(8,128)(2,1)}), bf16[2048,2304]{1,0:T(8,128)(2,1)}) %all-gather.7.cloned.1.call-update) | async-done | bytes 9437200 | tf_op jit(solution)/shard_map/all_gather | solution.py:282
  207.0 4.9 %fusion = f32[256,1536]{1,0:T(8,128)S(1)} fusion(bf16[256,2048]{1,0:T(8,128)(2,1)} %fusion.9, bf16[2048,2304]{1,0:T(8,128)(2,1)} %all-gather.7.cloned.1.call-done), kind=kOutput, calls=%fused_computation | convolution fusion | flops 1610612736 | bytes 8912896 | tf_op jit(solution)/shard_map/dot_general | solution.py:291
  212.0 3.9 %fusion.4.refs_0_ = bf16[256,2048]{1,0:T(8,128)(2,1)} fusion(bf16[2048,2304]{1,0:T(8,128)(2,1)} %all-gather.7.cloned.1.call-done, f32[256,1536]{1,0:T(8,128)S(1)} %fusion), kind=kOutput, calls=%fused_computation.10 | convolution fusion | flops 807010304 | bytes 5767168 | tf_op jit(solution)/shard_map/dot_general | solution.py:293
  215.9 29.9 %shard_map.150 = bf16[256,2048]{1,0:T(8,128)(2,1)} custom-call(bf16[256,2048]{1,0:T(8,128)(2,1)} %fusion.4.refs_0_, bf16[256,2048]{1,0:T(8,128)(2,1)} %copy-done.1), custom_call_target="tpu_custom_call" | custom-call | tf_op jit(solution)/shard_map/pallas_call | solution.py:104
  245.8 2.3 copy.39
  (55 shorter events, 4.1 us)
Async XLA Ops:
  7.2 124.4 %copy-start = (bf16[512,2048]{1,0:T(8,128)(2,1)S(1)}, bf16[512,2048]{1,0:T(8,128)(2,1)}, u32[]{:S(2)}) copy-start(bf16[512,2048]{1,0:T(8,128)(2,1)} %param.19) | copy-start | bytes 6291460
  7.2 4.8 %copy-start.12 = (s32[256]{0:T(256)S(1)}, s32[256]{0:T(256)}, u32[]{:S(2)}) copy-start(s32[256]{0:T(256)} %param.22) | copy-start | bytes 3076
  7.2 115.2 %all-gather.5.cloned.1.call-start = ((), (), s32[]{:S(2)}) async-start(), calls=%async_computation | async-start | bytes 17039360 | tf_op jit(solution)/shard_map/all_gather | solution.py:257
  8.9 4.4 %copy-start.13 = (f32[128]{0:T(128)S(1)}, f32[128]{0:T(128)}, u32[]{:S(2)}) copy-start(f32[128]{0:T(128)} %param.21) | copy-start | bytes 1540
  8.9 6.2 %copy-start.2 = (bf16[256,2048]{1,0:T(8,128)(2,1)S(1)}, bf16[256,2048]{1,0:T(8,128)(2,1)}, u32[]{:S(2)}) copy-start(bf16[256,2048]{1,0:T(8,128)(2,1)} %param.14) | copy-start | bytes 3145732
  12.6 5.8 %copy-start.8 = (s32[256]{0:T(256)}, s32[256]{0:T(256)S(1)}, u32[]{:S(2)}) copy-start(s32[256]{0:T(256)S(1)} %get-tuple-element.25) | copy-start | bytes 3076
  15.1 2.4 copy-start.3
  16.9 0.7 copy-start.4
  18.3 188.7 %all-gather.7.cloned.1.call-start = ((), (), s32[]{:S(2)}) async-start(), calls=%async_computation.1 | async-start | bytes 9584640 | tf_op jit(solution)/shard_map/all_gather | solution.py:282
  21.6 4.8 %copy-start.14 = (f32[128]{0:T(128)S(1)}, f32[128]{0:T(128)}, u32[]{:S(2)}) copy-start(f32[128]{0:T(128)} %param.20) | copy-start | bytes 1540
  26.4 1.0 copy-start.9
  26.4 1.0 copy-start.11
  26.8 2.8 %copy-start.5 = (bf16[768,32]{0,1:T(8,128)(2,1)S(1)}, bf16[768,32]{0,1:T(8,128)(2,1)}, u32[]{:S(2)}) copy-start(bf16[768,32]{0,1:T(8,128)(2,1)} %param.26) | copy-start | bytes 147460
  26.8 2.8 %copy-start.6 = (bf16[32,768]{1,0:T(8,128)(2,1)S(1)}, bf16[32,768]{1,0:T(8,128)(2,1)}, u32[]{:S(2)}) copy-start(bf16[32,768]{1,0:T(8,128)(2,1)} %param.25) | copy-start | bytes 147460
  26.8 2.8 %copy-start.7 = (bf16[32,768]{1,0:T(8,128)(2,1)S(1)}, bf16[32,768]{1,0:T(8,128)(2,1)}, u32[]{:S(2)}) copy-start(bf16[32,768]{1,0:T(8,128)(2,1)} %param.24) | copy-start | bytes 147460
  163.5 2.1 copy-start.10
  165.6 46.4 %copy-start.1 = (bf16[256,2048]{1,0:T(8,128)(2,1)}, bf16[256,2048]{1,0:T(8,128)(2,1)S(1)}, u32[]{:S(2)}) copy-start(bf16[256,2048]{1,0:T(8,128)(2,1)S(1)} %get-tuple-element.16.refs_1_) | copy-start | bytes 3145732
Sparse Core Ops, SparseCore 0:
  18.4 103.8 all-gather.4
  125.1 81.8 all-gather.6

commit v14 on v13

--- a/solution.py
+++ b/solution.py
@@ -100,7 +100,7 @@
     rows, width = x.shape
     cols = width // n
     operands = (x,) if base is None else (x, base)
-    parts = 2 if rows % 32 == 0 else 1
+    parts = 4 if rows % 64 == 0 else 1
     return pl.pallas_call(
         functools.partial(tp_sum_kernel, n, parts, base is not None),
         out_shape=jax.ShapeDtypeStruct((rows, width), x.dtype),

time: 255 us -> 256 us (level)
  no operation moved by 1% of the time
where the time goes in v14:
time: 256 us; the launch traced here: 255 us
  waiting for transfers between devices  132 us (52%)
  Pallas kernels  67 us (26%)
  matrix products  19.4 us (8%)
  between operations  17 us (7%)
  other arithmetic  11.9 us (5%)
  local copies, waits for them, and re-layouts  7.57 us (3%)
    all_gather x1, waiting for transfers between devices, body(): kv_gathered = lax.all_gather(kv_packed, 'seq', axis=0, tiled=False)  92.1 us
    pallas_call x2, Pallas kernels, tp_sum(): pl.pallas_call(functools.partial(tp_sum_kernel, n, parts, base is not Non...  59.5 us
    all_gather x1, waiting for transfers between devices, body(): lax.all_gather(weights_packed, 'seq', axis=0, tiled=False)  40 us
    pallas_call x1, Pallas kernels, attention(): pl.pallas_call(attention_kernel, out_shape=jax.ShapeDtypeStruct((rows, ou...  7.45 us
  transfers between devices with their start and end apart: 2, of which 2 were waited for; matrix products, arithmetic and copies ran while one was open for 6% of the time, Pallas kernels for 14%

profile of v14, /device:TPU:1, one launch (start us, length us, event | category | flops | bytes accessed | tf_op | source)
XLA Modules:
  0.0 255.1 jit_solution(2546401606273595768)
XLA Ops:
  7.3 1.6 fusion.10
  8.9 3.0 %multiply_reduce_fusion.1 = (f32[256,2]{0,1:T(2,128)S(1)}, f32[256,256]{0,1:T(8,128)}) fusion(bf16[2048,256]{1,0:T(8,128)(2,1)} %param.17, bf16[256,2048]{1,0:T(8,128)(2,1)} %param.14, f32[2048]{0:T(1024)} %param.15, f32[256]{0:T(256)S(1)} %add_rsqrt_fusion.3), kind=kOutput, calls=%fused_computation.29 | convolution fusion | flops 270663168 | bytes 2370560 | tf_op jit(solution)/shard_map/dot_general | solution.py:243
  13.3 1.0 multiply_multiply_fusion.1
  14.4 0.8 copy.34
  15.1 1.8 convolution_convert_fusion.1
  17.6 0.7 pad_maximum_fusion
  21.6 3.2 %fusion.19 = f32[256,512]{1,0:T(8,128)} fusion(bf16[2048,512]{1,0:T(8,128)(2,1)} %param.16, bf16[256,2048]{1,0:T(8,128)(2,1)S(1)} %copy-done.2, f32[2048]{0:T(1024)} %param.15, f32[256]{0:T(256)S(1)} %add_rsqrt_fusion.3), kind=kOutput, calls=%fused_computation.47 | convolution fusion | flops 538968064 | bytes 3679232 | tf_op jit(solution)/shard_map/dot_general | solution.py:239
  24.8 1.2 reshape.120
  27.4 1.3 pad_add_fusion.info
  28.7 0.8 pad_maximum_fusion.1
  29.6 0.7 pad_maximum_fusion.2
  30.3 92.1 %all-gather.5.cloned.1.call-done = bf16[32768,256]{1,0:T(8,128)(2,1)} async-done(((bf16[512,256]{1,0:T(8,128)(2,1)}), bf16[32768,256]{1,0:T(8,128)(2,1)}) %all-gather.5.cloned.1.call-update) | async-done | bytes 16777232 | tf_op jit(solution)/shard_map/all_gather | solution.py:257
  122.4 0.8 broadcast_in_dim.11.q_first_ref
  123.2 0.8 broadcast_in_dim.9.q_last_ref
  124.1 7.5 %shard_map.148 = bf16[256,512]{1,0:T(8,128)(2,1)} custom-call(s32[4]{0:T(128)} %pad_add_fusion.info, bf16[2,512,128]{2,1,0:T(8,128)(2,1)} %bitcast.28, s32[512,128]{1,0:T(8,128)} %broadcast_in_dim.9.q_last_ref, s32[512,128]{1,0:T(8,128)} %broadcast_in_dim.11.q_first_ref, bf16[64,512,256]{2,1,0:T(8,128)(2,1)} %bitcast.27), custom_call_target="tpu_custom_call" | custom-call | tf_op jit(solution)/shard_map/pallas_call | solution.py:205
  131.6 2.6 %convolution_convert_fusion.refs_0_ = bf16[256,2048]{1,0:T(8,128)(2,1)} fusion(bf16[256,512]{1,0:T(8,128)(2,1)} %shard_map.148, bf16[512,2048]{1,0:T(8,128)(2,1)S(1)} %copy-done), kind=kOutput, calls=%fused_computation.9 | convolution fusion | flops 537395200 | bytes 3407872 | tf_op jit(solution)/shard_map/dot_general | solution.py:286
  134.2 29.5 %shard_map.149 = bf16[256,2048]{1,0:T(8,128)(2,1)} custom-call(bf16[256,2048]{1,0:T(8,128)(2,1)} %convolution_convert_fusion.refs_0_), custom_call_target="tpu_custom_call" | custom-call | tf_op jit(solution)/shard_map/pallas_call | solution.py:104
  163.7 2.1 fusion.7
  165.8 1.3 fusion.9
  167.1 40.0 %all-gather.7.cloned.1.call-done = bf16[2048,2304]{1,0:T(8,128)(2,1)} async-done(((bf16[32,2304]{1,0:T(8,128)(2,1)}), bf16[2048,2304]{1,0:T(8,128)(2,1)}) %all-gather.7.cloned.1.call-update) | async-done | bytes 9437200 | tf_op jit(solution)/shard_map/all_gather | solution.py:282
  207.1 4.9 %fusion = f32[256,1536]{1,0:T(8,128)S(1)} fusion(bf16[256,2048]{1,0:T(8,128)(2,1)} %fusion.9, bf16[2048,2304]{1,0:T(8,128)(2,1)} %all-gather.7.cloned.1.call-done), kind=kOutput, calls=%fused_computation | convolution fusion | flops 1610612736 | bytes 8912896 | tf_op jit(solution)/shard_map/dot_general | solution.py:291
  212.0 3.9 %fusion.4.refs_0_ = bf16[256,2048]{1,0:T(8,128)(2,1)} fusion(bf16[2048,2304]{1,0:T(8,128)(2,1)} %all-gather.7.cloned.1.call-done, f32[256,1536]{1,0:T(8,128)S(1)} %fusion), kind=kOutput, calls=%fused_computation.10 | convolution fusion | flops 807010304 | bytes 5767168 | tf_op jit(solution)/shard_map/dot_general | solution.py:293
  215.9 30.0 %shard_map.150 = bf16[256,2048]{1,0:T(8,128)(2,1)} custom-call(bf16[256,2048]{1,0:T(8,128)(2,1)} %fusion.4.refs_0_, bf16[256,2048]{1,0:T(8,128)(2,1)} %copy-done.1), custom_call_target="tpu_custom_call" | custom-call | tf_op jit(solution)/shard_map/pallas_call | solution.py:104
  245.9 2.3 copy.39
  (55 shorter events, 4.1 us)
Async XLA Ops:
  7.2 124.4 %copy-start = (bf16[512,2048]{1,0:T(8,128)(2,1)S(1)}, bf16[512,2048]{1,0:T(8,128)(2,1)}, u32[]{:S(2)}) copy-start(bf16[512,2048]{1,0:T(8,128)(2,1)} %param.19) | copy-start | bytes 6291460
  7.2 4.8 %copy-start.12 = (s32[256]{0:T(256)S(1)}, s32[256]{0:T(256)}, u32[]{:S(2)}) copy-start(s32[256]{0:T(256)} %param.22) | copy-start | bytes 3076
  7.2 115.2 %all-gather.5.cloned.1.call-start = ((), (), s32[]{:S(2)}) async-start(), calls=%async_computation | async-start | bytes 17039360 | tf_op jit(solution)/shard_map/all_gather | solution.py:257
  8.9 4.4 %copy-start.13 = (f32[128]{0:T(128)S(1)}, f32[128]{0:T(128)}, u32[]{:S(2)}) copy-start(f32[128]{0:T(128)} %param.21) | copy-start | bytes 1540
  8.9 6.2 %copy-start.2 = (bf16[256,2048]{1,0:T(8,128)(2,1)S(1)}, bf16[256,2048]{1,0:T(8,128)(2,1)}, u32[]{:S(2)}) copy-start(bf16[256,2048]{1,0:T(8,128)(2,1)} %param.14) | copy-start | bytes 3145732
  12.6 5.8 %copy-start.8 = (s32[256]{0:T(256)}, s32[256]{0:T(256)S(1)}, u32[]{:S(2)}) copy-start(s32[256]{0:T(256)S(1)} %get-tuple-element.25) | copy-start | bytes 3076
  15.1 2.4 copy-start.3
  16.9 0.7 copy-start.4
  18.3 188.7 %all-gather.7.cloned.1.call-start = ((), (), s32[]{:S(2)}) async-start(), calls=%async_computation.1 | async-start | bytes 9584640 | tf_op jit(solution)/shard_map/all_gather | solution.py:282
  21.6 4.8 %copy-start.14 = (f32[128]{0:T(128)S(1)}, f32[128]{0:T(128)}, u32[]{:S(2)}) copy-start(f32[128]{0:T(128)} %param.20) | copy-start | bytes 1540
  26.4 1.0 copy-start.9
  26.4 1.0 copy-start.11
  26.8 2.8 %copy-start.5 = (bf16[768,32]{0,1:T(8,128)(2,1)S(1)}, bf16[768,32]{0,1:T(8,128)(2,1)}, u32[]{:S(2)}) copy-start(bf16[768,32]{0,1:T(8,128)(2,1)} %param.26) | copy-start | bytes 147460
  26.8 2.8 %copy-start.6 = (bf16[32,768]{1,0:T(8,128)(2,1)S(1)}, bf16[32,768]{1,0:T(8,128)(2,1)}, u32[]{:S(2)}) copy-start(bf16[32,768]{1,0:T(8,128)(2,1)} %param.25) | copy-start | bytes 147460
  26.8 2.8 %copy-start.7 = (bf16[32,768]{1,0:T(8,128)(2,1)S(1)}, bf16[32,768]{1,0:T(8,128)(2,1)}, u32[]{:S(2)}) copy-start(bf16[32,768]{1,0:T(8,128)(2,1)} %param.24) | copy-start | bytes 147460
  163.7 2.1 copy-start.10
  165.7 46.2 %copy-start.1 = (bf16[256,2048]{1,0:T(8,128)(2,1)}, bf16[256,2048]{1,0:T(8,128)(2,1)S(1)}, u32[]{:S(2)}) copy-start(bf16[256,2048]{1,0:T(8,128)(2,1)S(1)} %get-tuple-element.16.refs_1_) | copy-start | bytes 3145732
Sparse Core Ops, SparseCore 0:
  18.4 103.8 all-gather.4
  125.1 81.8 all-gather.6

commit v15 on v13

--- a/solution.py
+++ b/solution.py
@@ -276,8 +276,8 @@
     lanes = 128
     q_last = jnp.broadcast_to(jnp.tile(q_index, head_group)[:, None], (head_group * rows, lanes))
     q_first = jnp.broadcast_to(jnp.tile(q_start, head_group)[:, None], (head_group * rows, lanes))
-    kv_gathered, weights_packed, q_grouped, q_last, q_first, info = lax.optimization_barrier(
-        (kv_gathered, weights_packed, q_grouped, q_last, q_first, info)
+    weights_packed, q_grouped, q_last, q_first, info = lax.optimization_barrier(
+        (weights_packed, q_grouped, q_last, q_first, info)
     )
     w_gathered = lax.all_gather(weights_packed, "seq", axis=0, tiled=False).reshape(
         shards * ff_rows, weights_packed.shape[1]

time: 255 us -> 253 us (level)
  transfers between devices with their start and end apart: 2 -> 2, of which waited for: 2 -> 2; matrix products, arithmetic and copies ran while one was open for 6% -> 7% of each run, Pallas kernels for 14% -> 15%
where the time goes in v15:
time: 253 us
  waiting for transfers between devices  132 us (52%)
  Pallas kernels  66.7 us (26%)
  matrix products  18.7 us (7%)
  between operations  17 us (7%)
  other arithmetic  11.9 us (5%)
  local copies, waits for them, and re-layouts  6.28 us (2%)
    all_gather x1, waiting for transfers between devices, body(): kv_gathered = lax.all_gather(kv_packed, 'seq', axis=0, tiled=False)  90.3 us
    pallas_call x2, Pallas kernels, tp_sum(): pl.pallas_call(functools.partial(tp_sum_kernel, n, parts, base is not Non...  59.2 us
    all_gather x1, waiting for transfers between devices, body(): lax.all_gather(weights_packed, 'seq', axis=0, tiled=False)  41.9 us
    pallas_call x1, Pallas kernels, attention(): pl.pallas_call(attention_kernel, out_shape=jax.ShapeDtypeStruct((rows, ou...  7.45 us
  transfers between devices with their start and end apart: 2, of which 2 were waited for; matrix products, arithmetic and copies ran while one was open for 7% of the time, Pallas kernels for 15%

profile of v15, /device:TPU:1, one launch (start us, length us, event | category | flops | bytes accessed | tf_op | source)
XLA Modules:
  0.0 252.8 jit_solution(2451672476509417340)
XLA Ops:
  7.8 1.6 fusion.10
  9.4 2.3 multiply_reduce_fusion.1
  11.7 1.0 multiply_cosine_fusion
  12.7 0.7 multiply_multiply_fusion.1
  13.6 1.8 convolution_convert_fusion.1
  15.4 0.7 pad_maximum_fusion.1
  19.7 3.2 %fusion.22 = f32[256,512]{1,0:T(8,128)} fusion(bf16[2048,512]{1,0:T(8,128)(2,1)} %param.16, bf16[256,2048]{1,0:T(8,128)(2,1)S(1)} %copy-done.2, f32[2048]{0:T(1024)} %param.15, f32[256]{0:T(256)S(1)} %add_rsqrt_fusion.3), kind=kOutput, calls=%fused_computation.48 | convolution fusion | flops 538968064 | bytes 3679232 | tf_op jit(solution)/shard_map/dot_general | solution.py:239
  22.9 1.2 reshape.119
  25.5 1.2 pad_add_fusion.info
  26.7 0.8 pad_maximum_fusion
  27.6 0.7 pad_maximum_fusion.2
  28.2 0.8 broadcast_in_dim.11.q_first_ref
  29.1 0.9 broadcast_in_dim.9.q_last_ref
  29.9 90.3 %all-gather.5.cloned.1.call-done = bf16[32768,256]{1,0:T(8,128)(2,1)} async-done(((bf16[512,256]{1,0:T(8,128)(2,1)}), bf16[32768,256]{1,0:T(8,128)(2,1)}) %all-gather.5.cloned.1.call-update) | async-done | bytes 16777232 | tf_op jit(solution)/shard_map/all_gather | solution.py:257
  120.2 7.5 %shard_map.148 = bf16[256,512]{1,0:T(8,128)(2,1)} custom-call(s32[4]{0:T(128)} %pad_add_fusion.info, bf16[2,512,128]{2,1,0:T(8,128)(2,1)} %bitcast.28, s32[512,128]{1,0:T(8,128)} %broadcast_in_dim.9.q_last_ref, s32[512,128]{1,0:T(8,128)} %broadcast_in_dim.11.q_first_ref, bf16[64,512,256]{2,1,0:T(8,128)(2,1)} %bitcast.27), custom_call_target="tpu_custom_call" | custom-call | tf_op jit(solution)/shard_map/pallas_call | solution.py:205
  127.7 2.6 %convolution_convert_fusion.refs_0_ = bf16[256,2048]{1,0:T(8,128)(2,1)} fusion(bf16[256,512]{1,0:T(8,128)(2,1)} %shard_map.148, bf16[512,2048]{1,0:T(8,128)(2,1)S(1)} %copy-done), kind=kOutput, calls=%fused_computation.9 | convolution fusion | flops 537395200 | bytes 3407872 | tf_op jit(solution)/shard_map/dot_general | solution.py:286
  130.3 29.3 %shard_map.149 = bf16[256,2048]{1,0:T(8,128)(2,1)} custom-call(bf16[256,2048]{1,0:T(8,128)(2,1)} %convolution_convert_fusion.refs_0_), custom_call_target="tpu_custom_call" | custom-call | tf_op jit(solution)/shard_map/pallas_call | solution.py:104
  159.7 2.1 fusion.7
  161.8 1.3 fusion.9
  163.0 41.9 %all-gather.7.cloned.1.call-done = bf16[2048,2304]{1,0:T(8,128)(2,1)} async-done(((bf16[32,2304]{1,0:T(8,128)(2,1)}), bf16[2048,2304]{1,0:T(8,128)(2,1)}) %all-gather.7.cloned.1.call-update) | async-done | bytes 9437200 | tf_op jit(solution)/shard_map/all_gather | solution.py:282
  204.9 4.9 %fusion = f32[256,1536]{1,0:T(8,128)S(1)} fusion(bf16[256,2048]{1,0:T(8,128)(2,1)} %fusion.9, bf16[2048,2304]{1,0:T(8,128)(2,1)} %all-gather.7.cloned.1.call-done), kind=kOutput, calls=%fused_computation | convolution fusion | flops 1610612736 | bytes 8912896 | tf_op jit(solution)/shard_map/dot_general | solution.py:291
  209.8 3.9 %fusion.4.refs_0_ = bf16[256,2048]{1,0:T(8,128)(2,1)} fusion(bf16[2048,2304]{1,0:T(8,128)(2,1)} %all-gather.7.cloned.1.call-done, f32[256,1536]{1,0:T(8,128)S(1)} %fusion), kind=kOutput, calls=%fused_computation.10 | convolution fusion | flops 807010304 | bytes 5767168 | tf_op jit(solution)/shard_map/dot_general | solution.py:293
  213.7 29.9 %shard_map.150 = bf16[256,2048]{1,0:T(8,128)(2,1)} custom-call(bf16[256,2048]{1,0:T(8,128)(2,1)} %fusion.4.refs_0_, bf16[256,2048]{1,0:T(8,128)(2,1)} %copy-done.1), custom_call_target="tpu_custom_call" | custom-call | tf_op jit(solution)/shard_map/pallas_call | solution.py:104
  243.6 2.3 copy.39
  (47 shorter events, 3.0 us)
Async XLA Ops:
  7.2 120.5 %copy-start = (bf16[512,2048]{1,0:T(8,128)(2,1)S(1)}, bf16[512,2048]{1,0:T(8,128)(2,1)}, u32[]{:S(2)}) copy-start(bf16[512,2048]{1,0:T(8,128)(2,1)} %param.19) | copy-start | bytes 6291460
  7.2 4.5 %copy-start.9 = (s32[256]{0:T(256)S(1)}, s32[256]{0:T(256)}, u32[]{:S(2)}) copy-start(s32[256]{0:T(256)} %param.22) | copy-start | bytes 3076
  7.2 113.1 %all-gather.5.cloned.1.call-start = ((), (), s32[]{:S(2)}) async-start(), calls=%async_computation | async-start | bytes 17039360 | tf_op jit(solution)/shard_map/all_gather | solution.py:257
  9.3 4.3 %copy-start.2 = (bf16[256,2048]{1,0:T(8,128)(2,1)S(1)}, bf16[256,2048]{1,0:T(8,128)(2,1)}, u32[]{:S(2)}) copy-start(bf16[256,2048]{1,0:T(8,128)(2,1)} %param.14) | copy-start | bytes 3145732
  13.6 5.9 %copy-start.3 = (bf16[256,256]{1,0:T(8,128)(2,1)}, bf16[256,256]{1,0:T(8,128)(2,1)S(1)}, u32[]{:S(2)}) copy-start(bf16[256,256]{1,0:T(8,128)(2,1)S(1)} %copy.34) | copy-start | bytes 393220
  15.4 4.1 %copy-start.4 = (bf16[256,256]{1,0:T(8,128)(2,1)}, bf16[256,256]{1,0:T(8,128)(2,1)S(1)}, u32[]{:S(2)}) copy-start(bf16[256,256]{1,0:T(8,128)(2,1)S(1)} %convolution_convert_fusion.1) | copy-start | bytes 393220
  16.2 188.7 %all-gather.7.cloned.1.call-start = ((), (), s32[]{:S(2)}) async-start(), calls=%async_computation.1 | async-start | bytes 9584640 | tf_op jit(solution)/shard_map/all_gather | solution.py:282
  19.7 4.8 %copy-start.10 = (f32[128]{0:T(128)S(1)}, f32[128]{0:T(128)}, u32[]{:S(2)}) copy-start(f32[128]{0:T(128)} %param.20) | copy-start | bytes 1540
  24.8 2.7 %copy-start.5 = (bf16[768,32]{0,1:T(8,128)(2,1)S(1)}, bf16[768,32]{0,1:T(8,128)(2,1)}, u32[]{:S(2)}) copy-start(bf16[768,32]{0,1:T(8,128)(2,1)} %param.26) | copy-start | bytes 147460
  24.8 2.7 %copy-start.6 = (bf16[32,768]{1,0:T(8,128)(2,1)S(1)}, bf16[32,768]{1,0:T(8,128)(2,1)}, u32[]{:S(2)}) copy-start(bf16[32,768]{1,0:T(8,128)(2,1)} %param.25) | copy-start | bytes 147460
  24.8 2.7 %copy-start.7 = (bf16[32,768]{1,0:T(8,128)(2,1)S(1)}, bf16[32,768]{1,0:T(8,128)(2,1)}, u32[]{:S(2)}) copy-start(bf16[32,768]{1,0:T(8,128)(2,1)} %param.24) | copy-start | bytes 147460
  159.7 2.1 copy-start.8
  161.7 48.1 %copy-start.1 = (bf16[256,2048]{1,0:T(8,128)(2,1)}, bf16[256,2048]{1,0:T(8,128)(2,1)S(1)}, u32[]{:S(2)}) copy-start(bf16[256,2048]{1,0:T(8,128)(2,1)S(1)} %get-tuple-element.14.refs_1_) | copy-start | bytes 3145732
Sparse Core Ops, SparseCore 0:
  16.3 103.9 all-gather.4
  123.0 81.8 all-gather.6

commit v16 on v15

--- a/solution.py
+++ b/solution.py
@@ -240,14 +240,15 @@
         rows, query_local, head_size
     )
     query_matrix = rope(rms(query_matrix, query_gain), positions).astype(jnp.bfloat16)
-    key_matrix = jnp.dot(normed_input, key_weight, preferred_element_type=jnp.float32).reshape(
-        rows, kv_local, head_size
-    )
+    key_value = jnp.dot(
+        normed_input,
+        jnp.concatenate([key_weight, value_weight], axis=1),
+        preferred_element_type=jnp.float32,
+    )
+    key_matrix = key_value[:, :kv_cols].reshape(rows, kv_local, head_size)
     key_matrix = rope(rms(key_matrix, key_gain), positions).astype(jnp.bfloat16)
     key_cache = key_matrix.reshape(rows, kv_cols)
-    value_cache = jnp.dot(normed_input, value_weight, preferred_element_type=jnp.float32).astype(
-        jnp.bfloat16
-    )
+    value_cache = key_value[:, kv_cols:].astype(jnp.bfloat16)
 
     width_all = 2 * kv_cols
     ff_rows, ff_local = w_gate.shape

time: 253 us -> 255 us (level)
  other arithmetic: 11.9 us -> 14.5 us
  transfers between devices with their start and end apart: 2 -> 2, of which waited for: 2 -> 2; matrix products, arithmetic and copies ran while one was open for 7% -> 7% of each run, Pallas kernels for 15% -> 14%
where the time goes in v16:
time: 255 us
  waiting for transfers between devices  132 us (52%)
  Pallas kernels  66.7 us (26%)
  matrix products  17.2 us (7%)
  between operations  17 us (7%)
  other arithmetic  14.5 us (6%)
  local copies, waits for them, and re-layouts  6.87 us (3%)
    all_gather x1, waiting for transfers between devices, body(): kv_gathered = lax.all_gather(kv_packed, 'seq', axis=0, tiled=False)  90.4 us
    pallas_call x2, Pallas kernels, tp_sum(): pl.pallas_call(functools.partial(tp_sum_kernel, n, parts, base is not Non...  59.2 us
    all_gather x1, waiting for transfers between devices, body(): lax.all_gather(weights_packed, 'seq', axis=0, tiled=False)  41.9 us
    pallas_call x1, Pallas kernels, attention(): pl.pallas_call(attention_kernel, out_shape=jax.ShapeDtypeStruct((rows, ou...  7.45 us
  transfers between devices with their start and end apart: 2, of which 2 were waited for; matrix products, arithmetic and copies ran while one was open for 7% of the time, Pallas kernels for 14%

profile of v16, /device:TPU:1, one launch (start us, length us, event | category | flops | bytes accessed | tf_op | source)
XLA Modules:
  0.0 254.7 jit_solution(2919640821700838689)
XLA Ops:
  7.8 1.6 fusion.10
  9.3 2.6 %fusion.14 = f32[256,512]{1,0:T(8,128)S(1)} fusion(bf16[2048,256]{1,0:T(8,128)(2,1)} %param.18, bf16[2048,256]{1,0:T(8,128)(2,1)} %param.17, bf16[256,2048]{1,0:T(8,128)(2,1)} %param.14, f32[2048]{0:T(1024)} %param.15, f32[256]{0:T(256)S(1)} %add_rsqrt_fusion.3), kind=kOutput, calls=%fused_computation.18 | convolution fusion | flops 543162368 | bytes 3679232 | tf_op jit(solution)/shard_map/dot_general | solution.py:243
  13.2 0.7 add_rsqrt_fusion
  13.9 1.2 multiply_cosine_fusion
  15.1 1.3 multiply_multiply_fusion.1
  17.3 0.7 pad_maximum_fusion.1
  21.4 3.2 %fusion.22 = f32[256,512]{1,0:T(8,128)} fusion(bf16[2048,512]{1,0:T(8,128)(2,1)} %param.16, bf16[256,2048]{1,0:T(8,128)(2,1)S(1)} %copy-done.2, f32[2048]{0:T(1024)} %param.15, f32[256]{0:T(256)S(1)} %add_rsqrt_fusion.3), kind=kOutput, calls=%fused_computation.29 | convolution fusion | flops 538968064 | bytes 3679232 | tf_op jit(solution)/shard_map/dot_general | solution.py:239
  24.6 1.2 reshape.119
  27.2 1.2 pad_add_fusion.info
  28.5 0.8 pad_maximum_fusion
  29.3 0.7 pad_maximum_fusion.2
  30.0 0.8 broadcast_in_dim.11.q_first_ref
  30.8 0.8 broadcast_in_dim.9.q_last_ref
  31.7 90.4 %all-gather.5.cloned.1.call-done = bf16[32768,256]{1,0:T(8,128)(2,1)} async-done(((bf16[512,256]{1,0:T(8,128)(2,1)}), bf16[32768,256]{1,0:T(8,128)(2,1)}) %all-gather.5.cloned.1.call-update) | async-done | bytes 16777232 | tf_op jit(solution)/shard_map/all_gather | solution.py:258
  122.1 7.5 %shard_map.148 = bf16[256,512]{1,0:T(8,128)(2,1)} custom-call(s32[4]{0:T(128)} %pad_add_fusion.info, bf16[2,512,128]{2,1,0:T(8,128)(2,1)} %bitcast.26, s32[512,128]{1,0:T(8,128)} %broadcast_in_dim.9.q_last_ref, s32[512,128]{1,0:T(8,128)} %broadcast_in_dim.11.q_first_ref, bf16[64,512,256]{2,1,0:T(8,128)(2,1)} %bitcast.25), custom_call_target="tpu_custom_call" | custom-call | tf_op jit(solution)/shard_map/pallas_call | solution.py:205
  129.6 2.6 %convolution_convert_fusion.refs_0_ = bf16[256,2048]{1,0:T(8,128)(2,1)} fusion(bf16[256,512]{1,0:T(8,128)(2,1)} %shard_map.148, bf16[512,2048]{1,0:T(8,128)(2,1)S(1)} %copy-done), kind=kOutput, calls=%fused_computation.9 | convolution fusion | flops 537395200 | bytes 3407872 | tf_op jit(solution)/shard_map/dot_general | solution.py:287
  132.2 29.3 %shard_map.149 = bf16[256,2048]{1,0:T(8,128)(2,1)} custom-call(bf16[256,2048]{1,0:T(8,128)(2,1)} %convolution_convert_fusion.refs_0_), custom_call_target="tpu_custom_call" | custom-call | tf_op jit(solution)/shard_map/pallas_call | solution.py:104
  161.6 2.1 fusion.7
  163.6 1.3 fusion.9
  164.9 41.9 %all-gather.7.cloned.1.call-done = bf16[2048,2304]{1,0:T(8,128)(2,1)} async-done(((bf16[32,2304]{1,0:T(8,128)(2,1)}), bf16[2048,2304]{1,0:T(8,128)(2,1)}) %all-gather.7.cloned.1.call-update) | async-done | bytes 9437200 | tf_op jit(solution)/shard_map/all_gather | solution.py:283
  206.8 4.9 %fusion = f32[256,1536]{1,0:T(8,128)S(1)} fusion(bf16[256,2048]{1,0:T(8,128)(2,1)} %fusion.9, bf16[2048,2304]{1,0:T(8,128)(2,1)} %all-gather.7.cloned.1.call-done), kind=kOutput, calls=%fused_computation | convolution fusion | flops 1610612736 | bytes 8912896 | tf_op jit(solution)/shard_map/dot_general | solution.py:292
  211.7 3.9 %fusion.4.refs_0_ = bf16[256,2048]{1,0:T(8,128)(2,1)} fusion(bf16[2048,2304]{1,0:T(8,128)(2,1)} %all-gather.7.cloned.1.call-done, f32[256,1536]{1,0:T(8,128)S(1)} %fusion), kind=kOutput, calls=%fused_computation.10 | convolution fusion | flops 807010304 | bytes 5767168 | tf_op jit(solution)/shard_map/dot_general | solution.py:294
  215.6 29.9 %shard_map.150 = bf16[256,2048]{1,0:T(8,128)(2,1)} custom-call(bf16[256,2048]{1,0:T(8,128)(2,1)} %fusion.4.refs_0_, bf16[256,2048]{1,0:T(8,128)(2,1)} %copy-done.1), custom_call_target="tpu_custom_call" | custom-call | tf_op jit(solution)/shard_map/pallas_call | solution.py:104
  245.5 2.3 copy.36
  (52 shorter events, 4.7 us)
Async XLA Ops:
  7.2 122.4 %copy-start = (bf16[512,2048]{1,0:T(8,128)(2,1)S(1)}, bf16[512,2048]{1,0:T(8,128)(2,1)}, u32[]{:S(2)}) copy-start(bf16[512,2048]{1,0:T(8,128)(2,1)} %param.19) | copy-start | bytes 6291460
  7.2 115.0 %all-gather.5.cloned.1.call-start = ((), (), s32[]{:S(2)}) async-start(), calls=%async_computation | async-start | bytes 17039360 | tf_op jit(solution)/shard_map/all_gather | solution.py:258
  9.3 4.5 %copy-start.11 = (s32[256]{0:T(256)S(1)}, s32[256]{0:T(256)}, u32[]{:S(2)}) copy-start(s32[256]{0:T(256)} %param.22) | copy-start | bytes 3076
  12.8 8.6 %copy-start.2 = (bf16[256,2048]{1,0:T(8,128)(2,1)S(1)}, bf16[256,2048]{1,0:T(8,128)(2,1)}, u32[]{:S(2)}) copy-start(bf16[256,2048]{1,0:T(8,128)(2,1)} %param.14) | copy-start | bytes 3145732
  13.9 3.5 %copy-start.5 = (bf16[256,256]{1,0:T(8,128)(2,1)S(1)}, bf16[256,256]{1,0:T(8,128)(2,1)}, u32[]{:S(2)}) copy-start(bf16[256,256]{1,0:T(8,128)(2,1)} %slice.80) | copy-start | bytes 393220
  15.1 1.8 copy-start.3
  17.3 7.3 %copy-start.6 = (bf16[32,8,2,128]{3,1,2,0:T(8,128)(2,1)}, bf16[32,8,2,128]{3,1,2,0:T(8,128)(2,1)S(1)}, u32[]{:S(2)}) copy-start(bf16[32,8,2,128]{3,1,2,0:T(8,128)(2,1)S(1)} %copy.34) | copy-start | bytes 393220
  18.1 188.7 %all-gather.7.cloned.1.call-start = ((), (), s32[]{:S(2)}) async-start(), calls=%async_computation.1 | async-start | bytes 9584640 | tf_op jit(solution)/shard_map/all_gather | solution.py:283
  21.4 4.8 %copy-start.12 = (f32[128]{0:T(128)S(1)}, f32[128]{0:T(128)}, u32[]{:S(2)}) copy-start(f32[128]{0:T(128)} %param.20) | copy-start | bytes 1540
  24.6 2.0 copy-start.4
  26.6 2.8 %copy-start.7 = (bf16[768,32]{0,1:T(8,128)(2,1)S(1)}, bf16[768,32]{0,1:T(8,128)(2,1)}, u32[]{:S(2)}) copy-start(bf16[768,32]{0,1:T(8,128)(2,1)} %param.26) | copy-start | bytes 147460
  26.6 2.8 %copy-start.8 = (bf16[32,768]{1,0:T(8,128)(2,1)S(1)}, bf16[32,768]{1,0:T(8,128)(2,1)}, u32[]{:S(2)}) copy-start(bf16[32,768]{1,0:T(8,128)(2,1)} %param.25) | copy-start | bytes 147460
  26.6 2.7 %copy-start.9 = (bf16[32,768]{1,0:T(8,128)(2,1)S(1)}, bf16[32,768]{1,0:T(8,128)(2,1)}, u32[]{:S(2)}) copy-start(bf16[32,768]{1,0:T(8,128)(2,1)} %param.24) | copy-start | bytes 147460
  161.5 2.1 copy-start.10
  163.6 48.1 %copy-start.1 = (bf16[256,2048]{1,0:T(8,128)(2,1)}, bf16[256,2048]{1,0:T(8,128)(2,1)S(1)}, u32[]{:S(2)}) copy-start(bf16[256,2048]{1,0:T(8,128)(2,1)S(1)} %get-tuple-element.14.refs_1_) | copy-start | bytes 3145732
Sparse Core Ops, SparseCore 0:
  18.2 103.9 all-gather.4
  124.9 81.8 all-gather.6

commit v17 on v15

--- a/solution.py
+++ b/solution.py
@@ -284,8 +284,7 @@
     )
     attended = attention(q_grouped, q_last, q_first, kv_gathered, info, rows, 2 * rows, shards_per)
     partial_out = jnp.dot(attended, w_out, preferred_element_type=jnp.float32)
-    summed = tp_sum(partial_out.astype(jnp.bfloat16), 0).astype(jnp.float32)
-    mid = (xf + summed).astype(jnp.bfloat16)
+    mid = tp_sum(partial_out.astype(jnp.bfloat16), 0, layer_input)
     mid_f = mid.astype(jnp.float32)
     post_normed = lax.optimization_barrier(rms(mid_f, post_gain).astype(jnp.bfloat16))
     gate_up = jnp.dot(post_normed, w_gathered[:, : 2 * ff_local], preferred_element_type=jnp.float32)

time: 253 us -> 253 us (level)
  no operation moved by 1% of the time
where the time goes in v17:
time: 253 us; the launch traced here: 252 us
  waiting for transfers between devices  132 us (52%)
  Pallas kernels  67.2 us (27%)
  matrix products  18.3 us (7%)
  between operations  17 us (7%)
  other arithmetic  11.6 us (5%)
  local copies, waits for them, and re-layouts  6.28 us (2%)
    all_gather x1, waiting for transfers between devices, body(): kv_gathered = lax.all_gather(kv_packed, 'seq', axis=0, tiled=False)  90.2 us
    pallas_call x2, Pallas kernels, tp_sum(): pl.pallas_call(functools.partial(tp_sum_kernel, n, parts, base is not Non...  59.7 us
    all_gather x1, waiting for transfers between devices, body(): lax.all_gather(weights_packed, 'seq', axis=0, tiled=False)  41.7 us
    pallas_call x1, Pallas kernels, attention(): pl.pallas_call(attention_kernel, out_shape=jax.ShapeDtypeStruct((rows, ou...  7.45 us
  transfers between devices with their start and end apart: 2, of which 2 were waited for; matrix products, arithmetic and copies ran while one was open for 7% of the time, Pallas kernels for 15%

profile of v17, /device:TPU:1, one launch (start us, length us, event | category | flops | bytes accessed | tf_op | source)
XLA Modules:
  0.0 252.4 jit_solution(10751718641841386813)
XLA Ops:
  7.8 1.6 fusion.7
  9.4 2.3 multiply_reduce_fusion.1
  11.7 1.0 multiply_cosine_fusion
  12.7 0.7 multiply_multiply_fusion.1
  13.6 1.8 convolution_convert_fusion.1
  15.4 0.7 pad_maximum_fusion.1
  16.2 0.7 fusion.23
  19.7 3.2 %fusion.21 = f32[256,512]{1,0:T(8,128)} fusion(bf16[2048,512]{1,0:T(8,128)(2,1)} %param.16, bf16[256,2048]{1,0:T(8,128)(2,1)S(1)} %copy-done.1, f32[2048]{0:T(1024)} %param.15, f32[256]{0:T(256)S(1)} %add_rsqrt_fusion.3), kind=kOutput, calls=%fused_computation.46 | convolution fusion | flops 538968064 | bytes 3679232 | tf_op jit(solution)/shard_map/dot_general | solution.py:239
  22.9 1.2 reshape.119
  25.5 1.3 pad_add_fusion.info
  26.8 0.8 pad_maximum_fusion
  28.3 0.8 broadcast_in_dim.11.q_first_ref
  29.1 0.8 broadcast_in_dim.9.q_last_ref
  30.0 90.2 %all-gather.5.cloned.1.call-done = bf16[32768,256]{1,0:T(8,128)(2,1)} async-done(((bf16[512,256]{1,0:T(8,128)(2,1)}), bf16[32768,256]{1,0:T(8,128)(2,1)}) %all-gather.5.cloned.1.call-update) | async-done | bytes 16777232 | tf_op jit(solution)/shard_map/all_gather | solution.py:257
  120.2 7.4 %shard_map.148 = bf16[256,512]{1,0:T(8,128)(2,1)} custom-call(s32[4]{0:T(128)} %pad_add_fusion.info, bf16[2,512,128]{2,1,0:T(8,128)(2,1)} %bitcast.28, s32[512,128]{1,0:T(8,128)} %broadcast_in_dim.9.q_last_ref, s32[512,128]{1,0:T(8,128)} %broadcast_in_dim.11.q_first_ref, bf16[64,512,256]{2,1,0:T(8,128)(2,1)} %bitcast.27), custom_call_target="tpu_custom_call" | custom-call | tf_op jit(solution)/shard_map/pallas_call | solution.py:205
  127.7 2.6 %convolution_convert_fusion.refs_0_ = bf16[256,2048]{1,0:T(8,128)(2,1)} fusion(bf16[256,512]{1,0:T(8,128)(2,1)} %shard_map.148, bf16[512,2048]{1,0:T(8,128)(2,1)S(1)} %copy-done), kind=kOutput, calls=%fused_computation.8 | convolution fusion | flops 537395200 | bytes 3407872 | tf_op jit(solution)/shard_map/dot_general | solution.py:286
  130.3 29.8 %shard_map.149.refs_1_ = bf16[256,2048]{1,0:T(8,128)(2,1)} custom-call(bf16[256,2048]{1,0:T(8,128)(2,1)} %convolution_convert_fusion.refs_0_, bf16[256,2048]{1,0:T(8,128)(2,1)} %refs_1_.1), custom_call_target="tpu_custom_call" | custom-call | tf_op jit(solution)/shard_map/pallas_call | solution.py:104
  160.1 1.5 fusion.10
  161.7 1.5 fusion.12
  163.2 41.7 %all-gather.7.cloned.1.call-done = bf16[2048,2304]{1,0:T(8,128)(2,1)} async-done(((bf16[32,2304]{1,0:T(8,128)(2,1)}), bf16[2048,2304]{1,0:T(8,128)(2,1)}) %all-gather.7.cloned.1.call-update) | async-done | bytes 9437200 | tf_op jit(solution)/shard_map/all_gather | solution.py:282
  204.9 4.6 %fusion = f32[256,1536]{1,0:T(8,128)S(1)} fusion(bf16[256,2048]{1,0:T(8,128)(2,1)S(1)} %fusion.12, bf16[2048,2304]{1,0:T(8,128)(2,1)} %all-gather.7.cloned.1.call-done), kind=kOutput, calls=%fused_computation | convolution fusion | flops 1610612736 | bytes 8912896 | tf_op jit(solution)/shard_map/dot_general | solution.py:290
  209.5 3.9 %fusion.4.refs_0_ = bf16[256,2048]{1,0:T(8,128)(2,1)} fusion(bf16[2048,2304]{1,0:T(8,128)(2,1)} %all-gather.7.cloned.1.call-done, f32[256,1536]{1,0:T(8,128)S(1)} %fusion), kind=kOutput, calls=%fused_computation.9 | convolution fusion | flops 807010304 | bytes 5767168 | tf_op jit(solution)/shard_map/dot_general | solution.py:292
  213.4 29.9 %shard_map.150 = bf16[256,2048]{1,0:T(8,128)(2,1)} custom-call(bf16[256,2048]{1,0:T(8,128)(2,1)} %fusion.4.refs_0_, bf16[256,2048]{1,0:T(8,128)(2,1)} %shard_map.149.refs_1_), custom_call_target="tpu_custom_call" | custom-call | tf_op jit(solution)/shard_map/pallas_call | solution.py:104
  243.3 2.3 copy.39
  (45 shorter events, 3.0 us)
Async XLA Ops:
  7.2 120.5 %copy-start = (bf16[512,2048]{1,0:T(8,128)(2,1)S(1)}, bf16[512,2048]{1,0:T(8,128)(2,1)}, u32[]{:S(2)}) copy-start(bf16[512,2048]{1,0:T(8,128)(2,1)} %param.19) | copy-start | bytes 6291460
  7.2 4.5 %copy-start.8 = (s32[256]{0:T(256)S(1)}, s32[256]{0:T(256)}, u32[]{:S(2)}) copy-start(s32[256]{0:T(256)} %param.22) | copy-start | bytes 3076
  7.2 113.0 %all-gather.5.cloned.1.call-start = ((), (), s32[]{:S(2)}) async-start(), calls=%async_computation | async-start | bytes 17039360 | tf_op jit(solution)/shard_map/all_gather | solution.py:257
  9.3 4.3 %copy-start.1 = (bf16[256,2048]{1,0:T(8,128)(2,1)S(1)}, bf16[256,2048]{1,0:T(8,128)(2,1)}, u32[]{:S(2)}) copy-start(bf16[256,2048]{1,0:T(8,128)(2,1)} %refs_1_.1) | copy-start | bytes 3145732
  13.6 5.9 %copy-start.2 = (bf16[256,256]{1,0:T(8,128)(2,1)}, bf16[256,256]{1,0:T(8,128)(2,1)S(1)}, u32[]{:S(2)}) copy-start(bf16[256,256]{1,0:T(8,128)(2,1)S(1)} %copy.34) | copy-start | bytes 393220
  15.4 4.1 %copy-start.3 = (bf16[256,256]{1,0:T(8,128)(2,1)}, bf16[256,256]{1,0:T(8,128)(2,1)S(1)}, u32[]{:S(2)}) copy-start(bf16[256,256]{1,0:T(8,128)(2,1)S(1)} %convolution_convert_fusion.1) | copy-start | bytes 393220
  16.2 188.7 %all-gather.7.cloned.1.call-start = ((), (), s32[]{:S(2)}) async-start(), calls=%async_computation.1 | async-start | bytes 9584640 | tf_op jit(solution)/shard_map/all_gather | solution.py:282
  19.7 4.8 %copy-start.9 = (f32[128]{0:T(128)S(1)}, f32[128]{0:T(128)}, u32[]{:S(2)}) copy-start(f32[128]{0:T(128)} %param.20) | copy-start | bytes 1540
  24.8 2.8 %copy-start.4 = (bf16[768,32]{0,1:T(8,128)(2,1)S(1)}, bf16[768,32]{0,1:T(8,128)(2,1)}, u32[]{:S(2)}) copy-start(bf16[768,32]{0,1:T(8,128)(2,1)} %param.26) | copy-start | bytes 147460
  24.8 2.8 %copy-start.5 = (bf16[32,768]{1,0:T(8,128)(2,1)S(1)}, bf16[32,768]{1,0:T(8,128)(2,1)}, u32[]{:S(2)}) copy-start(bf16[32,768]{1,0:T(8,128)(2,1)} %param.25) | copy-start | bytes 147460
  24.9 2.8 %copy-start.6 = (bf16[32,768]{1,0:T(8,128)(2,1)S(1)}, bf16[32,768]{1,0:T(8,128)(2,1)}, u32[]{:S(2)}) copy-start(bf16[32,768]{1,0:T(8,128)(2,1)} %param.24) | copy-start | bytes 147460
  130.3 31.3 %copy-start.7 = (f32[2048]{0:T(1024)S(1)}, f32[2048]{0:T(1024)}, u32[]{:S(2)}) copy-start(f32[2048]{0:T(1024)} %param.23) | copy-start | bytes 24580
Sparse Core Ops, SparseCore 0:
  16.3 103.9 all-gather.4
  123.0 81.8 all-gather.6
